TPU v7x, 512 devices: a whole 4x4x16 slice. The times are simulated.
512 devices in a mesh: group: 64 (over z, y_hi, core), tp: 8 (over x, y_lo).
Axes of the slice: x: 4, y: 4 (y_hi: 2, y_lo: 2; y = y_hi * 2 + y_lo), z: 16, core: 2. Of those that a mesh axis runs over, the one named last changes fastest.
Arguments:
- queries: bfloat16 [4096, 2048], P('group', 'tp'), may hold values from -22 to 22
- new_kv: bfloat16 [4096, 1024], P('group', 'tp'), may hold values from -6 to 6
- local_cache: bfloat16 [16384, 1024], P('group', 'tp'), may hold values from -6 to 6
- remote_pool: bfloat16 [32768, 1024], P('group', 'tp'), may hold values from -6 to 6
- page_index: int32 [64, 64], P('group'), may hold values from 0 to 63, each once within a row
- lengths: int32 [64], P('group'), may hold values from 256 to 768, as said below
- sinks: float32 [32], P('tp'), may hold values from 4 to 8
- out_weight: bfloat16 [2048, 2880], P('tp'), may hold values from -0.125 to 0.125
- residual: bfloat16 [4096, 2880], P('group', 'tp'), may hold values from -6 to 6
- norm_gain: float32 [2880], replicated, may hold values from 0.5 to 2
- routes: int32 [4096, 4], P('group'), may hold values from 0 to 31, all different within a row; in each aligned block of 64 rows (0 to 63, 64 to 127, ...) at most 10 rows name the same one
- route_weights: float32 [4096, 4], P('group'), may hold values from 0.1 to 1
- expert_gate: bfloat16 [64, 2880, 1440], P('group', None, 'tp'), may hold values from -0.109375 to 0.109375
- expert_up: bfloat16 [64, 2880, 1440], P('group', None, 'tp'), may hold values from -0.109375 to 0.109375
- expert_down: bfloat16 [64, 1440, 2880], P('group', None, 'tp'), may hold values from -0.109375 to 0.109375
Outputs:
- layer_out: bfloat16 [4096, 2880], P('group', 'tp')
Inputs may be any that keep to these rules, and one draw needn't show every extreme that they name: `lengths`: every request has at least 256 cached positions; some request has exactly 256, some exactly 768. `routes`: within the rows of one request no expert is named by more than 10 rows. `page_index`: each row is a permutation.
All inputs are finite; a program needn't handle non-finite values.
Results may differ from a plain program's by a relative error of at most 0.013.
Values may be sent and summed in bfloat16 or wider, within the bound.
A program may use at most 64 MiB of HBM per device.

v0:
```python
import jax
import jax.numpy as jnp
from jax import lax
from jax.sharding import PartitionSpec as P

HEAD = 64


THETA = 150000.0
ALPHA = 1.702
EPSILON = 1e-05


def rotate(values, positions):
    half_dim = values.shape[-1] // 2
    inverse = THETA ** (-2.0 * jnp.arange(half_dim, dtype=jnp.float32) / values.shape[-1])
    angles = positions[:, None, None] * inverse[None, None, :]
    cosine = jnp.cos(angles)
    sine_part = jnp.sin(angles)
    first_part = values[..., :half_dim]
    second_part = values[..., half_dim:]
    return jnp.concatenate(
        [
            first_part * cosine - second_part * sine_part,
            second_part * cosine + first_part * sine_part,
        ],
        axis=-1,
    )


def attend(query_rows, kv_rows, cache_kv, cache_valid, sinks, length):
    block_len = query_rows.shape[0]
    kv_heads = kv_rows.shape[1] // (2 * HEAD)
    query_heads = query_rows.shape[1] // HEAD
    group_size = query_heads // kv_heads
    positions = (length + jnp.arange(block_len, dtype=jnp.int32)).astype(jnp.float32)
    query_rot = rotate(
        query_rows.astype(jnp.float32).reshape(block_len, query_heads, HEAD), positions
    ).astype(jnp.bfloat16)
    kv_parts = kv_rows.reshape(block_len, kv_heads, 2, HEAD)
    key_rot = rotate(kv_parts[:, :, 0].astype(jnp.float32), positions).astype(jnp.bfloat16)
    cache_parts = cache_kv.reshape(cache_kv.shape[0], kv_heads, 2, HEAD)
    all_keys = jnp.concatenate([cache_parts[:, :, 0], key_rot], axis=0)
    all_values = jnp.concatenate([cache_parts[:, :, 1], kv_parts[:, :, 1]], axis=0)
    token_order = jnp.arange(block_len, dtype=jnp.int32)
    causal = token_order[None, :] <= token_order[:, None]
    allowed = jnp.concatenate(
        [jnp.broadcast_to(cache_valid[None, :], (block_len, cache_valid.shape[0])), causal], axis=1
    )
    row_allowed = jnp.repeat(allowed, group_size, axis=0)
    score_scale = HEAD ** (-0.5)
    query_block = query_rot.reshape(block_len * group_size, HEAD)
    scores = (
        jnp.dot(query_block, all_keys[:, 0].T, preferred_element_type=jnp.float32) * score_scale
    )
    scores = jnp.where(row_allowed, scores, -jnp.inf)
    sink_rows = jnp.tile(sinks, block_len)
    row_max = jnp.maximum(jnp.max(scores, axis=1), sink_rows)
    weights = jnp.exp(scores - row_max[:, None])
    denominator = jnp.sum(weights, axis=1) + jnp.exp(sink_rows - row_max)
    blended = (
        jnp.dot(weights.astype(jnp.bfloat16), all_values[:, 0], preferred_element_type=jnp.float32)
        / denominator[:, None]
    )
    outputs = blended.astype(jnp.bfloat16).reshape(block_len, group_size * HEAD)
    return outputs


def on_device(
    queries,
    new_kv,
    local_cache,
    remote_pool,
    page_index,
    lengths,
    sinks,
    out_weight,
    residual,
    norm_gain,
    routes,
    route_weights,
    expert_gate,
    expert_up,
    expert_down,
):
    groups = lax.axis_size("group")
    lane_count = remote_pool.shape[1]
    local_len = local_cache.shape[0]
    fetched = lax.all_to_all(
        remote_pool.reshape(groups, -1, lane_count),
        "group",
        split_axis=0,
        concat_axis=0,
        tiled=True,
    )
    page_len = fetched.shape[1]
    length = lengths[0]
    offsets = jnp.arange(page_len, dtype=jnp.int32)
    remote_pos = local_len + page_index[0][:, None] * page_len + offsets[None, :]
    cache_valid = jnp.concatenate(
        [jnp.ones((local_len,), jnp.bool_), (remote_pos < length).reshape(-1)]
    )
    cache_kv = jnp.concatenate([local_cache, fetched.reshape(-1, lane_count)], axis=0)
    attended = attend(queries, new_kv, cache_kv, cache_valid, sinks, length)
    width = residual.shape[1]
    start = lax.axis_index("tp") * width
    own_gain = lax.dynamic_slice_in_dim(norm_gain, start, width, 0)
    partial_sum = jnp.dot(attended, out_weight, preferred_element_type=jnp.float32)
    own_cols = lax.dynamic_slice_in_dim(partial_sum, start, width, 1) + residual.astype(jnp.float32)
    partial_sum = lax.dynamic_update_slice_in_dim(partial_sum, own_cols, start, 1)
    hidden_state = lax.psum(partial_sum, "tp")
    mean_square = jnp.mean(hidden_state * hidden_state, axis=1, keepdims=True)
    own_state = lax.dynamic_slice_in_dim(hidden_state, start, width, 1)
    normed_own = (own_state * lax.rsqrt(mean_square + EPSILON) * own_gain).astype(jnp.bfloat16)
    block_len = normed_own.shape[0]
    top_count = routes.shape[1]
    experts = groups // 2
    capacity = 5 * block_len * top_count // (4 * experts)
    member = jnp.any(
        routes[:, :, None] == jnp.arange(experts, dtype=jnp.int32)[None, None, :], axis=1
    ).astype(jnp.int32)
    slot_rank = jnp.cumsum(member, axis=0) - member
    slot_hit = member[:, :, None] * (
        slot_rank[:, :, None] == jnp.arange(capacity, dtype=jnp.int32)[None, None, :]
    ).astype(jnp.int32)
    slot_token = jnp.sum(slot_hit * jnp.arange(block_len, dtype=jnp.int32)[:, None, None], axis=0)
    slot_valid = jnp.sum(slot_hit, axis=0)
    send_own = jnp.take(normed_own, slot_token.reshape(-1), axis=0) * slot_valid.reshape(
        -1, 1
    ).astype(jnp.bfloat16)
    hidden_part = expert_gate.shape[2]
    gate_and_up = jnp.concatenate([expert_gate[0], expert_up[0]], axis=1)
    outgoing = send_own
    feature_count = outgoing.shape[1]
    outgoing = outgoing.reshape(experts, 1, capacity, feature_count)
    outgoing = jnp.broadcast_to(outgoing, (experts, 2, capacity, feature_count)).reshape(
        groups, capacity, feature_count
    )
    whole = lax.all_gather(
        lax.all_to_all(outgoing, "group", split_axis=0, concat_axis=0, tiled=True),
        "tp",
        axis=2,
        tiled=True,
    )
    sources, slot_count, features = whole.shape
    flat_rows = whole.reshape(sources * slot_count, features)
    both = jnp.dot(flat_rows, gate_and_up, preferred_element_type=jnp.float32)
    gate_val = both[:, :hidden_part]
    up_val = both[:, hidden_part:]
    active = (gate_val * jax.nn.sigmoid(ALPHA * gate_val) * (up_val + 1.0)).astype(jnp.bfloat16)
    joined = lax.all_gather(active, "tp", axis=1, tiled=True)
    result = jnp.dot(joined, expert_down[0], preferred_element_type=jnp.float32).astype(
        jnp.bfloat16
    )
    returned = result.reshape(sources, slot_count, result.shape[1])
    arrived = lax.all_to_all(returned, "group", split_axis=0, concat_axis=0, tiled=True)
    halves = arrived.reshape(experts, 2, capacity, width).astype(jnp.float32)
    summed = (halves[:, 0] + halves[:, 1]).reshape(experts * capacity, width)
    rank_at = jnp.take_along_axis(slot_rank, routes, axis=1)
    picked = jnp.take(summed, (routes * capacity + rank_at).reshape(-1), axis=0).reshape(
        block_len, top_count, width
    )
    mixing = route_weights / jnp.sum(route_weights, axis=1, keepdims=True)
    moe_out = jnp.sum(mixing[:, :, None] * picked, axis=1)
    return (own_state + moe_out).astype(jnp.bfloat16)


def solution(mesh):
    return jax.shard_map(
        on_device,
        mesh=mesh,
        in_specs=(
            P("group", "tp"),
            P("group", "tp"),
            P("group", "tp"),
            P("group", "tp"),
            P("group", None),
            P("group"),
            P("tp"),
            P("tp", None),
            P("group", "tp"),
            P(),
            P("group", None),
            P("group", None),
            P("group", None, "tp"),
            P("group", None, "tp"),
            P("group", None, "tp"),
        ),
        out_specs=P("group", "tp"),
        check_vma=False,
    )
```

profile of v0, /device:TPU:24, one launch (start us, length us, event | category | flops | bytes accessed | tf_op | source)
XLA Modules:
  0.0 589.4 jit_solution(3634151493439080288)
XLA Ops:
  6.5 18.7 %all-to-all-start = ((bf16[64,8,128]{2,1,0:T(8,128)(2,1)}), bf16[64,8,128]{2,1,0:T(8,128)(2,1)S(1)}, u32[]{:S(2)}, u32[]{:S(2)}) async-start(bf16[64,8,128]{2,1,0:T(8,128)(2,1)} %bitcast.65), calls=%async_computation | async-start | bytes 262144 | tf_op jit(solution)/shard_map/all_to_all | solution.py:89
  27.8 0.9 copy.144
  32.3 9.6 %all-to-all-done = bf16[64,8,128]{2,1,0:T(8,128)(2,1)S(1)} async-done(((bf16[64,8,128]{2,1,0:T(8,128)(2,1)}), bf16[64,8,128]{2,1,0:T(8,128)(2,1)S(1)}, u32[]{:S(2)}, u32[]{:S(2)}) %all-to-all-start) | async-done | bytes 131104 | tf_op jit(solution)/shard_map/all_to_all | solution.py:89
  45.2 1.1 dynamic_update_slice.3
  48.2 79.8 %all-reduce.3.cloned.1.call-done = f32[64,2880]{1,0:T(8,128)} async-done(((f32[64,2880]{1,0:T(8,128)}), f32[64,2880]{1,0:T(8,128)}) %all-reduce.3.cloned.1.call-update) | async-done | bytes 737296 | tf_op jit(solution)/shard_map/psum | solution.py:111
  128.0 1.3 multiply_reduce_fusion
  129.3 1.0 multiply_convert_fusion
  130.3 2.0 gather_fusion
  132.7 60.3 %all_to_all.15 = bf16[64,10,360]{2,1,0:T(8,128)(2,1)S(1)} all-to-all(bf16[64,10,360]{2,1,0:T(8,128)(2,1)S(1)} %bitcast.58), channel_id=1, replica_groups=mesh['group'=64,'tp'=8] {'group'}, dimensions={0} | all-to-all | bytes 921600 | tf_op jit(solution)/shard_map/all_to_all | solution.py:140
  193.1 2.0 copy.165
  195.3 230.1 %all-gather.4.cloned.1.call-done = bf16[64,10,2880]{0,1,2:T(8,128)(2,1)} async-done(((bf16[64,10,360]{0,1,2:T(8,128)(2,1)}), bf16[64,10,2880]{0,1,2:T(8,128)(2,1)}) %all-gather.4.cloned.1.call-update) | async-done | bytes 3686416 | tf_op jit(solution)/shard_map/all_gather | solution.py:139
  425.4 17.0 %copy.166 = bf16[64,10,2880]{2,1,0:T(8,128)(2,1)} copy(bf16[64,10,2880]{0,1,2:T(8,128)(2,1)} %all-gather.4.cloned.1.call-done) | data formatting | bytes 7372800 | tf_op jit(solution)/shard_map/all_gather | solution.py:139
  442.4 7.9 %reshape.386 = bf16[640,2880]{1,0:T(8,128)(2,1)} reshape(bf16[64,10,2880]{2,1,0:T(8,128)(2,1)} %copy.166) | data formatting | bytes 7372800 | tf_op jit(solution)/shard_map/reshape | solution.py:146
  450.3 4.3 fusion
  455.5 56.3 %all-gather.6.cloned.1.call-done = bf16[8,180,640]{2,1,0:T(8,128)(2,1)} async-done(((bf16[1,180,640]{2,1,0:T(8,128)(2,1)}), bf16[8,180,640]{2,1,0:T(8,128)(2,1)}) %all-gather.6.cloned.1.call-update) | async-done | bytes 1843216 | tf_op jit(solution)/shard_map/all_gather | solution.py:151
  511.7 1.7 reshape.421
  513.4 3.1 convolution_convert_fusion
  516.5 1.3 copy.167
  517.8 1.1 reshape.387
  518.8 15.7 %all-to-all-start.2 = ((bf16[64,10,360]{2,1,0:T(8,128)(2,1)}), bf16[64,10,360]{2,1,0:T(8,128)(2,1)S(1)}, u32[]{:S(2)}, u32[]{:S(2)}) async-start(bf16[64,10,360]{2,1,0:T(8,128)(2,1)} %reshape.387), calls=%async_computation.2 | async-start | bytes 1572864 | tf_op jit(solution)/shard_map/all_to_all | solution.py:156
  534.8 1.9 gather_fusion.2
  537.4 42.0 %all-to-all-done.2 = bf16[64,10,360]{2,1,0:T(8,128)(2,1)S(1)} async-done(((bf16[64,10,360]{2,1,0:T(8,128)(2,1)}), bf16[64,10,360]{2,1,0:T(8,128)(2,1)S(1)}, u32[]{:S(2)}, u32[]{:S(2)}) %all-to-all-start.2) | async-done | bytes 460832 | tf_op jit(solution)/shard_map/all_to_all | solution.py:156
  579.8 1.0 gather_fusion.1
  581.2 1.6 add_convert_fusion.1
  (94 shorter events, 13.5 us)
Async XLA Ops:
  6.5 38.0 %copy-start = (bf16[256,2880]{0,1:T(8,128)(2,1)S(1)}, bf16[256,2880]{0,1:T(8,128)(2,1)}, u32[]{:S(2)}) copy-start(bf16[256,2880]{0,1:T(8,128)(2,1)} %param.22) | copy-start | bytes 4423684
  6.5 24.0 %copy-start.5 = (f32[4]{0:T(128)S(1)}, f32[4]{0:T(128)}, u32[]{:S(2)}) copy-start(f32[4]{0:T(128)} %param.21) | copy-start | bytes 52
  6.5 24.3 %copy-start.3 = (s32[64,4]{0,1:T(4,128)S(1)}, s32[64,4]{0,1:T(4,128)}, u32[]{:S(2)}) copy-start(s32[64,4]{0,1:T(4,128)} %param.25) | copy-start | bytes 3076
  6.5 35.4 %all-to-all-start = ((bf16[64,8,128]{2,1,0:T(8,128)(2,1)}), bf16[64,8,128]{2,1,0:T(8,128)(2,1)S(1)}, u32[]{:S(2)}, u32[]{:S(2)}) async-start(bf16[64,8,128]{2,1,0:T(8,128)(2,1)} %bitcast.65), calls=%async_computation | async-start | bytes 262144 | tf_op jit(solution)/shard_map/all_to_all | solution.py:89
  25.3 102.7 %all-reduce.3.cloned.1.call-start = ((), (), s32[]{:S(2)}) async-start(), calls=%async_computation.3 | async-start | bytes 1507328 | tf_op jit(solution)/shard_map/psum | solution.py:111
  44.0 1.1 copy-start.2
  46.3 0.9 copy-start.1
  47.2 378.2 %all-gather.4.cloned.1.call-start = ((), (), s32[]{:S(2)}) async-start(), calls=%async_computation.4 | async-start | bytes 13271040 | tf_op jit(solution)/shard_map/all_gather | solution.py:139
  195.1 316.6 %all-gather.6.cloned.1.call-start = ((), (), s32[]{:S(2)}) async-start(), calls=%async_computation.5 | async-start | bytes 2119680 | tf_op jit(solution)/shard_map/all_gather | solution.py:151
  442.4 7.9 %copy-start.6 = (bf16[1,2880,180]{1,2,0:T(8,128)(2,1)S(1)}, bf16[1,2880,180]{1,2,0:T(8,128)(2,1)}, u32[]{:S(2)}) copy-start(bf16[1,2880,180]{1,2,0:T(8,128)(2,1)} %param.28) | copy-start | bytes 3110404
  518.8 60.5 %all-to-all-start.2 = ((bf16[64,10,360]{2,1,0:T(8,128)(2,1)}), bf16[64,10,360]{2,1,0:T(8,128)(2,1)S(1)}, u32[]{:S(2)}, u32[]{:S(2)}) async-start(bf16[64,10,360]{2,1,0:T(8,128)(2,1)} %reshape.387), calls=%async_computation.2 | async-start | bytes 1572864 | tf_op jit(solution)/shard_map/all_to_all | solution.py:156
  534.8 2.5 copy-start.4
Sparse Core Ops, SparseCore 0:
  47.3 80.6 all-reduce.2
  195.2 230.1 all-gather.3
  455.6 56.0 all-gather.5
where the time goes:
time: 592 us; the launch traced here: 589 us
  waiting for transfers between devices  418 us (71%)
  blocking collectives  60.3 us (10%)
  local copies, waits for them, and re-layouts  45.1 us (8%)
  starting transfers between devices  34.8 us (6%)
  between operations  14.2 us (2%)
  matrix products  8.63 us (1%)
  other arithmetic  8.61 us (1%)
    all_gather x1, waiting for transfers between devices, on_device(): lax.all_gather(lax.all_to_all(outgoing, 'group', split_axis=0, concat_axi...  230 us
    psum x1, waiting for transfers between devices, on_device(): hidden_state = lax.psum(partial_sum, 'tp')  79.8 us
    all_to_all x1, blocking collectives, on_device(): lax.all_to_all(outgoing, 'group', split_axis=0, concat_axis=0, tiled=True)  60.3 us
    all_gather x1, waiting for transfers between devices, on_device(): joined = lax.all_gather(active, 'tp', axis=1, tiled=True)  56.3 us
    all_to_all x1, waiting for transfers between devices, on_device(): lax.all_to_all(returned, 'group', split_axis=0, concat_axis=0, tiled=True)  42 us
    all_to_all x1, starting transfers between devices, on_device(): lax.all_to_all(remote_pool.reshape(groups, -1, lane_count), 'group', spli...  18.7 us
    all_gather x1, local copies, waits for them, and re-layouts, on_device(): lax.all_gather(lax.all_to_all(outgoing, 'group', split_axis=0, concat_axi...  17 us
    all_to_all x1, starting transfers between devices, on_device(): lax.all_to_all(returned, 'group', split_axis=0, concat_axis=0, tiled=True)  15.7 us
  transfers between devices with their start and end apart: 5, of which 5 were waited for; matrix products, arithmetic and copies ran while one was open for 2% of the time, Pallas kernels for 0%

commit v1 on v0

--- a/solution.py
+++ b/solution.py
@@ -103,14 +103,15 @@
     cache_kv = jnp.concatenate([local_cache, fetched.reshape(-1, lane_count)], axis=0)
     attended = attend(queries, new_kv, cache_kv, cache_valid, sinks, length)
     width = residual.shape[1]
+    tp_count = lax.axis_size("tp")
     start = lax.axis_index("tp") * width
     own_gain = lax.dynamic_slice_in_dim(norm_gain, start, width, 0)
     partial_sum = jnp.dot(attended, out_weight, preferred_element_type=jnp.float32)
-    own_cols = lax.dynamic_slice_in_dim(partial_sum, start, width, 1) + residual.astype(jnp.float32)
-    partial_sum = lax.dynamic_update_slice_in_dim(partial_sum, own_cols, start, 1)
-    hidden_state = lax.psum(partial_sum, "tp")
-    mean_square = jnp.mean(hidden_state * hidden_state, axis=1, keepdims=True)
-    own_state = lax.dynamic_slice_in_dim(hidden_state, start, width, 1)
+    partial_blocks = partial_sum.reshape(partial_sum.shape[0], tp_count, width).transpose(1, 0, 2)
+    own_attn = lax.psum_scatter(partial_blocks, "tp", scatter_dimension=0, tiled=False)
+    own_state = own_attn + residual.astype(jnp.float32)
+    square_sum = lax.psum(jnp.sum(own_state * own_state, axis=1, keepdims=True), "tp")
+    mean_square = square_sum / (width * tp_count)
     normed_own = (own_state * lax.rsqrt(mean_square + EPSILON) * own_gain).astype(jnp.bfloat16)
     block_len = normed_own.shape[0]
     top_count = routes.shape[1]
@@ -136,20 +137,17 @@
     outgoing = jnp.broadcast_to(outgoing, (experts, 2, capacity, feature_count)).reshape(
         groups, capacity, feature_count
     )
-    whole = lax.all_gather(
-        lax.all_to_all(outgoing, "group", split_axis=0, concat_axis=0, tiled=True),
-        "tp",
-        axis=2,
-        tiled=True,
-    )
-    sources, slot_count, features = whole.shape
-    flat_rows = whole.reshape(sources * slot_count, features)
-    both = jnp.dot(flat_rows, gate_and_up, preferred_element_type=jnp.float32)
+    received = lax.all_to_all(outgoing, "group", split_axis=0, concat_axis=0, tiled=True)
+    sources, slot_count, part_features = received.shape
+    whole = lax.all_gather(received.reshape(sources * slot_count, part_features), "tp", axis=0)
+    gate_blocks = gate_and_up.reshape(tp_count, part_features, gate_and_up.shape[1])
+    both = jnp.einsum("tsf,tfh->sh", whole, gate_blocks, preferred_element_type=jnp.float32)
     gate_val = both[:, :hidden_part]
     up_val = both[:, hidden_part:]
     active = (gate_val * jax.nn.sigmoid(ALPHA * gate_val) * (up_val + 1.0)).astype(jnp.bfloat16)
-    joined = lax.all_gather(active, "tp", axis=1, tiled=True)
-    result = jnp.dot(joined, expert_down[0], preferred_element_type=jnp.float32).astype(
+    joined = lax.all_gather(active, "tp", axis=0)
+    down_blocks = expert_down[0].reshape(tp_count, hidden_part, expert_down.shape[2])
+    result = jnp.einsum("tsh,thd->sd", joined, down_blocks, preferred_element_type=jnp.float32).astype(
         jnp.bfloat16
     )
     returned = result.reshape(sources, slot_count, result.shape[1])

time: 592 us -> 381 us (0.64)
  waiting for transfers between devices: 418 us -> 210 us
  local copies, waits for them, and re-layouts: 45.1 us -> 26 us
  blocking collectives: 60.3 us -> 78.7 us
    all_gather x2, waiting for transfers between devices: 286 us -> 124 us  [the longest x1 68.8 us: on_device(): lax.all_gather(received.reshape(sources * slot_count, part_features), 'tp...]
    psum x1 -> x0, waiting for transfers between devices: 79.8 us -> none  [on_device(): hidden_state = lax.psum(partial_sum, 'tp')]
    reduce_scatter x0 -> x1, waiting for transfers between devices: none -> 33.2 us  [on_device(): lax.psum_scatter(partial_blocks, 'tp', scatter_dimension=0, tiled=False)]
    psum x0 -> x1, blocking collectives: none -> 18.5 us  [on_device(): lax.psum(jnp.sum(own_state * own_state, axis=1, keepdims=True), 'tp')]
    all_gather x1 -> x0, local copies, waits for them, and re-layouts: 17 us -> none  [on_device(): lax.all_gather(lax.all_to_all(outgoing, 'group', split_axis=0, concat_axi...]
    concatenate x0 -> x4, local copies, waits for them, and re-layouts: none -> 7.9 us  [on_device(): gate_and_up = jnp.concatenate([expert_gate[0], expert_up[0]], axis=1)]
    reshape x1 -> x0, local copies, waits for them, and re-layouts: 7.87 us -> none  [on_device(): flat_rows = whole.reshape(sources * slot_count, features)]
  transfers between devices with their start and end apart: 5 -> 5, of which waited for: 5 -> 5; matrix products, arithmetic and copies ran while one was open for 2% -> 5% of each run, Pallas kernels for 0% -> 0%
where the time goes in v1:
time: 381 us; the launch traced here: 379 us
  waiting for transfers between devices  210 us (55%)
  blocking collectives  78.7 us (21%)
  starting transfers between devices  34.8 us (9%)
  local copies, waits for them, and re-layouts  26 us (7%)
  between operations  14.2 us (4%)
  matrix products  7.92 us (2%)
  other arithmetic  7.24 us (2%)
    all_gather x1, waiting for transfers between devices, on_device(): lax.all_gather(received.reshape(sources * slot_count, part_features), 'tp...  68.8 us
    all_to_all x1, blocking collectives, on_device(): lax.all_to_all(outgoing, 'group', split_axis=0, concat_axis=0, tiled=True)  60.2 us
    all_gather x1, waiting for transfers between devices, on_device(): joined = lax.all_gather(active, 'tp', axis=0)  55 us
    all_to_all x1, waiting for transfers between devices, on_device(): lax.all_to_all(returned, 'group', split_axis=0, concat_axis=0, tiled=True)  42 us
    reduce_scatter x1, waiting for transfers between devices, on_device(): lax.psum_scatter(partial_blocks, 'tp', scatter_dimension=0, tiled=False)  33.2 us
    all_to_all x1, starting transfers between devices, on_device(): lax.all_to_all(remote_pool.reshape(groups, -1, lane_count), 'group', spli...  18.7 us
    psum x1, blocking collectives, on_device(): lax.psum(jnp.sum(own_state * own_state, axis=1, keepdims=True), 'tp')  18.5 us
    all_to_all x1, starting transfers between devices, on_device(): lax.all_to_all(returned, 'group', split_axis=0, concat_axis=0, tiled=True)  15.7 us
  transfers between devices with their start and end apart: 5, of which 5 were waited for; matrix products, arithmetic and copies ran while one was open for 5% of the time, Pallas kernels for 0%

profile of v1, /device:TPU:24, one launch (start us, length us, event | category | flops | bytes accessed | tf_op | source)
XLA Modules:
  0.0 378.6 jit_solution(3430151987980551286)
XLA Ops:
  6.5 18.7 %all-to-all-start = ((bf16[64,8,128]{2,1,0:T(8,128)(2,1)}), bf16[64,8,128]{2,1,0:T(8,128)(2,1)S(1)}, u32[]{:S(2)}, u32[]{:S(2)}) async-start(bf16[64,8,128]{2,1,0:T(8,128)(2,1)} %bitcast.95), calls=%async_computation | async-start | bytes 262144 | tf_op jit(solution)/shard_map/all_to_all | solution.py:89
  31.2 10.7 %all-to-all-done = bf16[64,8,128]{2,1,0:T(8,128)(2,1)S(1)} async-done(((bf16[64,8,128]{2,1,0:T(8,128)(2,1)}), bf16[64,8,128]{2,1,0:T(8,128)(2,1)S(1)}, u32[]{:S(2)}, u32[]{:S(2)}) %all-to-all-start) | async-done | bytes 131104 | tf_op jit(solution)/shard_map/all_to_all | solution.py:89
  44.5 1.5 convolution_bitcast_fusion
  48.1 33.2 %reduce-scatter.2.cloned.1.call-done = f32[1,64,360]{2,1,0:T(8,128)} async-done(((f32[8,64,360]{2,1,0:T(8,128)}), f32[1,64,360]{2,1,0:T(8,128)}) %reduce-scatter.2.cloned.1.call-update) | async-done | bytes 92176 | tf_op jit(solution)/shard_map/reduce_scatter | solution.py:111
  81.4 1.0 multiply_reduce_fusion.1
  82.4 18.5 %psum.7 = f32[64,1]{0,1:T(1,128)S(1)} all-reduce(f32[64,1]{0,1:T(1,128)S(1)} %bitcast.98), channel_id=1, replica_groups=mesh['group'=64,'tp'=8] {'tp'}, use_global_device_ids=true, to_apply=%region_8.9 | all-reduce | flops 64 | bytes 512 | tf_op jit(solution)/shard_map/psum | solution.py:113
  101.9 2.0 gather_fusion
  104.4 60.2 %all_to_all.15 = bf16[64,10,360]{2,1,0:T(8,128)(2,1)S(1)} all-to-all(bf16[64,10,360]{2,1,0:T(8,128)(2,1)S(1)} %bitcast.86), channel_id=1, replica_groups=mesh['group'=64,'tp'=8] {'group'}, dimensions={0} | all-to-all | bytes 921600 | tf_op jit(solution)/shard_map/all_to_all | solution.py:140
  164.8 1.0 copy.122
  166.1 2.8 concatenate.60
  168.9 1.2 copy.123
  170.1 2.8 concatenate.61
  172.8 1.2 copy.124
  174.0 68.8 %all-gather.4.cloned.1.call-done = bf16[8,640,360]{1,2,0:T(8,128)(2,1)} async-done(((bf16[1,640,360]{1,2,0:T(8,128)(2,1)}), bf16[8,640,360]{1,2,0:T(8,128)(2,1)}) %all-gather.4.cloned.1.call-update) | async-done | bytes 3686416 | tf_op jit(solution)/shard_map/all_gather | solution.py:142
  242.8 4.7 %fusion.10 = f32[640,360]{0,1:T(8,128)S(1)} fusion(bf16[8,640,360]{1,2,0:T(8,128)(2,1)} %all-gather.4.cloned.1.call-done, bf16[8,360,180]{1,2,0:T(8,128)(2,1)} %copy.124, bf16[8,360,180]{1,2,0:T(8,128)(2,1)} %copy.123), kind=kOutput, calls=%fused_computation.11 | convolution fusion | flops 1331251200 | bytes 6681600 | tf_op jit(solution)/shard_map/tsf,tfh->sh/dot_general | solution.py:144
  248.3 1.4 reshape_squeeze.3
  249.7 55.0 %all-gather.6.cloned.1.call-done = bf16[5120,180]{0,1:T(8,128)(2,1)} async-done(((bf16[640,180]{0,1:T(8,128)(2,1)}), bf16[5120,180]{0,1:T(8,128)(2,1)}) %all-gather.6.cloned.1.call-update) | async-done | bytes 1843216 | tf_op jit(solution)/shard_map/all_gather | solution.py:148
  304.7 1.8 copy.133
  306.6 1.1 fusion.14
  307.9 1.1 reshape.382
  309.0 15.7 %all-to-all-start.2 = ((bf16[64,10,360]{2,1,0:T(8,128)(2,1)}), bf16[64,10,360]{2,1,0:T(8,128)(2,1)S(1)}, u32[]{:S(2)}, u32[]{:S(2)}) async-start(bf16[64,10,360]{2,1,0:T(8,128)(2,1)} %reshape.382), calls=%async_computation.3 | async-start | bytes 1572864 | tf_op jit(solution)/shard_map/all_to_all | solution.py:154
  325.0 1.9 gather_fusion.2
  327.6 42.0 %all-to-all-done.2 = bf16[64,10,360]{2,1,0:T(8,128)(2,1)S(1)} async-done(((bf16[64,10,360]{2,1,0:T(8,128)(2,1)}), bf16[64,10,360]{2,1,0:T(8,128)(2,1)S(1)}, u32[]{:S(2)}, u32[]{:S(2)}) %all-to-all-start.2) | async-done | bytes 460832 | tf_op jit(solution)/shard_map/all_to_all | solution.py:154
  370.0 1.0 gather_fusion.1
  (95 shorter events, 15.1 us)
Async XLA Ops:
  6.5 38.0 %copy-start = (bf16[256,2880]{0,1:T(8,128)(2,1)S(1)}, bf16[256,2880]{0,1:T(8,128)(2,1)}, u32[]{:S(2)}) copy-start(bf16[256,2880]{0,1:T(8,128)(2,1)} %param.22) | copy-start | bytes 4423684
  6.5 24.1 %copy-start.5 = (f32[4]{0:T(128)S(1)}, f32[4]{0:T(128)}, u32[]{:S(2)}) copy-start(f32[4]{0:T(128)} %param.21) | copy-start | bytes 52
  6.5 35.4 %all-to-all-start = ((bf16[64,8,128]{2,1,0:T(8,128)(2,1)}), bf16[64,8,128]{2,1,0:T(8,128)(2,1)S(1)}, u32[]{:S(2)}, u32[]{:S(2)}) async-start(bf16[64,8,128]{2,1,0:T(8,128)(2,1)} %bitcast.95), calls=%async_computation | async-start | bytes 262144 | tf_op jit(solution)/shard_map/all_to_all | solution.py:89
  25.3 56.1 %reduce-scatter.2.cloned.1.call-start = ((), (), s32[]{:S(2)}) async-start(), calls=%async_computation.4 | async-start | bytes 884736 | tf_op jit(solution)/shard_map/reduce_scatter | solution.py:111
  44.5 1.6 copy-start.3
  44.5 36.8 %copy-start.2 = (bf16[64,360]{1,0:T(8,128)(2,1)S(1)}, bf16[64,360]{1,0:T(8,128)(2,1)}, u32[]{:S(2)}) copy-start(bf16[64,360]{1,0:T(8,128)(2,1)} %param.23) | copy-start | bytes 138244
  46.0 196.7 %all-gather.4.cloned.1.call-start = ((), (), s32[]{:S(2)}) async-start(), calls=%async_computation.5 | async-start | bytes 4147200 | tf_op jit(solution)/shard_map/all_gather | solution.py:142
  165.9 138.9 %all-gather.6.cloned.1.call-start = ((), (), s32[]{:S(2)}) async-start(), calls=%async_computation.6 | async-start | bytes 2119680 | tf_op jit(solution)/shard_map/all_gather | solution.py:148
  309.0 60.5 %all-to-all-start.2 = ((bf16[64,10,360]{2,1,0:T(8,128)(2,1)}), bf16[64,10,360]{2,1,0:T(8,128)(2,1)S(1)}, u32[]{:S(2)}, u32[]{:S(2)}) async-start(bf16[64,10,360]{2,1,0:T(8,128)(2,1)} %reshape.382), calls=%async_computation.3 | async-start | bytes 1572864 | tf_op jit(solution)/shard_map/all_to_all | solution.py:154
  325.0 2.5 copy-start.4
  370.0 1.5 copy-start.1
Sparse Core Ops, SparseCore 0:
  46.2 35.1 reduce-scatter.1
  166.0 76.7 all-gather.3
  248.5 56.2 all-gather.5

commit v2 on v1

--- a/solution.py
+++ b/solution.py
@@ -1,6 +1,8 @@
 import jax
 import jax.numpy as jnp
 from jax import lax
+from jax.experimental import pallas as pl
+from jax.experimental.pallas import tpu as pltpu
 from jax.sharding import PartitionSpec as P
 
 HEAD = 64
@@ -9,6 +11,65 @@
 THETA = 150000.0
 ALPHA = 1.702
 EPSILON = 1e-05
+
+
+def _exchange_kernel(x_ref, o_ref, buf, send_sem, recv_sem, local_sem):
+    count = x_ref.shape[0]
+    me = lax.axis_index("group")
+    lane = lax.axis_index("tp")
+    barrier = pltpu.get_barrier_semaphore()
+
+    def greet(step, carry):
+        peer = lax.rem(me + step, count)
+        pl.semaphore_signal(barrier, inc=1, device_id=(peer, lane), device_id_type=pl.DeviceIdType.MESH)
+        return carry
+
+    lax.fori_loop(1, count, greet, 0)
+    pl.semaphore_wait(barrier, count - 1)
+    local = pltpu.make_async_copy(x_ref.at[me], buf.at[me], local_sem)
+    local.start()
+
+    def send(step, carry):
+        peer = lax.rem(me + step, count)
+        pltpu.make_async_remote_copy(
+            src_ref=x_ref.at[peer],
+            dst_ref=buf.at[me],
+            send_sem=send_sem,
+            recv_sem=recv_sem,
+            device_id=(peer, lane),
+            device_id_type=pl.DeviceIdType.MESH,
+        ).start()
+        return carry
+
+    lax.fori_loop(1, count, send, 0)
+    local.wait()
+    every = pltpu.make_async_remote_copy(
+        src_ref=x_ref.at[pl.ds(0, count - 1)],
+        dst_ref=buf.at[pl.ds(0, count - 1)],
+        send_sem=send_sem,
+        recv_sem=recv_sem,
+        device_id=(lax.rem(me + 1, count), lane),
+        device_id_type=pl.DeviceIdType.MESH,
+    )
+    every.wait_send()
+    every.wait_recv()
+    o_ref[...] = buf[...]
+
+
+def group_exchange(x, collective_id):
+    return pl.pallas_call(
+        _exchange_kernel,
+        out_shape=jax.ShapeDtypeStruct(x.shape, x.dtype),
+        in_specs=[pl.BlockSpec(memory_space=pltpu.VMEM)],
+        out_specs=pl.BlockSpec(memory_space=pltpu.VMEM),
+        scratch_shapes=[
+            pltpu.VMEM(x.shape, x.dtype),
+            pltpu.SemaphoreType.DMA(()),
+            pltpu.SemaphoreType.DMA(()),
+            pltpu.SemaphoreType.DMA(()),
+        ],
+        compiler_params=pltpu.CompilerParams(collective_id=collective_id, has_side_effects=True),
+    )(x)
 
 
 def rotate(values, positions):
@@ -86,13 +147,7 @@
     groups = lax.axis_size("group")
     lane_count = remote_pool.shape[1]
     local_len = local_cache.shape[0]
-    fetched = lax.all_to_all(
-        remote_pool.reshape(groups, -1, lane_count),
-        "group",
-        split_axis=0,
-        concat_axis=0,
-        tiled=True,
-    )
+    fetched = group_exchange(remote_pool.reshape(groups, -1, lane_count), 1)
     page_len = fetched.shape[1]
     length = lengths[0]
     offsets = jnp.arange(page_len, dtype=jnp.int32)
@@ -137,7 +192,7 @@
     outgoing = jnp.broadcast_to(outgoing, (experts, 2, capacity, feature_count)).reshape(
         groups, capacity, feature_count
     )
-    received = lax.all_to_all(outgoing, "group", split_axis=0, concat_axis=0, tiled=True)
+    received = group_exchange(outgoing, 2)
     sources, slot_count, part_features = received.shape
     whole = lax.all_gather(received.reshape(sources * slot_count, part_features), "tp", axis=0)
     gate_blocks = gate_and_up.reshape(tp_count, part_features, gate_and_up.shape[1])
@@ -151,7 +206,7 @@
         jnp.bfloat16
     )
     returned = result.reshape(sources, slot_count, result.shape[1])
-    arrived = lax.all_to_all(returned, "group", split_axis=0, concat_axis=0, tiled=True)
+    arrived = group_exchange(returned, 3)
     halves = arrived.reshape(experts, 2, capacity, width).astype(jnp.float32)
     summed = (halves[:, 0] + halves[:, 1]).reshape(experts * capacity, width)
     rank_at = jnp.take_along_axis(slot_rank, routes, axis=1)

time: 381 us -> 382 us (level)
  Pallas kernels: 0 us -> 131 us
  blocking collectives: 78.7 us -> 18.4 us
  waiting for transfers between devices: 210 us -> 171 us
  starting transfers between devices: 34.8 us -> 0.27 us
    pallas_call x0 -> x3, Pallas kernels: none -> 131 us  [group_exchange(): pl.pallas_call(_exchange_kernel, out_shape=jax.ShapeDtypeStruct(x.shape,...]
    all_to_all x1 -> x0, blocking collectives: 60.2 us -> none  [on_device(): lax.all_to_all(outgoing, 'group', split_axis=0, concat_axis=0, tiled=True)]
    all_to_all x2 -> x0, waiting for transfers between devices: 52.7 us -> none  [the longest x1 42 us: on_device(): lax.all_to_all(returned, 'group', split_axis=0, concat_axis=0, tiled=True)]
    all_to_all x2 -> x0, starting transfers between devices: 34.4 us -> none  [the longest x1 18.7 us: on_device(): lax.all_to_all(remote_pool.reshape(groups, -1, lane_count), 'group', spli...]
    all_gather x1, waiting for transfers between devices: 68.8 us -> 77.5 us  [on_device(): lax.all_gather(received.reshape(sources * slot_count, part_features), 'tp...]
    reduce_scatter x1, waiting for transfers between devices: 33.2 us -> 41.7 us  [on_device(): lax.psum_scatter(partial_blocks, 'tp', scatter_dimension=0, tiled=False)]
  transfers between devices with their start and end apart: 5 -> 3, of which waited for: 5 -> 3; matrix products, arithmetic and copies ran while one was open for 5% -> 4% of each run, Pallas kernels for 0% -> 0%
where the time goes in v2:
time: 382 us; the launch traced here: 380 us
  waiting for transfers between devices  171 us (45%)
  Pallas kernels  131 us (34%)
  local copies, waits for them, and re-layouts  29 us (8%)
  blocking collectives  18.4 us (5%)
  between operations  14.4 us (4%)
  matrix products  7.92 us (2%)
  other arithmetic  7.72 us (2%)
    pallas_call x3, Pallas kernels, group_exchange(): pl.pallas_call(_exchange_kernel, out_shape=jax.ShapeDtypeStruct(x.shape,...  131 us
    all_gather x1, waiting for transfers between devices, on_device(): lax.all_gather(received.reshape(sources * slot_count, part_features), 'tp...  77.5 us
    all_gather x1, waiting for transfers between devices, on_device(): joined = lax.all_gather(active, 'tp', axis=0)  52.2 us
    reduce_scatter x1, waiting for transfers between devices, on_device(): lax.psum_scatter(partial_blocks, 'tp', scatter_dimension=0, tiled=False)  41.7 us
    psum x1, blocking collectives, on_device(): lax.psum(jnp.sum(own_state * own_state, axis=1, keepdims=True), 'tp')  18.4 us
    concatenate x4, local copies, waits for them, and re-layouts, on_device(): gate_and_up = jnp.concatenate([expert_gate[0], expert_up[0]], axis=1)  7.9 us
  transfers between devices with their start and end apart: 3, of which 3 were waited for; matrix products, arithmetic and copies ran while one was open for 4% of the time, Pallas kernels for 0%

profile of v2, /device:TPU:24, one launch (start us, length us, event | category | flops | bytes accessed | tf_op | source)
XLA Modules:
  0.0 379.6 jit_solution(2030516666422580559)
XLA Ops:
  9.4 26.8 %shard_map.145 = bf16[64,8,128]{2,1,0:T(8,128)(2,1)} custom-call(bf16[64,8,128]{2,1,0:T(8,128)(2,1)} %bitcast.95), custom_call_target="tpu_custom_call" | custom-call | tf_op jit(solution)/shard_map/pallas_call | solution.py:60
  36.3 1.0 concatenate.55
  42.2 1.5 convolution_bitcast_fusion
  45.8 41.7 %reduce-scatter.2.cloned.1.call-done = f32[1,64,360]{2,1,0:T(8,128)} async-done(((f32[8,64,360]{2,1,0:T(8,128)}), f32[1,64,360]{2,1,0:T(8,128)}) %reduce-scatter.2.cloned.1.call-update) | async-done | bytes 92176 | tf_op jit(solution)/shard_map/reduce_scatter | solution.py:166
  87.6 1.0 multiply_reduce_fusion.1
  88.6 18.4 %psum.7 = f32[64,1]{0,1:T(1,128)S(1)} all-reduce(f32[64,1]{0,1:T(1,128)S(1)} %bitcast.98), channel_id=1, replica_groups=mesh['group'=64,'tp'=8] {'tp'}, use_global_device_ids=true, to_apply=%region_8.9 | all-reduce | flops 64 | bytes 512 | tf_op jit(solution)/shard_map/psum | solution.py:168
  108.0 2.0 gather_fusion
  111.3 51.9 %shard_map.146 = bf16[64,10,360]{2,1,0:T(8,128)(2,1)} custom-call(bf16[64,10,360]{2,1,0:T(8,128)(2,1)} %bitcast.86), custom_call_target="tpu_custom_call" | custom-call | tf_op jit(solution)/shard_map/pallas_call | solution.py:60
  163.2 1.5 all_gather_reshape.3
  164.6 1.0 copy.115
  165.9 2.8 concatenate.60
  168.7 1.2 copy.116
  169.8 2.8 concatenate.61
  172.6 1.2 copy.117
  173.8 77.5 %all-gather.4.cloned.1.call-done = bf16[8,640,360]{1,2,0:T(8,128)(2,1)} async-done(((bf16[1,640,360]{1,2,0:T(8,128)(2,1)}), bf16[8,640,360]{1,2,0:T(8,128)(2,1)}) %all-gather.4.cloned.1.call-update) | async-done | bytes 3686416 | tf_op jit(solution)/shard_map/all_gather | solution.py:197
  251.3 4.7 %fusion.10 = f32[640,360]{0,1:T(8,128)S(1)} fusion(bf16[8,640,360]{1,2,0:T(8,128)(2,1)} %all-gather.4.cloned.1.call-done, bf16[8,360,180]{1,2,0:T(8,128)(2,1)} %copy.117, bf16[8,360,180]{1,2,0:T(8,128)(2,1)} %copy.116), kind=kOutput, calls=%fused_computation.11 | convolution fusion | flops 1331251200 | bytes 6681600 | tf_op jit(solution)/shard_map/tsf,tfh->sh/dot_general | solution.py:199
  256.9 1.4 reshape_squeeze.3
  258.5 1.9 gather_fusion.2
  261.1 52.2 %all-gather.6.cloned.1.call-done = bf16[5120,180]{0,1:T(8,128)(2,1)} async-done(((bf16[640,180]{0,1:T(8,128)(2,1)}), bf16[5120,180]{0,1:T(8,128)(2,1)}) %all-gather.6.cloned.1.call-update) | async-done | bytes 1843216 | tf_op jit(solution)/shard_map/all_gather | solution.py:203
  313.3 1.8 copy.125
  315.1 1.1 fusion.14
  316.5 1.1 reshape.382.x_ref
  317.6 51.9 %shard_map.147 = bf16[64,10,360]{2,1,0:T(8,128)(2,1)} custom-call(bf16[64,10,360]{2,1,0:T(8,128)(2,1)} %reshape.382.x_ref), custom_call_target="tpu_custom_call" | custom-call | tf_op jit(solution)/shard_map/pallas_call | solution.py:60
  369.5 1.3 convert.22
  (95 shorter events, 15.7 us)
Async XLA Ops:
  6.5 35.7 %copy-start = (bf16[256,2880]{0,1:T(8,128)(2,1)S(1)}, bf16[256,2880]{0,1:T(8,128)(2,1)}, u32[]{:S(2)}) copy-start(bf16[256,2880]{0,1:T(8,128)(2,1)} %param.22) | copy-start | bytes 4423684
  6.5 81.0 %reduce-scatter.2.cloned.1.call-start = ((), (), s32[]{:S(2)}) async-start(), calls=%async_computation.1 | async-start | bytes 884736 | tf_op jit(solution)/shard_map/reduce_scatter | solution.py:166
  8.2 31.2 %copy-start.6 = (s32[1,64]{1,0:T(1,128)S(1)}, s32[1,64]{1,0:T(1,128)}, u32[]{:S(2)}) copy-start(s32[1,64]{1,0:T(1,128)} %param.19) | copy-start | bytes 772
  38.4 2.1 copy-start.5
  42.2 1.6 copy-start.3
  42.2 45.3 %copy-start.2 = (bf16[64,360]{1,0:T(8,128)(2,1)S(1)}, bf16[64,360]{1,0:T(8,128)(2,1)}, u32[]{:S(2)}) copy-start(bf16[64,360]{1,0:T(8,128)(2,1)} %param.23) | copy-start | bytes 138244
  43.7 207.6 %all-gather.4.cloned.1.call-start = ((), (), s32[]{:S(2)}) async-start(), calls=%async_computation.2 | async-start | bytes 4147200 | tf_op jit(solution)/shard_map/all_gather | solution.py:197
  165.6 147.6 %all-gather.6.cloned.1.call-start = ((), (), s32[]{:S(2)}) async-start(), calls=%async_computation.3 | async-start | bytes 2119680 | tf_op jit(solution)/shard_map/all_gather | solution.py:203
  258.5 2.5 copy-start.4
  371.0 1.5 copy-start.1
Sparse Core Ops, SparseCore 0:
  43.9 43.6 reduce-scatter.1
  165.8 85.5 all-gather.3
  257.0 56.2 all-gather.5

commit v3 on v2

--- a/solution.py
+++ b/solution.py
@@ -1,3 +1,5 @@
+import functools
+
 import jax
 import jax.numpy as jnp
 from jax import lax
@@ -13,30 +15,38 @@
 EPSILON = 1e-05
 
 
-def _exchange_kernel(x_ref, o_ref, buf, send_sem, recv_sem, local_sem):
-    count = x_ref.shape[0]
-    me = lax.axis_index("group")
-    lane = lax.axis_index("tp")
+def _transfer_kernel(axis, gather, x_ref, o_ref, buf, send_sem, recv_sem, local_sem):
+    count = buf.shape[0]
+    group_at = lax.axis_index("group")
+    tp_at = lax.axis_index("tp")
+    me = tp_at if axis == "tp" else group_at
+
+    def device(peer):
+        return (group_at, peer) if axis == "tp" else (peer, tp_at)
+
+    def piece(peer):
+        return x_ref if gather else x_ref.at[peer]
+
     barrier = pltpu.get_barrier_semaphore()
 
     def greet(step, carry):
         peer = lax.rem(me + step, count)
-        pl.semaphore_signal(barrier, inc=1, device_id=(peer, lane), device_id_type=pl.DeviceIdType.MESH)
+        pl.semaphore_signal(barrier, inc=1, device_id=device(peer), device_id_type=pl.DeviceIdType.MESH)
         return carry
 
     lax.fori_loop(1, count, greet, 0)
     pl.semaphore_wait(barrier, count - 1)
-    local = pltpu.make_async_copy(x_ref.at[me], buf.at[me], local_sem)
+    local = pltpu.make_async_copy(piece(me), buf.at[me], local_sem)
     local.start()
 
     def send(step, carry):
         peer = lax.rem(me + step, count)
         pltpu.make_async_remote_copy(
-            src_ref=x_ref.at[peer],
+            src_ref=piece(peer),
             dst_ref=buf.at[me],
             send_sem=send_sem,
             recv_sem=recv_sem,
-            device_id=(peer, lane),
+            device_id=device(peer),
             device_id_type=pl.DeviceIdType.MESH,
         ).start()
         return carry
@@ -44,11 +54,11 @@
     lax.fori_loop(1, count, send, 0)
     local.wait()
     every = pltpu.make_async_remote_copy(
-        src_ref=x_ref.at[pl.ds(0, count - 1)],
+        src_ref=buf.at[pl.ds(0, count - 1)],
         dst_ref=buf.at[pl.ds(0, count - 1)],
         send_sem=send_sem,
         recv_sem=recv_sem,
-        device_id=(lax.rem(me + 1, count), lane),
+        device_id=device(lax.rem(me + 1, count)),
         device_id_type=pl.DeviceIdType.MESH,
     )
     every.wait_send()
@@ -56,20 +66,30 @@
     o_ref[...] = buf[...]
 
 
-def group_exchange(x, collective_id):
+def _transfer(x, axis, gather, collective_id):
+    count = lax.axis_size(axis)
+    shape = ((count,) + x.shape) if gather else x.shape
     return pl.pallas_call(
-        _exchange_kernel,
-        out_shape=jax.ShapeDtypeStruct(x.shape, x.dtype),
+        functools.partial(_transfer_kernel, axis, gather),
+        out_shape=jax.ShapeDtypeStruct(shape, x.dtype),
         in_specs=[pl.BlockSpec(memory_space=pltpu.VMEM)],
         out_specs=pl.BlockSpec(memory_space=pltpu.VMEM),
         scratch_shapes=[
-            pltpu.VMEM(x.shape, x.dtype),
+            pltpu.VMEM(shape, x.dtype),
             pltpu.SemaphoreType.DMA(()),
             pltpu.SemaphoreType.DMA(()),
             pltpu.SemaphoreType.DMA(()),
         ],
         compiler_params=pltpu.CompilerParams(collective_id=collective_id, has_side_effects=True),
     )(x)
+
+
+def group_exchange(x, collective_id):
+    return _transfer(x, "group", False, collective_id)
+
+
+def tp_gather(x, collective_id):
+    return _transfer(x, "tp", True, collective_id)
 
 
 def rotate(values, positions):
@@ -194,15 +214,15 @@
     )
     received = group_exchange(outgoing, 2)
     sources, slot_count, part_features = received.shape
-    whole = lax.all_gather(received.reshape(sources * slot_count, part_features), "tp", axis=0)
+    whole = tp_gather(received.reshape(sources * slot_count, part_features), 4)
     gate_blocks = gate_and_up.reshape(tp_count, part_features, gate_and_up.shape[1])
     both = jnp.einsum("tsf,tfh->sh", whole, gate_blocks, preferred_element_type=jnp.float32)
     gate_val = both[:, :hidden_part]
     up_val = both[:, hidden_part:]
     active = (gate_val * jax.nn.sigmoid(ALPHA * gate_val) * (up_val + 1.0)).astype(jnp.bfloat16)
-    joined = lax.all_gather(active, "tp", axis=0)
+    joined = tp_gather(active.T, 5)
     down_blocks = expert_down[0].reshape(tp_count, hidden_part, expert_down.shape[2])
-    result = jnp.einsum("tsh,thd->sd", joined, down_blocks, preferred_element_type=jnp.float32).astype(
+    result = jnp.einsum("ths,thd->sd", joined, down_blocks, preferred_element_type=jnp.float32).astype(
         jnp.bfloat16
     )
     returned = result.reshape(sources, slot_count, result.shape[1])

time: 382 us -> 346 us (0.906)
  waiting for transfers between devices: 171 us -> 29.7 us
  Pallas kernels: 131 us -> 236 us
    all_gather x2 -> x0, waiting for transfers between devices: 130 us -> none  [the longest x1 77.5 us: on_device(): lax.all_gather(received.reshape(sources * slot_count, part_features), 'tp...]
    pallas_call x3 -> x5, Pallas kernels: 131 us -> 236 us  [_transfer(): pl.pallas_call(functools.partial(_transfer_kernel, axis, gather), out_sha...]
    reduce_scatter x1, waiting for transfers between devices: 41.7 us -> 29.7 us  [on_device(): lax.psum_scatter(partial_blocks, 'tp', scatter_dimension=0, tiled=False)]
  transfers between devices with their start and end apart: 3 -> 1, of which waited for: 3 -> 1; matrix products, arithmetic and copies ran while one was open for 4% -> 4% of each run, Pallas kernels for 0% -> 0%
where the time goes in v3:
time: 346 us; the launch traced here: 342 us
  Pallas kernels  236 us (68%)
  waiting for transfers between devices  29.7 us (9%)
  local copies, waits for them, and re-layouts  26.8 us (8%)
  blocking collectives  18.6 us (5%)
  between operations  14.7 us (4%)
  matrix products  9.42 us (3%)
  other arithmetic  7.7 us (2%)
    pallas_call x5, Pallas kernels, _transfer(): pl.pallas_call(functools.partial(_transfer_kernel, axis, gather), out_sha...  236 us
    reduce_scatter x1, waiting for transfers between devices, on_device(): lax.psum_scatter(partial_blocks, 'tp', scatter_dimension=0, tiled=False)  29.7 us
    psum x1, blocking collectives, on_device(): lax.psum(jnp.sum(own_state * own_state, axis=1, keepdims=True), 'tp')  18.6 us
    concatenate x4, local copies, waits for them, and re-layouts, on_device(): gate_and_up = jnp.concatenate([expert_gate[0], expert_up[0]], axis=1)  7.86 us
  transfers between devices with their start and end apart: 1, of which 1 were waited for; matrix products, arithmetic and copies ran while one was open for 4% of the time, Pallas kernels for 0%

profile of v3, /device:TPU:24, one launch (start us, length us, event | category | flops | bytes accessed | tf_op | source)
XLA Modules:
  0.0 342.5 jit_solution(6136848199122486958)
XLA Ops:
  9.4 26.8 %shard_map.145 = bf16[64,8,128]{2,1,0:T(8,128)(2,1)} custom-call(bf16[64,8,128]{2,1,0:T(8,128)(2,1)} %bitcast.86), custom_call_target="tpu_custom_call" | custom-call | tf_op jit(solution)/shard_map/pallas_call | solution.py:72
  36.3 1.0 concatenate.55
  42.2 1.5 convolution_bitcast_fusion.1
  45.0 2.8 concatenate.60
  47.7 1.2 copy.89
  48.9 2.8 concatenate.61
  51.7 1.1 copy.90
  52.8 1.4 reshape_squeeze.3
  54.4 1.9 gather_fusion.2
  57.9 29.7 %reduce-scatter.2.cloned.1.call-done = f32[1,64,360]{2,1,0:T(8,128)} async-done(((f32[8,64,360]{2,1,0:T(8,128)}), f32[1,64,360]{2,1,0:T(8,128)}) %reduce-scatter.2.cloned.1.call-update) | async-done | bytes 92176 | tf_op jit(solution)/shard_map/reduce_scatter | solution.py:186
  87.6 1.0 multiply_reduce_fusion.1
  88.6 18.6 %psum.7 = f32[64,1]{0,1:T(1,128)S(1)} all-reduce(f32[64,1]{0,1:T(1,128)S(1)} %bitcast.89), channel_id=1, replica_groups=mesh['group'=64,'tp'=8] {'tp'}, use_global_device_ids=true, to_apply=%region_8.9 | all-reduce | flops 64 | bytes 512 | tf_op jit(solution)/shard_map/psum | solution.py:188
  107.2 1.0 multiply_convert_fusion
  108.1 2.0 gather_fusion
  111.5 51.9 %shard_map.146 = bf16[64,10,360]{2,1,0:T(8,128)(2,1)} custom-call(bf16[64,10,360]{2,1,0:T(8,128)(2,1)} %bitcast.79), custom_call_target="tpu_custom_call" | custom-call | tf_op jit(solution)/shard_map/pallas_call | solution.py:72
  163.4 2.2 reshape.385.x_ref
  165.6 72.8 %shard_map.147 = bf16[8,640,360]{2,1,0:T(8,128)(2,1)} custom-call(bf16[640,360]{1,0:T(8,128)(2,1)} %reshape.385.x_ref), custom_call_target="tpu_custom_call" | custom-call | tf_op jit(solution)/shard_map/pallas_call | solution.py:72
  238.4 4.7 %fusion.4 = f32[640,360]{0,1:T(8,128)S(1)} fusion(bf16[8,640,360]{2,1,0:T(8,128)(2,1)} %shard_map.147, bf16[8,360,180]{1,2,0:T(8,128)(2,1)} %copy.90, bf16[8,360,180]{1,2,0:T(8,128)(2,1)} %copy.89), kind=kOutput, calls=%fused_computation.7 | convolution fusion | flops 1331251200 | bytes 6681600 | tf_op jit(solution)/shard_map/tsf,tfh->sh/dot_general | solution.py:219
  244.0 33.9 %shard_map.148 = bf16[8,180,640]{2,1,0:T(8,128)(2,1)} custom-call(bf16[180,640]{1,0:T(8,128)(2,1)} %fusion.17.x_ref), custom_call_target="tpu_custom_call" | custom-call | tf_op jit(solution)/shard_map/pallas_call | solution.py:72
  277.9 2.6 fusion.8
  280.8 1.1 reshape.386.x_ref
  281.9 50.1 %shard_map.149 = bf16[64,10,360]{2,1,0:T(8,128)(2,1)} custom-call(bf16[64,10,360]{2,1,0:T(8,128)(2,1)} %reshape.386.x_ref), custom_call_target="tpu_custom_call" | custom-call | tf_op jit(solution)/shard_map/pallas_call | solution.py:72
  332.0 1.3 convert.22
  333.5 1.0 gather_fusion.1
  (89 shorter events, 13.4 us)
Async XLA Ops:
  6.5 35.7 %copy-start = (bf16[256,2880]{0,1:T(8,128)(2,1)S(1)}, bf16[256,2880]{0,1:T(8,128)(2,1)}, u32[]{:S(2)}) copy-start(bf16[256,2880]{0,1:T(8,128)(2,1)} %param.22) | copy-start | bytes 4423684
  6.5 81.0 %reduce-scatter.2.cloned.1.call-start = ((), (), s32[]{:S(2)}) async-start(), calls=%async_computation.1 | async-start | bytes 884736 | tf_op jit(solution)/shard_map/reduce_scatter | solution.py:186
  8.2 31.2 %copy-start.6 = (s32[1,64]{1,0:T(1,128)S(1)}, s32[1,64]{1,0:T(1,128)}, u32[]{:S(2)}) copy-start(s32[1,64]{1,0:T(1,128)} %param.19) | copy-start | bytes 772
  38.4 2.1 copy-start.5
  42.2 1.5 copy-start.3
  54.4 2.5 copy-start.4
  54.4 33.2 %copy-start.2 = (bf16[64,360]{1,0:T(8,128)(2,1)S(1)}, bf16[64,360]{1,0:T(8,128)(2,1)}, u32[]{:S(2)}) copy-start(bf16[64,360]{1,0:T(8,128)(2,1)} %param.23) | copy-start | bytes 138244
  333.5 1.5 copy-start.1
Sparse Core Ops, SparseCore 0:
  43.8 43.6 reduce-scatter.1

commit v4 on v3

--- a/solution.py
+++ b/solution.py
@@ -19,10 +19,20 @@
     count = buf.shape[0]
     group_at = lax.axis_index("group")
     tp_at = lax.axis_index("tp")
-    me = tp_at if axis == "tp" else group_at
+    core = lax.rem(group_at, 2)
+    if axis == "tp":
+        me = tp_at
+    elif axis == "pair":
+        me = lax.div(group_at, 2)
+    else:
+        me = group_at
 
     def device(peer):
-        return (group_at, peer) if axis == "tp" else (peer, tp_at)
+        if axis == "tp":
+            return (group_at, peer)
+        if axis == "pair":
+            return (2 * peer + core, tp_at)
+        return (peer, tp_at)
 
     def piece(peer):
         return x_ref if gather else x_ref.at[peer]
@@ -67,7 +77,7 @@
 
 
 def _transfer(x, axis, gather, collective_id):
-    count = lax.axis_size(axis)
+    count = lax.axis_size("group") // 2 if axis == "pair" else lax.axis_size(axis)
     shape = ((count,) + x.shape) if gather else x.shape
     return pl.pallas_call(
         functools.partial(_transfer_kernel, axis, gather),
@@ -82,6 +92,79 @@
         ],
         compiler_params=pltpu.CompilerParams(collective_id=collective_id, has_side_effects=True),
     )(x)
+
+
+def _pair_gather_kernel(x_ref, o_ref, buf, send_sem, recv_sem, local_sem, pass_send, pass_recv):
+    count = buf.shape[0]
+    group_at = lax.axis_index("group")
+    tp_at = lax.axis_index("tp")
+    core = lax.rem(group_at, 2)
+    sibling = (group_at + 1 - 2 * core, tp_at)
+    barrier = pltpu.get_barrier_semaphore()
+
+    def greet(step, carry):
+        peer = lax.rem(tp_at + step, count)
+        pl.semaphore_signal(barrier, inc=1, device_id=(group_at, peer), device_id_type=pl.DeviceIdType.MESH)
+        return carry
+
+    lax.fori_loop(1, count, greet, 0)
+    pl.semaphore_signal(barrier, inc=1, device_id=sibling, device_id_type=pl.DeviceIdType.MESH)
+    pl.semaphore_wait(barrier, count)
+    local = pltpu.make_async_copy(x_ref, buf.at[tp_at, core], local_sem)
+    local.start()
+
+    def send(step, carry):
+        peer = lax.rem(tp_at + step, count)
+        pltpu.make_async_remote_copy(
+            src_ref=x_ref,
+            dst_ref=buf.at[tp_at, core],
+            send_sem=send_sem,
+            recv_sem=recv_sem,
+            device_id=(group_at, peer),
+            device_id_type=pl.DeviceIdType.MESH,
+        ).start()
+        return carry
+
+    lax.fori_loop(1, count, send, 0)
+    local.wait()
+    every = pltpu.make_async_remote_copy(
+        src_ref=buf.at[pl.ds(0, count - 1), 0],
+        dst_ref=buf.at[pl.ds(0, count - 1), 0],
+        send_sem=send_sem,
+        recv_sem=recv_sem,
+        device_id=(group_at, lax.rem(tp_at + 1, count)),
+        device_id_type=pl.DeviceIdType.MESH,
+    )
+    every.wait_recv()
+    onward = pltpu.make_async_remote_copy(
+        src_ref=buf.at[:, core],
+        dst_ref=buf.at[:, core],
+        send_sem=pass_send,
+        recv_sem=pass_recv,
+        device_id=sibling,
+        device_id_type=pl.DeviceIdType.MESH,
+    )
+    onward.start()
+    every.wait_send()
+    onward.wait_send()
+    onward.wait_recv()
+    o_ref[...] = buf[...]
+
+
+def pair_gather(x, collective_id):
+    shape = (lax.axis_size("tp"), 2) + x.shape
+    return pl.pallas_call(
+        _pair_gather_kernel,
+        out_shape=jax.ShapeDtypeStruct(shape, x.dtype),
+        in_specs=[pl.BlockSpec(memory_space=pltpu.VMEM)],
+        out_specs=pl.BlockSpec(memory_space=pltpu.VMEM),
+        scratch_shapes=[pltpu.VMEM(shape, x.dtype)] + [pltpu.SemaphoreType.DMA(())] * 5,
+        compiler_params=pltpu.CompilerParams(collective_id=collective_id, has_side_effects=True),
+    )(x)
+
+
+def pair_exchange(x, collective_id):
+    return _transfer(x, "pair", False, collective_id)
 
 
 def group_exchange(x, collective_id):
@@ -206,15 +289,10 @@
     ).astype(jnp.bfloat16)
     hidden_part = expert_gate.shape[2]
     gate_and_up = jnp.concatenate([expert_gate[0], expert_up[0]], axis=1)
-    outgoing = send_own
-    feature_count = outgoing.shape[1]
-    outgoing = outgoing.reshape(experts, 1, capacity, feature_count)
-    outgoing = jnp.broadcast_to(outgoing, (experts, 2, capacity, feature_count)).reshape(
-        groups, capacity, feature_count
-    )
-    received = group_exchange(outgoing, 2)
+    received = pair_exchange(send_own.reshape(experts, capacity, -1), 2)
     sources, slot_count, part_features = received.shape
-    whole = tp_gather(received.reshape(sources * slot_count, part_features), 4)
+    whole = pair_gather(received.reshape(sources * slot_count, part_features), 4)
+    whole = whole.reshape(tp_count, 2 * sources * slot_count, part_features)
     gate_blocks = gate_and_up.reshape(tp_count, part_features, gate_and_up.shape[1])
     both = jnp.einsum("tsf,tfh->sh", whole, gate_blocks, preferred_element_type=jnp.float32)
     gate_val = both[:, :hidden_part]
@@ -225,10 +303,16 @@
     result = jnp.einsum("ths,thd->sd", joined, down_blocks, preferred_element_type=jnp.float32).astype(
         jnp.bfloat16
     )
-    returned = result.reshape(sources, slot_count, result.shape[1])
-    arrived = group_exchange(returned, 3)
-    halves = arrived.reshape(experts, 2, capacity, width).astype(jnp.float32)
-    summed = (halves[:, 0] + halves[:, 1]).reshape(experts * capacity, width)
+    halves = result.reshape(2, experts, capacity, width)
+    core = lax.rem(lax.axis_index("group"), 2)
+    groups_total = lax.axis_size("group")
+    swap = [(i, i + 1 - 2 * (i % 2)) for i in range(groups_total)]
+    mine = lax.dynamic_index_in_dim(halves, core, 0, keepdims=False)
+    theirs = lax.dynamic_index_in_dim(halves, 1 - core, 0, keepdims=False)
+    other_half = lax.ppermute(theirs, "group", swap)
+    joined_halves = (mine.astype(jnp.float32) + other_half.astype(jnp.float32)).astype(jnp.bfloat16)
+    arrived = pair_exchange(joined_halves, 3)
+    summed = arrived.astype(jnp.float32).reshape(experts * capacity, width)
     rank_at = jnp.take_along_axis(slot_rank, routes, axis=1)
     picked = jnp.take(summed, (routes * capacity + rank_at).reshape(-1), axis=0).reshape(
         block_len, top_count, width

time: 346 us -> 269 us (0.78)
  Pallas kernels: 236 us -> 158 us
    pallas_call x5 -> x4, Pallas kernels: 236 us -> 124 us  [_transfer(): pl.pallas_call(functools.partial(_transfer_kernel, axis, gather), out_sha...]
    pallas_call x0 -> x1, Pallas kernels: none -> 33.4 us  [pair_gather(): pl.pallas_call(_pair_gather_kernel, out_shape=jax.ShapeDtypeStruct(shape,...]
  transfers between devices with their start and end apart: 1 -> 2, of which waited for: 1 -> 2; matrix products, arithmetic and copies ran while one was open for 4% -> 5% of each run, Pallas kernels for 0% -> 0%
where the time goes in v4:
time: 269 us; the launch traced here: 267 us
  Pallas kernels  158 us (59%)
  waiting for transfers between devices  31.4 us (12%)
  local copies, waits for them, and re-layouts  25.7 us (10%)
  blocking collectives  18.6 us (7%)
  between operations  14.7 us (5%)
  matrix products  9.42 us (4%)
  other arithmetic  7.87 us (3%)
    pallas_call x4, Pallas kernels, _transfer(): pl.pallas_call(functools.partial(_transfer_kernel, axis, gather), out_sha...  124 us
    pallas_call x1, Pallas kernels, pair_gather(): pl.pallas_call(_pair_gather_kernel, out_shape=jax.ShapeDtypeStruct(shape,...  33.4 us
    reduce_scatter x1, waiting for transfers between devices, on_device(): lax.psum_scatter(partial_blocks, 'tp', scatter_dimension=0, tiled=False)  29.7 us
    psum x1, blocking collectives, on_device(): lax.psum(jnp.sum(own_state * own_state, axis=1, keepdims=True), 'tp')  18.6 us
    concatenate x4, local copies, waits for them, and re-layouts, on_device(): gate_and_up = jnp.concatenate([expert_gate[0], expert_up[0]], axis=1)  7.86 us
  transfers between devices with their start and end apart: 2, of which 2 were waited for; matrix products, arithmetic and copies ran while one was open for 5% of the time, Pallas kernels for 0%

profile of v4, /device:TPU:24, one launch (start us, length us, event | category | flops | bytes accessed | tf_op | source)
XLA Modules:
  0.0 267.4 jit_solution(12661074292620204455)
XLA Ops:
  9.4 26.8 %shard_map.145 = bf16[64,8,128]{2,1,0:T(8,128)(2,1)} custom-call(bf16[64,8,128]{2,1,0:T(8,128)(2,1)} %bitcast.78), custom_call_target="tpu_custom_call" | custom-call | tf_op jit(solution)/shard_map/pallas_call | solution.py:82
  36.3 1.0 concatenate.55
  42.2 1.5 convolution_bitcast_fusion.1
  45.0 2.8 %concatenate.60 = bf16[8,360,180]{1,0,2:T(8,128)(2,1)S(1)} reshape(bf16[1,2880,180]{1,2,0:T(8,128)(2,1)} %param.27) | data formatting | bytes 2073600 | tf_op jit(solution)/shard_map/concatenate | solution.py:291
  47.7 1.2 copy.85
  48.9 2.8 %concatenate.61 = bf16[8,360,180]{1,0,2:T(8,128)(2,1)S(1)} reshape(bf16[1,2880,180]{1,2,0:T(8,128)(2,1)} %param.28) | data formatting | bytes 2073600 | tf_op jit(solution)/shard_map/concatenate | solution.py:291
  51.7 1.1 copy.86
  52.8 1.4 reshape_squeeze.3
  54.4 1.9 gather_fusion.2
  57.9 29.7 %reduce-scatter.2.cloned.1.call-done = f32[1,64,360]{2,1,0:T(8,128)} async-done(((f32[8,64,360]{2,1,0:T(8,128)}), f32[1,64,360]{2,1,0:T(8,128)}) %reduce-scatter.2.cloned.1.call-update) | async-done | bytes 92176 | tf_op jit(solution)/shard_map/reduce_scatter | solution.py:269
  87.6 1.0 multiply_reduce_fusion.1
  88.6 18.6 %psum.7 = f32[64,1]{0,1:T(1,128)S(1)} all-reduce(f32[64,1]{0,1:T(1,128)S(1)} %bitcast.81), channel_id=1, replica_groups=mesh['group'=64,'tp'=8] {'tp'}, use_global_device_ids=true, to_apply=%region_8.9 | all-reduce | flops 64 | bytes 512 | tf_op jit(solution)/shard_map/psum | solution.py:271
  108.2 2.0 gather_fusion
  111.3 26.5 %shard_map.146 = bf16[32,10,360]{2,1,0:T(8,128)(2,1)} custom-call(bf16[32,10,360]{2,1,0:T(8,128)(2,1)} %select_multiply_fusion.x_ref), custom_call_target="tpu_custom_call" | custom-call | tf_op jit(solution)/shard_map/pallas_call | solution.py:82
  137.8 1.8 reshape.376.x_ref
  139.7 33.4 %shard_map.147 = bf16[8,2,320,360]{3,2,1,0:T(8,128)(2,1)} custom-call(bf16[320,360]{1,0:T(8,128)(2,1)} %reshape.376.x_ref), custom_call_target="tpu_custom_call" | custom-call | tf_op jit(solution)/shard_map/pallas_call | solution.py:156
  173.1 4.7 %fusion.4 = f32[640,360]{0,1:T(8,128)S(1)} fusion(bf16[8,640,360]{2,1,0:T(8,128)(2,1)} %bitcast.72, bf16[8,360,180]{1,2,0:T(8,128)(2,1)} %copy.86, bf16[8,360,180]{1,2,0:T(8,128)(2,1)} %copy.85), kind=kOutput, calls=%fused_computation.7 | convolution fusion | flops 1331251200 | bytes 6681600 | tf_op jit(solution)/shard_map/tsf,tfh->sh/dot_general | solution.py:297
  178.7 36.6 %shard_map.148 = bf16[8,180,640]{2,1,0:T(8,128)(2,1)} custom-call(bf16[180,640]{1,0:T(8,128)(2,1)} %fusion.17.x_ref), custom_call_target="tpu_custom_call" | custom-call | tf_op jit(solution)/shard_map/pallas_call | solution.py:82
  215.3 2.6 fusion.8
  218.4 1.9 collective-permute-start
  220.4 1.7 collective-permute-done
  222.9 34.4 %shard_map.149 = bf16[32,10,360]{2,1,0:T(8,128)(2,1)} custom-call(bf16[32,10,360]{2,1,0:T(8,128)(2,1)} %fusion.10.x_ref), custom_call_target="tpu_custom_call" | custom-call | tf_op jit(solution)/shard_map/pallas_call | solution.py:82
  257.3 1.1 reshape.387
  258.5 1.0 gather_fusion.1
  (90 shorter events, 15.1 us)
Async XLA Ops:
  6.5 35.7 %copy-start = (bf16[256,2880]{0,1:T(8,128)(2,1)S(1)}, bf16[256,2880]{0,1:T(8,128)(2,1)}, u32[]{:S(2)}) copy-start(bf16[256,2880]{0,1:T(8,128)(2,1)} %param.22) | copy-start | bytes 4423684
  6.5 81.0 %reduce-scatter.2.cloned.1.call-start = ((), (), s32[]{:S(2)}) async-start(), calls=%async_computation.1 | async-start | bytes 884736 | tf_op jit(solution)/shard_map/reduce_scatter | solution.py:269
  8.2 31.2 %copy-start.6 = (s32[1,64]{1,0:T(1,128)S(1)}, s32[1,64]{1,0:T(1,128)}, u32[]{:S(2)}) copy-start(s32[1,64]{1,0:T(1,128)} %param.19) | copy-start | bytes 772
  38.4 2.1 copy-start.5
  42.2 1.5 copy-start.3
  54.4 2.5 copy-start.4
  54.4 33.1 %copy-start.2 = (bf16[64,360]{1,0:T(8,128)(2,1)S(1)}, bf16[64,360]{1,0:T(8,128)(2,1)}, u32[]{:S(2)}) copy-start(bf16[64,360]{1,0:T(8,128)(2,1)} %param.23) | copy-start | bytes 138244
  218.4 3.6 %collective-permute-start = (bf16[32,10,360]{2,1,0:T(8,128)(2,1)S(1)}, bf16[32,10,360]{2,1,0:T(8,128)(2,1)S(1)}, u32[]{:S(2)}, u32[]{:S(2)}) collective-permute-start(bf16[32,10,360]{2,1,0:T(8,128)(2,1)S(1)} %dynamic-slice_bitcast_fusion), channel_id=1, source_target_pairs={{0,8},{8,0},{16,24},{24,16},{32,40},{40,32},{48,56},{56,48},{64,72... | collective-permute-start | bytes 691208 | tf_op jit(solution)/shard_map/ppermute | solution.py:312
  258.5 1.5 copy-start.1
Sparse Core Ops, SparseCore 0:
  43.8 43.6 reduce-scatter.1

commit v5 on v4

--- a/solution.py
+++ b/solution.py
@@ -169,6 +169,10 @@
 
 def group_exchange(x, collective_id):
     return _transfer(x, "group", False, collective_id)
+
+
+def tp_exchange(x, collective_id):
+    return _transfer(x, "tp", False, collective_id)
 
 
 def tp_gather(x, collective_id):
@@ -266,11 +270,17 @@
     own_gain = lax.dynamic_slice_in_dim(norm_gain, start, width, 0)
     partial_sum = jnp.dot(attended, out_weight, preferred_element_type=jnp.float32)
     partial_blocks = partial_sum.reshape(partial_sum.shape[0], tp_count, width).transpose(1, 0, 2)
-    own_attn = lax.psum_scatter(partial_blocks, "tp", scatter_dimension=0, tiled=False)
+    own_attn = jnp.sum(tp_exchange(partial_blocks, 6), axis=0)
     own_state = own_attn + residual.astype(jnp.float32)
-    square_sum = lax.psum(jnp.sum(own_state * own_state, axis=1, keepdims=True), "tp")
-    mean_square = square_sum / (width * tp_count)
-    normed_own = (own_state * lax.rsqrt(mean_square + EPSILON) * own_gain).astype(jnp.bfloat16)
+    square_sum = jnp.sum(own_state * own_state, axis=1, keepdims=True)
+    square_high = square_sum.astype(jnp.bfloat16)
+    square_low = (square_sum - square_high.astype(jnp.float32)).astype(jnp.bfloat16)
+    row_width = -(-(width + 2) // 128) * 128
+    scaled_own = (own_state * own_gain).astype(jnp.bfloat16)
+    normed_own = jnp.concatenate(
+        [scaled_own, square_high, square_low, jnp.zeros((own_state.shape[0], row_width - width - 2), jnp.bfloat16)],
+        axis=1,
+    )
     block_len = normed_own.shape[0]
     top_count = routes.shape[1]
     experts = groups // 2
@@ -293,8 +303,11 @@
     sources, slot_count, part_features = received.shape
     whole = pair_gather(received.reshape(sources * slot_count, part_features), 4)
     whole = whole.reshape(tp_count, 2 * sources * slot_count, part_features)
-    gate_blocks = gate_and_up.reshape(tp_count, part_features, gate_and_up.shape[1])
-    both = jnp.einsum("tsf,tfh->sh", whole, gate_blocks, preferred_element_type=jnp.float32)
+    gate_blocks = gate_and_up.reshape(tp_count, width, gate_and_up.shape[1])
+    total_square = jnp.sum(whole[:, :, width:width + 2].astype(jnp.float32), axis=(0, 2))
+    row_scale = lax.rsqrt(total_square / (width * tp_count) + EPSILON)
+    both = jnp.einsum("tsf,tfh->sh", whole[:, :, :width], gate_blocks, preferred_element_type=jnp.float32)
+    both = both * row_scale[:, None]
     gate_val = both[:, :hidden_part]
     up_val = both[:, hidden_part:]
     active = (gate_val * jax.nn.sigmoid(ALPHA * gate_val) * (up_val + 1.0)).astype(jnp.bfloat16)

time: 269 us -> 233 us (0.87)
  waiting for transfers between devices: 31.4 us -> 0.01 us
  Pallas kernels: 158 us -> 182 us
  blocking collectives: 18.6 us -> 0 us
  between operations: 14.7 us -> 1.32 us
    reduce_scatter x1 -> x0, waiting for transfers between devices: 29.7 us -> none  [on_device(): lax.psum_scatter(partial_blocks, 'tp', scatter_dimension=0, tiled=False)]
    psum x1 -> x0, blocking collectives: 18.6 us -> none  [on_device(): lax.psum(jnp.sum(own_state * own_state, axis=1, keepdims=True), 'tp')]
    pallas_call x4 -> x5, Pallas kernels: 124 us -> 143 us  [_transfer(): pl.pallas_call(functools.partial(_transfer_kernel, axis, gather), out_sha...]
    pallas_call x1, Pallas kernels: 33.4 us -> 39.1 us  [pair_gather(): pl.pallas_call(_pair_gather_kernel, out_shape=jax.ShapeDtypeStruct(shape,...]
  transfers between devices with their start and end apart: 2 -> 1, of which waited for: 2 -> 0; matrix products, arithmetic and copies ran while one was open for 5% -> 1% of each run, Pallas kernels for 0% -> 0%
where the time goes in v5:
time: 233 us; the launch traced here: 231 us
  Pallas kernels  182 us (78%)
  local copies, waits for them, and re-layouts  26.3 us (11%)
  other arithmetic  9.85 us (4%)
  matrix products  9.61 us (4%)
    pallas_call x5, Pallas kernels, _transfer(): pl.pallas_call(functools.partial(_transfer_kernel, axis, gather), out_sha...  143 us
    pallas_call x1, Pallas kernels, pair_gather(): pl.pallas_call(_pair_gather_kernel, out_shape=jax.ShapeDtypeStruct(shape,...  39.1 us
    concatenate x4, local copies, waits for them, and re-layouts, on_device(): gate_and_up = jnp.concatenate([expert_gate[0], expert_up[0]], axis=1)  7.86 us
  transfers between devices with their start and end apart: 1, of which 0 were waited for; matrix products, arithmetic and copies ran while one was open for 1% of the time, Pallas kernels for 0%

profile of v5, /device:TPU:24, one launch (start us, length us, event | category | flops | bytes accessed | tf_op | source)
XLA Modules:
  0.0 230.8 jit_solution(13196861768803882314)
XLA Ops:
  3.7 26.8 %shard_map.145 = bf16[64,8,128]{2,1,0:T(8,128)(2,1)} custom-call(bf16[64,8,128]{2,1,0:T(8,128)(2,1)} %bitcast.76), custom_call_target="tpu_custom_call" | custom-call | tf_op jit(solution)/shard_map/pallas_call | solution.py:82
  30.6 1.0 concatenate.58
  34.8 1.5 convolution_bitcast_fusion.1.x_ref
  36.2 18.3 %shard_map.146 = f32[8,64,360]{2,1,0:T(8,128)} custom-call(f32[8,64,360]{2,1,0:T(8,128)} %convolution_bitcast_fusion.1.x_ref), custom_call_target="tpu_custom_call" | custom-call | tf_op jit(solution)/shard_map/pallas_call | solution.py:82
  55.3 1.2 reduce_sum.75
  57.6 2.8 %concatenate.65 = bf16[8,360,180]{1,0,2:T(8,128)(2,1)S(1)} reshape(bf16[1,2880,180]{1,2,0:T(8,128)(2,1)} %param.28) | data formatting | bytes 2073600 | tf_op jit(solution)/shard_map/concatenate | solution.py:301
  60.3 1.1 copy.95
  61.5 2.8 %concatenate.64 = bf16[8,360,180]{1,0,2:T(8,128)(2,1)S(1)} reshape(bf16[1,2880,180]{1,2,0:T(8,128)(2,1)} %param.27) | data formatting | bytes 2073600 | tf_op jit(solution)/shard_map/concatenate | solution.py:301
  64.3 1.2 copy.94
  66.0 2.0 gather_fusion
  69.3 30.8 %shard_map.147 = bf16[32,10,384]{2,1,0:T(8,128)(2,1)} custom-call(bf16[32,10,384]{2,1,0:T(8,128)(2,1)} %select_multiply_fusion.x_ref), custom_call_target="tpu_custom_call" | custom-call | tf_op jit(solution)/shard_map/pallas_call | solution.py:82
  100.1 1.8 reshape.405.x_ref
  101.9 39.1 %shard_map.148 = bf16[8,2,320,384]{3,2,1,0:T(8,128)(2,1)} custom-call(bf16[320,384]{1,0:T(8,128)(2,1)} %reshape.405.x_ref), custom_call_target="tpu_custom_call" | custom-call | tf_op jit(solution)/shard_map/pallas_call | solution.py:156
  141.0 1.9 convert_reduce_fusion
  142.9 4.4 %fusion.11 = f32[640,360]{0,1:T(8,128)S(1)} fusion(bf16[8,360,180]{1,2,0:T(8,128)(2,1)S(1)} %copy-done.2, bf16[8,360,180]{1,2,0:T(8,128)(2,1)} %copy.94, bf16[8,640,384]{2,1,0:T(8,128)(2,1)} %bitcast.70, f32[640]{0:T(1024)S(1)} %add_rsqrt_fusion), kind=kOutput, calls=%fused_computation.13 | convolution fusion | flops 1331481600 | bytes 6929920 | tf_op jit(solution)/shard_map/tsf,tfh->sh/dot_general | solution.py:309
  148.2 37.4 %shard_map.149 = bf16[8,180,640]{2,1,0:T(8,128)(2,1)} custom-call(bf16[180,640]{1,0:T(8,128)(2,1)} %fusion.25.x_ref), custom_call_target="tpu_custom_call" | custom-call | tf_op jit(solution)/shard_map/pallas_call | solution.py:82
  185.6 2.3 %reshape_squeeze.3 = bf16[8,180,360]{2,1,0:T(8,128)(2,1)} reshape(bf16[1,1440,360]{2,1,0:T(8,128)(2,1)} %param.29) | data formatting | bytes 2073600 | tf_op jit(solution)/shard_map/reshape;squeeze | solution.py:315
  187.9 3.1 %fusion.16 = bf16[640,360]{0,1:T(8,128)(2,1)} fusion(bf16[8,180,640]{2,1,0:T(8,128)(2,1)S(1)} %copy-done.1, bf16[8,180,360]{2,1,0:T(8,128)(2,1)} %reshape_squeeze.3), kind=kOutput, calls=%fused_computation.15 | convolution fusion | flops 663782400 | bytes 3340800 | tf_op jit(solution)/shard_map/ths,thd->sd/dot_general | solution.py:316
  191.0 1.3 copy.96
  192.6 1.9 collective-permute-start
  194.7 1.9 gather_fusion.2
  198.2 29.4 %shard_map.150 = bf16[32,10,360]{2,1,0:T(8,128)(2,1)} custom-call(bf16[32,10,360]{2,1,0:T(8,128)(2,1)} %fusion.18.x_ref), custom_call_target="tpu_custom_call" | custom-call | tf_op jit(solution)/shard_map/pallas_call | solution.py:82
  227.6 1.1 reshape.416
  228.7 1.0 gather_fusion.1
  (99 shorter events, 13.4 us)
Async XLA Ops:
  0.0 34.7 %copy-start = (bf16[256,2880]{0,1:T(8,128)(2,1)S(1)}, bf16[256,2880]{0,1:T(8,128)(2,1)}, u32[]{:S(2)}) copy-start(bf16[256,2880]{0,1:T(8,128)(2,1)} %param.22) | copy-start | bytes 4423684
  0.0 31.6 %copy-start.4 = (bf16[256,128]{1,0:T(8,128)(2,1)S(1)}, bf16[256,128]{1,0:T(8,128)(2,1)}, u32[]{:S(2)}) copy-start(bf16[256,128]{1,0:T(8,128)(2,1)} %param.17) | copy-start | bytes 196612
  2.5 30.4 %copy-start.5 = (bf16[64,256]{1,0:T(8,128)(2,1)S(1)}, bf16[64,256]{1,0:T(8,128)(2,1)}, u32[]{:S(2)}) copy-start(bf16[64,256]{1,0:T(8,128)(2,1)} %param.15) | copy-start | bytes 98308
  3.4 29.7 %copy-start.8 = (f32[4]{0:T(128)S(1)}, f32[4]{0:T(128)}, u32[]{:S(2)}) copy-start(f32[4]{0:T(128)} %param.21) | copy-start | bytes 52
  36.2 20.3 %copy-start.3 = (bf16[64,360]{1,0:T(8,128)(2,1)S(1)}, bf16[64,360]{1,0:T(8,128)(2,1)}, u32[]{:S(2)}) copy-start(bf16[64,360]{1,0:T(8,128)(2,1)} %param.23) | copy-start | bytes 138244
  36.2 20.4 %copy-start.6 = (s32[64,4]{0,1:T(4,128)S(1)}, s32[64,4]{0,1:T(4,128)}, u32[]{:S(2)}) copy-start(s32[64,4]{0,1:T(4,128)} %param.25) | copy-start | bytes 3076
  101.9 41.0 %copy-start.2 = (bf16[8,360,180]{1,2,0:T(8,128)(2,1)S(1)}, bf16[8,360,180]{1,2,0:T(8,128)(2,1)}, u32[]{:S(2)}) copy-start(bf16[8,360,180]{1,2,0:T(8,128)(2,1)} %copy.95) | copy-start | bytes 3110404
  185.6 2.3 %copy-start.1 = (bf16[8,180,640]{2,1,0:T(8,128)(2,1)S(1)}, bf16[8,180,640]{2,1,0:T(8,128)(2,1)}, u32[]{:S(2)}) copy-start(bf16[8,180,640]{2,1,0:T(8,128)(2,1)} %shard_map.149) | copy-start | bytes 5529604
  192.6 4.8 %collective-permute-start = (bf16[32,10,360]{2,1,0:T(8,128)(2,1)S(1)}, bf16[32,10,360]{2,1,0:T(8,128)(2,1)S(1)}, u32[]{:S(2)}, u32[]{:S(2)}) collective-permute-start(bf16[32,10,360]{2,1,0:T(8,128)(2,1)S(1)} %dynamic-slice_bitcast_fusion), channel_id=1, source_target_pairs={{0,8},{8,0},{16,24},{24,16},{32,40},{40,32},{48,56},{56,48},{64,72... | collective-permute-start | bytes 691208 | tf_op jit(solution)/shard_map/ppermute | solution.py:325
  194.7 2.4 %copy-start.7 = (f32[64,4]{0,1:T(4,128)S(1)}, f32[64,4]{0,1:T(4,128)}, u32[]{:S(2)}) copy-start(f32[64,4]{0,1:T(4,128)} %param.26) | copy-start | bytes 3076

commit v6 on v5

--- a/solution.py
+++ b/solution.py
@@ -232,6 +232,13 @@
     )
     outputs = blended.astype(jnp.bfloat16).reshape(block_len, group_size * HEAD)
     return outputs
+
+
+def lane_dense(rows):
+    count, length = rows.shape
+    padded = -(-length // 128) * 128
+    rows = jnp.pad(rows, ((0, 0), (0, padded - length)))
+    return rows.reshape(count, padded // 128, 128)
 
 
 def on_device(
@@ -299,7 +306,9 @@
     ).astype(jnp.bfloat16)
     hidden_part = expert_gate.shape[2]
     gate_and_up = jnp.concatenate([expert_gate[0], expert_up[0]], axis=1)
-    received = pair_exchange(send_own.reshape(experts, capacity, -1), 2)
+    row_width = send_own.shape[1]
+    received = pair_exchange(lane_dense(send_own.reshape(experts, capacity * row_width)), 2)
+    received = received.reshape(experts, -1)[:, : capacity * row_width].reshape(experts, capacity, row_width)
     sources, slot_count, part_features = received.shape
     whole = pair_gather(received.reshape(sources * slot_count, part_features), 4)
     whole = whole.reshape(tp_count, 2 * sources * slot_count, part_features)
@@ -324,8 +333,8 @@
     theirs = lax.dynamic_index_in_dim(halves, 1 - core, 0, keepdims=False)
     other_half = lax.ppermute(theirs, "group", swap)
     joined_halves = (mine.astype(jnp.float32) + other_half.astype(jnp.float32)).astype(jnp.bfloat16)
-    arrived = pair_exchange(joined_halves, 3)
-    summed = arrived.astype(jnp.float32).reshape(experts * capacity, width)
+    arrived = pair_exchange(lane_dense(joined_halves.reshape(experts, capacity * width)), 3)
+    summed = arrived.reshape(experts, -1)[:, : capacity * width].astype(jnp.float32).reshape(experts * capacity, width)
     rank_at = jnp.take_along_axis(slot_rank, routes, axis=1)
     picked = jnp.take(summed, (routes * capacity + rank_at).reshape(-1), axis=0).reshape(
         block_len, top_count, width

time: 233 us -> 224 us (0.961)
  Pallas kernels: 182 us -> 171 us
  local copies, waits for them, and re-layouts: 26.3 us -> 28.8 us
    pallas_call x5, Pallas kernels: 143 us -> 132 us  [_transfer(): pl.pallas_call(functools.partial(_transfer_kernel, axis, gather), out_sha...]
where the time goes in v6:
time: 224 us; the launch traced here: 222 us
  Pallas kernels  171 us (76%)
  local copies, waits for them, and re-layouts  28.8 us (13%)
  matrix products  9.61 us (4%)
  other arithmetic  9.22 us (4%)
    pallas_call x5, Pallas kernels, _transfer(): pl.pallas_call(functools.partial(_transfer_kernel, axis, gather), out_sha...  132 us
    pallas_call x1, Pallas kernels, pair_gather(): pl.pallas_call(_pair_gather_kernel, out_shape=jax.ShapeDtypeStruct(shape,...  39.6 us
    concatenate x4, local copies, waits for them, and re-layouts, on_device(): gate_and_up = jnp.concatenate([expert_gate[0], expert_up[0]], axis=1)  7.86 us
  transfers between devices with their start and end apart: 1, of which 0 were waited for; matrix products, arithmetic and copies ran while one was open for 1% of the time, Pallas kernels for 0%

profile of v6, /device:TPU:24, one launch (start us, length us, event | category | flops | bytes accessed | tf_op | source)
XLA Modules:
  0.0 222.3 jit_solution(12242086979572296365)
XLA Ops:
  3.7 26.8 %shard_map.145 = bf16[64,8,128]{2,1,0:T(8,128)(2,1)} custom-call(bf16[64,8,128]{2,1,0:T(8,128)(2,1)} %bitcast.86), custom_call_target="tpu_custom_call" | custom-call | tf_op jit(solution)/shard_map/pallas_call | solution.py:82
  30.6 1.0 concatenate.58
  34.8 1.5 convolution_bitcast_fusion.1.x_ref
  36.2 18.3 %shard_map.146 = f32[8,64,360]{2,1,0:T(8,128)} custom-call(f32[8,64,360]{2,1,0:T(8,128)} %convolution_bitcast_fusion.1.x_ref), custom_call_target="tpu_custom_call" | custom-call | tf_op jit(solution)/shard_map/pallas_call | solution.py:82
  55.3 1.2 reduce_sum.75
  57.5 2.8 %concatenate.65 = bf16[8,360,180]{1,0,2:T(8,128)(2,1)S(1)} reshape(bf16[1,2880,180]{1,2,0:T(8,128)(2,1)} %param.28) | data formatting | bytes 2073600 | tf_op jit(solution)/shard_map/concatenate | solution.py:308
  60.3 1.1 copy.98
  61.5 2.8 %concatenate.64 = bf16[8,360,180]{1,0,2:T(8,128)(2,1)S(1)} reshape(bf16[1,2880,180]{1,2,0:T(8,128)(2,1)} %param.27) | data formatting | bytes 2073600 | tf_op jit(solution)/shard_map/concatenate | solution.py:308
  64.3 1.2 copy.97
  66.0 2.0 gather_fusion
  68.5 1.0 select_multiply_fusion.x_ref
  69.5 25.1 %shard_map.147 = bf16[32,30,128]{2,1,0:T(8,128)(2,1)} custom-call(bf16[32,30,128]{2,1,0:T(8,128)(2,1)} %select_multiply_fusion.x_ref), custom_call_target="tpu_custom_call" | custom-call | tf_op jit(solution)/shard_map/pallas_call | solution.py:82
  94.6 1.8 reshape_reshape_reshape.3.x_ref
  96.4 39.6 %shard_map.148 = bf16[8,2,320,384]{3,2,1,0:T(8,128)(2,1)} custom-call(bf16[320,384]{1,0:T(8,128)(2,1)} %reshape_reshape_reshape.3.x_ref), custom_call_target="tpu_custom_call" | custom-call | tf_op jit(solution)/shard_map/pallas_call | solution.py:156
  136.0 1.9 convert_reduce_fusion
  137.9 4.4 %fusion.11 = f32[640,360]{0,1:T(8,128)S(1)} fusion(bf16[8,360,180]{1,2,0:T(8,128)(2,1)S(1)} %copy-done.2, bf16[8,360,180]{1,2,0:T(8,128)(2,1)} %copy.97, bf16[8,640,384]{2,1,0:T(8,128)(2,1)} %bitcast.78, f32[640]{0:T(1024)S(1)} %add_rsqrt_fusion), kind=kOutput, calls=%fused_computation.13 | convolution fusion | flops 1331481600 | bytes 6929920 | tf_op jit(solution)/shard_map/tsf,tfh->sh/dot_general | solution.py:318
  143.1 36.8 %shard_map.149 = bf16[8,180,640]{2,1,0:T(8,128)(2,1)} custom-call(bf16[180,640]{1,0:T(8,128)(2,1)} %fusion.25.x_ref), custom_call_target="tpu_custom_call" | custom-call | tf_op jit(solution)/shard_map/pallas_call | solution.py:82
  179.9 2.3 %reshape_squeeze.3 = bf16[8,180,360]{2,1,0:T(8,128)(2,1)} reshape(bf16[1,1440,360]{2,1,0:T(8,128)(2,1)} %param.29) | data formatting | bytes 2073600 | tf_op jit(solution)/shard_map/reshape;squeeze | solution.py:324
  182.2 3.1 %fusion.16 = bf16[640,360]{0,1:T(8,128)(2,1)} fusion(bf16[8,180,640]{2,1,0:T(8,128)(2,1)S(1)} %copy-done.1, bf16[8,180,360]{2,1,0:T(8,128)(2,1)} %reshape_squeeze.3), kind=kOutput, calls=%fused_computation.15 | convolution fusion | flops 663782400 | bytes 3340800 | tf_op jit(solution)/shard_map/ths,thd->sd/dot_general | solution.py:325
  185.3 1.3 copy.99
  187.6 1.9 collective-permute-start
  189.8 2.1 gather_fusion.2
  193.9 24.8 %shard_map.150 = bf16[32,29,128]{2,1,0:T(8,128)(2,1)} custom-call(bf16[32,29,128]{2,1,0:T(8,128)(2,1)} %reshape.412.x_ref), custom_call_target="tpu_custom_call" | custom-call | tf_op jit(solution)/shard_map/pallas_call | solution.py:82
  218.7 1.0 copy.104
  (108 shorter events, 15.1 us)
Async XLA Ops:
  0.0 34.7 %copy-start = (bf16[256,2880]{0,1:T(8,128)(2,1)S(1)}, bf16[256,2880]{0,1:T(8,128)(2,1)}, u32[]{:S(2)}) copy-start(bf16[256,2880]{0,1:T(8,128)(2,1)} %param.22) | copy-start | bytes 4423684
  0.0 31.6 %copy-start.4 = (bf16[256,128]{1,0:T(8,128)(2,1)S(1)}, bf16[256,128]{1,0:T(8,128)(2,1)}, u32[]{:S(2)}) copy-start(bf16[256,128]{1,0:T(8,128)(2,1)} %param.17) | copy-start | bytes 196612
  2.5 30.4 %copy-start.5 = (bf16[64,256]{1,0:T(8,128)(2,1)S(1)}, bf16[64,256]{1,0:T(8,128)(2,1)}, u32[]{:S(2)}) copy-start(bf16[64,256]{1,0:T(8,128)(2,1)} %param.15) | copy-start | bytes 98308
  3.4 29.7 %copy-start.8 = (f32[4]{0:T(128)S(1)}, f32[4]{0:T(128)}, u32[]{:S(2)}) copy-start(f32[4]{0:T(128)} %param.21) | copy-start | bytes 52
  36.2 20.3 %copy-start.3 = (bf16[64,360]{1,0:T(8,128)(2,1)S(1)}, bf16[64,360]{1,0:T(8,128)(2,1)}, u32[]{:S(2)}) copy-start(bf16[64,360]{1,0:T(8,128)(2,1)} %param.23) | copy-start | bytes 138244
  36.2 20.4 %copy-start.6 = (s32[64,4]{0,1:T(4,128)S(1)}, s32[64,4]{0,1:T(4,128)}, u32[]{:S(2)}) copy-start(s32[64,4]{0,1:T(4,128)} %param.25) | copy-start | bytes 3076
  96.4 41.5 %copy-start.2 = (bf16[8,360,180]{1,2,0:T(8,128)(2,1)S(1)}, bf16[8,360,180]{1,2,0:T(8,128)(2,1)}, u32[]{:S(2)}) copy-start(bf16[8,360,180]{1,2,0:T(8,128)(2,1)} %copy.98) | copy-start | bytes 3110404
  179.9 2.3 %copy-start.1 = (bf16[8,180,640]{2,1,0:T(8,128)(2,1)S(1)}, bf16[8,180,640]{2,1,0:T(8,128)(2,1)}, u32[]{:S(2)}) copy-start(bf16[8,180,640]{2,1,0:T(8,128)(2,1)} %shard_map.149) | copy-start | bytes 5529604
  187.6 5.0 %collective-permute-start = (bf16[32,10,360]{2,1,0:T(8,128)(2,1)}, bf16[32,10,360]{2,1,0:T(8,128)(2,1)S(1)}, u32[]{:S(2)}, u32[]{:S(2)}) collective-permute-start(bf16[32,10,360]{2,1,0:T(8,128)(2,1)} %dynamic-slice_bitcast_fusion), channel_id=1, source_target_pairs={{0,8},{8,0},{16,24},{24,16},{32,40},{40,32},{48,56},{56,48},{64,72... | collective-permute-start | bytes 691208 | tf_op jit(solution)/shard_map/ppermute | solution.py:334
  189.7 2.6 %copy-start.7 = (f32[64,4]{0,1:T(4,128)S(1)}, f32[64,4]{0,1:T(4,128)}, u32[]{:S(2)}) copy-start(f32[64,4]{0,1:T(4,128)} %param.26) | copy-start | bytes 3076

commit v7 on v6

--- a/solution.py
+++ b/solution.py
@@ -277,7 +277,7 @@
     own_gain = lax.dynamic_slice_in_dim(norm_gain, start, width, 0)
     partial_sum = jnp.dot(attended, out_weight, preferred_element_type=jnp.float32)
     partial_blocks = partial_sum.reshape(partial_sum.shape[0], tp_count, width).transpose(1, 0, 2)
-    own_attn = jnp.sum(tp_exchange(partial_blocks, 6), axis=0)
+    own_attn = jnp.sum(tp_exchange(partial_blocks.astype(jnp.bfloat16), 6).astype(jnp.float32), axis=0)
     own_state = own_attn + residual.astype(jnp.float32)
     square_sum = jnp.sum(own_state * own_state, axis=1, keepdims=True)
     square_high = square_sum.astype(jnp.bfloat16)

time: 224 us -> 220 us (0.982)
  Pallas kernels: 171 us -> 167 us
    pallas_call x5, Pallas kernels: 132 us -> 127 us  [_transfer(): pl.pallas_call(functools.partial(_transfer_kernel, axis, gather), out_sha...]
where the time goes in v7:
time: 220 us; the launch traced here: 217 us
  Pallas kernels  167 us (76%)
  local copies, waits for them, and re-layouts  28.8 us (13%)
  matrix products  9.47 us (4%)
  other arithmetic  9.1 us (4%)
    pallas_call x5, Pallas kernels, _transfer(): pl.pallas_call(functools.partial(_transfer_kernel, axis, gather), out_sha...  127 us
    pallas_call x1, Pallas kernels, pair_gather(): pl.pallas_call(_pair_gather_kernel, out_shape=jax.ShapeDtypeStruct(shape,...  40.1 us
    concatenate x4, local copies, waits for them, and re-layouts, on_device(): gate_and_up = jnp.concatenate([expert_gate[0], expert_up[0]], axis=1)  7.86 us
  transfers between devices with their start and end apart: 1, of which 0 were waited for; matrix products, arithmetic and copies ran while one was open for 1% of the time, Pallas kernels for 0%

profile of v7, /device:TPU:24, one launch (start us, length us, event | category | flops | bytes accessed | tf_op | source)
XLA Modules:
  0.0 217.4 jit_solution(953176005474019992)
XLA Ops:
  3.7 26.8 %shard_map.145 = bf16[64,8,128]{2,1,0:T(8,128)(2,1)} custom-call(bf16[64,8,128]{2,1,0:T(8,128)(2,1)} %bitcast.86), custom_call_target="tpu_custom_call" | custom-call | tf_op jit(solution)/shard_map/pallas_call | solution.py:82
  30.6 1.0 concatenate.58
  34.8 1.3 fusion.17.x_ref
  36.1 12.7 %shard_map.146 = bf16[8,64,360]{2,1,0:T(8,128)(2,1)} custom-call(bf16[8,64,360]{2,1,0:T(8,128)(2,1)} %fusion.17.x_ref), custom_call_target="tpu_custom_call" | custom-call | tf_op jit(solution)/shard_map/pallas_call | solution.py:82
  48.8 1.1 convert_reduce_fusion.1
  51.8 2.8 %concatenate.65 = bf16[8,360,180]{1,0,2:T(8,128)(2,1)S(1)} reshape(bf16[1,2880,180]{1,2,0:T(8,128)(2,1)} %param.28) | data formatting | bytes 2073600 | tf_op jit(solution)/shard_map/concatenate | solution.py:308
  54.5 1.1 copy.98
  55.7 2.8 %concatenate.64 = bf16[8,360,180]{1,0,2:T(8,128)(2,1)S(1)} reshape(bf16[1,2880,180]{1,2,0:T(8,128)(2,1)} %param.27) | data formatting | bytes 2073600 | tf_op jit(solution)/shard_map/concatenate | solution.py:308
  58.5 1.2 copy.97
  60.2 2.0 gather_fusion
  62.7 1.0 select_multiply_fusion.x_ref
  63.7 25.4 %shard_map.147 = bf16[32,30,128]{2,1,0:T(8,128)(2,1)} custom-call(bf16[32,30,128]{2,1,0:T(8,128)(2,1)} %select_multiply_fusion.x_ref), custom_call_target="tpu_custom_call" | custom-call | tf_op jit(solution)/shard_map/pallas_call | solution.py:82
  89.1 1.8 reshape_reshape_reshape.3.x_ref
  90.9 40.1 %shard_map.148 = bf16[8,2,320,384]{3,2,1,0:T(8,128)(2,1)} custom-call(bf16[320,384]{1,0:T(8,128)(2,1)} %reshape_reshape_reshape.3.x_ref), custom_call_target="tpu_custom_call" | custom-call | tf_op jit(solution)/shard_map/pallas_call | solution.py:156
  131.0 1.9 convert_reduce_fusion
  132.9 4.4 %fusion.11 = f32[640,360]{0,1:T(8,128)S(1)} fusion(bf16[8,360,180]{1,2,0:T(8,128)(2,1)S(1)} %copy-done.2, bf16[8,360,180]{1,2,0:T(8,128)(2,1)} %copy.97, bf16[8,640,384]{2,1,0:T(8,128)(2,1)} %bitcast.78, f32[640]{0:T(1024)S(1)} %add_rsqrt_fusion), kind=kOutput, calls=%fused_computation.13 | convolution fusion | flops 1331481600 | bytes 6929920 | tf_op jit(solution)/shard_map/tsf,tfh->sh/dot_general | solution.py:318
  138.2 37.0 %shard_map.149 = bf16[8,180,640]{2,1,0:T(8,128)(2,1)} custom-call(bf16[180,640]{1,0:T(8,128)(2,1)} %fusion.26.x_ref), custom_call_target="tpu_custom_call" | custom-call | tf_op jit(solution)/shard_map/pallas_call | solution.py:82
  175.2 2.3 %reshape_squeeze.3 = bf16[8,180,360]{2,1,0:T(8,128)(2,1)} reshape(bf16[1,1440,360]{2,1,0:T(8,128)(2,1)} %param.29) | data formatting | bytes 2073600 | tf_op jit(solution)/shard_map/reshape;squeeze | solution.py:324
  177.5 3.1 %fusion.16 = bf16[640,360]{0,1:T(8,128)(2,1)} fusion(bf16[8,180,640]{2,1,0:T(8,128)(2,1)S(1)} %copy-done.1, bf16[8,180,360]{2,1,0:T(8,128)(2,1)} %reshape_squeeze.3), kind=kOutput, calls=%fused_computation.14 | convolution fusion | flops 663782400 | bytes 3340800 | tf_op jit(solution)/shard_map/ths,thd->sd/dot_general | solution.py:325
  180.6 1.3 copy.99
  182.9 1.9 collective-permute-start
  185.1 2.1 gather_fusion.2
  189.2 24.7 %shard_map.150 = bf16[32,29,128]{2,1,0:T(8,128)(2,1)} custom-call(bf16[32,29,128]{2,1,0:T(8,128)(2,1)} %reshape.412.x_ref), custom_call_target="tpu_custom_call" | custom-call | tf_op jit(solution)/shard_map/pallas_call | solution.py:82
  213.9 1.0 copy.104
  (108 shorter events, 15.1 us)
Async XLA Ops:
  0.0 34.7 %copy-start = (bf16[256,2880]{0,1:T(8,128)(2,1)S(1)}, bf16[256,2880]{0,1:T(8,128)(2,1)}, u32[]{:S(2)}) copy-start(bf16[256,2880]{0,1:T(8,128)(2,1)} %param.22) | copy-start | bytes 4423684
  0.0 31.6 %copy-start.4 = (bf16[256,128]{1,0:T(8,128)(2,1)S(1)}, bf16[256,128]{1,0:T(8,128)(2,1)}, u32[]{:S(2)}) copy-start(bf16[256,128]{1,0:T(8,128)(2,1)} %param.17) | copy-start | bytes 196612
  2.5 30.4 %copy-start.5 = (bf16[64,256]{1,0:T(8,128)(2,1)S(1)}, bf16[64,256]{1,0:T(8,128)(2,1)}, u32[]{:S(2)}) copy-start(bf16[64,256]{1,0:T(8,128)(2,1)} %param.15) | copy-start | bytes 98308
  3.4 29.7 %copy-start.8 = (f32[4]{0:T(128)S(1)}, f32[4]{0:T(128)}, u32[]{:S(2)}) copy-start(f32[4]{0:T(128)} %param.21) | copy-start | bytes 52
  34.8 15.9 %copy-start.3 = (bf16[64,360]{1,0:T(8,128)(2,1)S(1)}, bf16[64,360]{1,0:T(8,128)(2,1)}, u32[]{:S(2)}) copy-start(bf16[64,360]{1,0:T(8,128)(2,1)} %param.23) | copy-start | bytes 138244
  34.8 16.1 %copy-start.6 = (s32[64,4]{0,1:T(4,128)S(1)}, s32[64,4]{0,1:T(4,128)}, u32[]{:S(2)}) copy-start(s32[64,4]{0,1:T(4,128)} %param.25) | copy-start | bytes 3076
  90.9 42.0 %copy-start.2 = (bf16[8,360,180]{1,2,0:T(8,128)(2,1)S(1)}, bf16[8,360,180]{1,2,0:T(8,128)(2,1)}, u32[]{:S(2)}) copy-start(bf16[8,360,180]{1,2,0:T(8,128)(2,1)} %copy.98) | copy-start | bytes 3110404
  175.2 2.3 %copy-start.1 = (bf16[8,180,640]{2,1,0:T(8,128)(2,1)S(1)}, bf16[8,180,640]{2,1,0:T(8,128)(2,1)}, u32[]{:S(2)}) copy-start(bf16[8,180,640]{2,1,0:T(8,128)(2,1)} %shard_map.149) | copy-start | bytes 5529604
  182.9 5.0 %collective-permute-start = (bf16[32,10,360]{2,1,0:T(8,128)(2,1)}, bf16[32,10,360]{2,1,0:T(8,128)(2,1)S(1)}, u32[]{:S(2)}, u32[]{:S(2)}) collective-permute-start(bf16[32,10,360]{2,1,0:T(8,128)(2,1)} %dynamic-slice_bitcast_fusion), channel_id=1, source_target_pairs={{0,8},{8,0},{16,24},{24,16},{32,40},{40,32},{48,56},{56,48},{64,72... | collective-permute-start | bytes 691208 | tf_op jit(solution)/shard_map/ppermute | solution.py:334
  185.0 2.6 %copy-start.7 = (f32[64,4]{0,1:T(4,128)S(1)}, f32[64,4]{0,1:T(4,128)}, u32[]{:S(2)}) copy-start(f32[64,4]{0,1:T(4,128)} %param.26) | copy-start | bytes 3076

commit v8 on v7

--- a/solution.py
+++ b/solution.py
@@ -299,10 +299,9 @@
     slot_hit = member[:, :, None] * (
         slot_rank[:, :, None] == jnp.arange(capacity, dtype=jnp.int32)[None, None, :]
     ).astype(jnp.int32)
-    slot_token = jnp.sum(slot_hit * jnp.arange(block_len, dtype=jnp.int32)[:, None, None], axis=0)
-    slot_valid = jnp.sum(slot_hit, axis=0)
-    send_own = jnp.take(normed_own, slot_token.reshape(-1), axis=0) * slot_valid.reshape(
-        -1, 1
+    slot_matrix = slot_hit.transpose(1, 2, 0).reshape(experts * capacity, block_len)
+    send_own = jnp.dot(
+        slot_matrix.astype(jnp.bfloat16), normed_own, preferred_element_type=jnp.float32
     ).astype(jnp.bfloat16)
     hidden_part = expert_gate.shape[2]
     gate_and_up = jnp.concatenate([expert_gate[0], expert_up[0]], axis=1)
@@ -335,12 +334,13 @@
     joined_halves = (mine.astype(jnp.float32) + other_half.astype(jnp.float32)).astype(jnp.bfloat16)
     arrived = pair_exchange(lane_dense(joined_halves.reshape(experts, capacity * width)), 3)
     summed = arrived.reshape(experts, -1)[:, : capacity * width].astype(jnp.float32).reshape(experts * capacity, width)
-    rank_at = jnp.take_along_axis(slot_rank, routes, axis=1)
-    picked = jnp.take(summed, (routes * capacity + rank_at).reshape(-1), axis=0).reshape(
-        block_len, top_count, width
-    )
     mixing = route_weights / jnp.sum(route_weights, axis=1, keepdims=True)
-    moe_out = jnp.sum(mixing[:, :, None] * picked, axis=1)
+    expert_weight = jnp.sum(
+        jnp.where(routes[:, :, None] == jnp.arange(experts, dtype=jnp.int32)[None, None, :], mixing[:, :, None], 0.0),
+        axis=1,
+    )
+    combine = (slot_hit.astype(jnp.float32) * expert_weight[:, :, None]).reshape(block_len, experts * capacity)
+    moe_out = jnp.dot(combine, summed, precision=lax.Precision.HIGHEST, preferred_element_type=jnp.float32)
     return (own_state + moe_out).astype(jnp.bfloat16)
 
 

time: 220 us -> 214 us (0.973)
  local copies, waits for them, and re-layouts: 28.8 us -> 23.4 us
  other arithmetic: 9.1 us -> 6.52 us
    gather x9 -> x0, local copies, waits for them, and re-layouts: 5.8 us -> none  [the longest x5 2.5 us: on_device(): rank_at = jnp.take_along_axis(slot_rank, routes, axis=1)]
  transfers between devices with their start and end apart: 1 -> 1, of which waited for: 0 -> 1; matrix products, arithmetic and copies ran while one was open for 1% -> 0% of each run, Pallas kernels for 0% -> 0%
where the time goes in v8:
time: 214 us; the launch traced here: 212 us
  Pallas kernels  167 us (78%)
  local copies, waits for them, and re-layouts  23.4 us (11%)
  matrix products  10.7 us (5%)
  other arithmetic  6.52 us (3%)
    pallas_call x5, Pallas kernels, _transfer(): pl.pallas_call(functools.partial(_transfer_kernel, axis, gather), out_sha...  127 us
    pallas_call x1, Pallas kernels, pair_gather(): pl.pallas_call(_pair_gather_kernel, out_shape=jax.ShapeDtypeStruct(shape,...  40.1 us
    concatenate x4, local copies, waits for them, and re-layouts, on_device(): gate_and_up = jnp.concatenate([expert_gate[0], expert_up[0]], axis=1)  7.86 us
    dot_general x1, matrix products, on_device(): jnp.einsum('tsf,tfh->sh', whole[:, :, :width], gate_blocks, preferred_ele...  4.35 us
  transfers between devices with their start and end apart: 1, of which 1 were waited for; matrix products, arithmetic and copies ran while one was open for 0% of the time, Pallas kernels for 0%

profile of v8, /device:TPU:24, one launch (start us, length us, event | category | flops | bytes accessed | tf_op | source)
XLA Modules:
  0.0 212.3 jit_solution(1782887338611462395)
XLA Ops:
  3.7 26.8 %shard_map.145 = bf16[64,8,128]{2,1,0:T(8,128)(2,1)} custom-call(bf16[64,8,128]{2,1,0:T(8,128)(2,1)} %bitcast.88), custom_call_target="tpu_custom_call" | custom-call | tf_op jit(solution)/shard_map/pallas_call | solution.py:82
  30.6 1.0 concatenate.58
  34.8 1.3 fusion.17.x_ref
  36.1 12.7 %shard_map.146 = bf16[8,64,360]{2,1,0:T(8,128)(2,1)} custom-call(bf16[8,64,360]{2,1,0:T(8,128)(2,1)} %fusion.17.x_ref), custom_call_target="tpu_custom_call" | custom-call | tf_op jit(solution)/shard_map/pallas_call | solution.py:82
  48.9 1.1 convert_reduce_fusion.1
  51.1 2.8 %concatenate.65 = bf16[8,360,180]{1,0,2:T(8,128)(2,1)S(1)} reshape(bf16[1,2880,180]{1,2,0:T(8,128)(2,1)} %param.28) | data formatting | bytes 2073600 | tf_op jit(solution)/shard_map/concatenate | solution.py:307
  53.9 1.1 copy.79
  55.0 2.8 %concatenate.64 = bf16[8,360,180]{1,0,2:T(8,128)(2,1)S(1)} reshape(bf16[1,2880,180]{1,2,0:T(8,128)(2,1)} %param.27) | data formatting | bytes 2073600 | tf_op jit(solution)/shard_map/concatenate | solution.py:307
  57.8 1.2 copy.78
  60.8 25.4 %shard_map.147 = bf16[32,30,128]{2,1,0:T(8,128)(2,1)} custom-call(bf16[32,30,128]{2,1,0:T(8,128)(2,1)} %reshape.356.x_ref), custom_call_target="tpu_custom_call" | custom-call | tf_op jit(solution)/shard_map/pallas_call | solution.py:82
  86.2 1.8 reshape_reshape_reshape.3.x_ref
  88.0 40.1 %shard_map.148 = bf16[8,2,320,384]{3,2,1,0:T(8,128)(2,1)} custom-call(bf16[320,384]{1,0:T(8,128)(2,1)} %reshape_reshape_reshape.3.x_ref), custom_call_target="tpu_custom_call" | custom-call | tf_op jit(solution)/shard_map/pallas_call | solution.py:156
  128.1 1.9 convert_reduce_fusion
  130.0 4.4 %fusion.11 = f32[640,360]{0,1:T(8,128)S(1)} fusion(bf16[8,360,180]{1,2,0:T(8,128)(2,1)S(1)} %copy-done.2, bf16[8,360,180]{1,2,0:T(8,128)(2,1)} %copy.78, bf16[8,640,384]{2,1,0:T(8,128)(2,1)} %bitcast.80, f32[640]{0:T(1024)S(1)} %add_rsqrt_fusion), kind=kOutput, calls=%fused_computation.10 | convolution fusion | flops 1331481600 | bytes 6929920 | tf_op jit(solution)/shard_map/tsf,tfh->sh/dot_general | solution.py:317
  134.3 0.9 fusion.27.x_ref
  135.2 37.0 %shard_map.149 = bf16[8,180,640]{2,1,0:T(8,128)(2,1)} custom-call(bf16[180,640]{1,0:T(8,128)(2,1)} %fusion.27.x_ref), custom_call_target="tpu_custom_call" | custom-call | tf_op jit(solution)/shard_map/pallas_call | solution.py:82
  172.2 2.3 %reshape_squeeze.3 = bf16[8,180,360]{2,1,0:T(8,128)(2,1)} reshape(bf16[1,1440,360]{2,1,0:T(8,128)(2,1)} %param.29) | data formatting | bytes 2073600 | tf_op jit(solution)/shard_map/reshape;squeeze | solution.py:323
  174.5 3.1 %fusion.16 = bf16[640,360]{0,1:T(8,128)(2,1)} fusion(bf16[8,180,640]{2,1,0:T(8,128)(2,1)S(1)} %copy-done.1, bf16[8,180,360]{2,1,0:T(8,128)(2,1)} %reshape_squeeze.3), kind=kOutput, calls=%fused_computation.11 | convolution fusion | flops 663782400 | bytes 3340800 | tf_op jit(solution)/shard_map/ths,thd->sd/dot_general | solution.py:324
  177.6 1.3 copy.80
  179.9 1.9 collective-permute-start
  182.2 1.6 collective-permute-done
  185.0 24.8 %shard_map.150 = bf16[32,29,128]{2,1,0:T(8,128)(2,1)} custom-call(bf16[32,29,128]{2,1,0:T(8,128)(2,1)} %reshape.360.x_ref), custom_call_target="tpu_custom_call" | custom-call | tf_op jit(solution)/shard_map/pallas_call | solution.py:82
  209.8 1.0 copy.84
  211.3 1.0 fusion.18
  (90 shorter events, 11.8 us)
Async XLA Ops:
  0.0 34.7 %copy-start = (bf16[256,2880]{0,1:T(8,128)(2,1)S(1)}, bf16[256,2880]{0,1:T(8,128)(2,1)}, u32[]{:S(2)}) copy-start(bf16[256,2880]{0,1:T(8,128)(2,1)} %param.22) | copy-start | bytes 4423684
  0.0 31.6 %copy-start.5 = (bf16[256,128]{1,0:T(8,128)(2,1)S(1)}, bf16[256,128]{1,0:T(8,128)(2,1)}, u32[]{:S(2)}) copy-start(bf16[256,128]{1,0:T(8,128)(2,1)} %param.17) | copy-start | bytes 196612
  2.5 30.4 %copy-start.6 = (bf16[64,256]{1,0:T(8,128)(2,1)S(1)}, bf16[64,256]{1,0:T(8,128)(2,1)}, u32[]{:S(2)}) copy-start(bf16[64,256]{1,0:T(8,128)(2,1)} %param.15) | copy-start | bytes 98308
  3.4 29.7 %copy-start.9 = (f32[4]{0:T(128)S(1)}, f32[4]{0:T(128)}, u32[]{:S(2)}) copy-start(f32[4]{0:T(128)} %param.21) | copy-start | bytes 52
  34.8 16.0 %copy-start.3 = (bf16[64,360]{1,0:T(8,128)(2,1)S(1)}, bf16[64,360]{1,0:T(8,128)(2,1)}, u32[]{:S(2)}) copy-start(bf16[64,360]{1,0:T(8,128)(2,1)} %param.23) | copy-start | bytes 138244
  34.8 16.1 %copy-start.7 = (s32[64,4]{0,1:T(4,128)S(1)}, s32[64,4]{0,1:T(4,128)}, u32[]{:S(2)}) copy-start(s32[64,4]{0,1:T(4,128)} %param.25) | copy-start | bytes 3076
  88.0 42.0 %copy-start.2 = (bf16[8,360,180]{1,2,0:T(8,128)(2,1)S(1)}, bf16[8,360,180]{1,2,0:T(8,128)(2,1)}, u32[]{:S(2)}) copy-start(bf16[8,360,180]{1,2,0:T(8,128)(2,1)} %copy.79) | copy-start | bytes 3110404
  172.2 2.3 %copy-start.1 = (bf16[8,180,640]{2,1,0:T(8,128)(2,1)S(1)}, bf16[8,180,640]{2,1,0:T(8,128)(2,1)}, u32[]{:S(2)}) copy-start(bf16[8,180,640]{2,1,0:T(8,128)(2,1)} %shard_map.149) | copy-start | bytes 5529604
  177.6 4.3 %copy-start.8 = (f32[64,4]{0,1:T(4,128)S(1)}, f32[64,4]{0,1:T(4,128)}, u32[]{:S(2)}) copy-start(f32[64,4]{0,1:T(4,128)} %param.26) | copy-start | bytes 3076
  179.9 3.8 %collective-permute-start = (bf16[32,10,360]{2,1,0:T(8,128)(2,1)}, bf16[32,10,360]{2,1,0:T(8,128)(2,1)S(1)}, u32[]{:S(2)}, u32[]{:S(2)}) collective-permute-start(bf16[32,10,360]{2,1,0:T(8,128)(2,1)} %dynamic-slice_bitcast_fusion), channel_id=1, source_target_pairs={{0,8},{8,0},{16,24},{24,16},{32,40},{40,32},{48,56},{56,48},{64,72... | collective-permute-start | bytes 691208 | tf_op jit(solution)/shard_map/ppermute | solution.py:333
  183.8 27.5 %copy-start.4 = (bf16[64,360]{1,0:T(8,128)(2,1)S(1)}, bf16[64,360]{1,0:T(8,128)(2,1)}, u32[]{:S(2)}) copy-start(bf16[64,360]{1,0:T(8,128)(2,1)} %param.23) | copy-start | bytes 138244

commit v9 on v8

--- a/solution.py
+++ b/solution.py
@@ -304,17 +304,24 @@
         slot_matrix.astype(jnp.bfloat16), normed_own, preferred_element_type=jnp.float32
     ).astype(jnp.bfloat16)
     hidden_part = expert_gate.shape[2]
-    gate_and_up = jnp.concatenate([expert_gate[0], expert_up[0]], axis=1)
     row_width = send_own.shape[1]
     received = pair_exchange(lane_dense(send_own.reshape(experts, capacity * row_width)), 2)
     received = received.reshape(experts, -1)[:, : capacity * row_width].reshape(experts, capacity, row_width)
     sources, slot_count, part_features = received.shape
     whole = pair_gather(received.reshape(sources * slot_count, part_features), 4)
     whole = whole.reshape(tp_count, 2 * sources * slot_count, part_features)
-    gate_blocks = gate_and_up.reshape(tp_count, width, gate_and_up.shape[1])
     total_square = jnp.sum(whole[:, :, width:width + 2].astype(jnp.float32), axis=(0, 2))
     row_scale = lax.rsqrt(total_square / (width * tp_count) + EPSILON)
-    both = jnp.einsum("tsf,tfh->sh", whole[:, :, :width], gate_blocks, preferred_element_type=jnp.float32)
+    tokens = whole[:, :, :width]
+    gate_view = expert_gate[0].reshape(tp_count, width, hidden_part)
+    up_view = expert_up[0].reshape(tp_count, width, hidden_part)
+    both = jnp.concatenate(
+        [
+            jnp.einsum("tsf,tfh->sh", tokens, gate_view, preferred_element_type=jnp.float32),
+            jnp.einsum("tsf,tfh->sh", tokens, up_view, preferred_element_type=jnp.float32),
+        ],
+        axis=1,
+    )
     both = both * row_scale[:, None]
     gate_val = both[:, :hidden_part]
     up_val = both[:, hidden_part:]

time: 214 us -> 216 us (level)
  matrix products: 10.7 us -> 13.4 us
    concatenate x4 -> x0, local copies, waits for them, and re-layouts: 7.86 us -> none  [on_device(): gate_and_up = jnp.concatenate([expert_gate[0], expert_up[0]], axis=1)]
    another operation x0 -> x2, local copies, waits for them, and re-layouts: none -> 5.56 us  [the longest x1 2.78 us: on_device(): up_view = expert_up[0].reshape(tp_count, width, hidden_part)]
    dot_general x1 -> x2, matrix products: 4.35 us -> 7.08 us  [the longest x1 3.54 us: on_device(): jnp.einsum('tsf,tfh->sh', tokens, up_view, preferred_element_type=jnp.flo...]
where the time goes in v9:
time: 216 us; the launch traced here: 214 us
  Pallas kernels  167 us (77%)
  local copies, waits for them, and re-layouts  22.8 us (11%)
  matrix products  13.4 us (6%)
  other arithmetic  5.94 us (3%)
    pallas_call x5, Pallas kernels, _transfer(): pl.pallas_call(functools.partial(_transfer_kernel, axis, gather), out_sha...  127 us
    pallas_call x1, Pallas kernels, pair_gather(): pl.pallas_call(_pair_gather_kernel, out_shape=jax.ShapeDtypeStruct(shape,...  39.9 us
  transfers between devices with their start and end apart: 1, of which 1 were waited for; matrix products, arithmetic and copies ran while one was open for 0% of the time, Pallas kernels for 0%

profile of v9, /device:TPU:24, one launch (start us, length us, event | category | flops | bytes accessed | tf_op | source)
XLA Modules:
  0.0 213.5 jit_solution(16779528469936881375)
XLA Ops:
  0.8 0.9 reshape.359
  2.9 26.8 %shard_map.145 = bf16[64,8,128]{2,1,0:T(8,128)(2,1)} custom-call(bf16[64,8,128]{2,1,0:T(8,128)(2,1)} %bitcast.89), custom_call_target="tpu_custom_call" | custom-call | tf_op jit(solution)/shard_map/pallas_call | solution.py:82
  29.7 1.0 concatenate.53
  30.8 0.9 copy.65
  35.7 1.3 fusion.12.x_ref
  37.0 12.7 %shard_map.146 = bf16[8,64,360]{2,1,0:T(8,128)(2,1)} custom-call(bf16[8,64,360]{2,1,0:T(8,128)(2,1)} %fusion.12.x_ref), custom_call_target="tpu_custom_call" | custom-call | tf_op jit(solution)/shard_map/pallas_call | solution.py:82
  49.8 1.1 convert_reduce_fusion.1
  53.8 25.4 %shard_map.147 = bf16[32,30,128]{2,1,0:T(8,128)(2,1)} custom-call(bf16[32,30,128]{2,1,0:T(8,128)(2,1)} %reshape.351.x_ref), custom_call_target="tpu_custom_call" | custom-call | tf_op jit(solution)/shard_map/pallas_call | solution.py:82
  79.2 1.8 reshape_reshape_reshape.3.x_ref
  81.0 39.9 %shard_map.148 = bf16[8,2,320,384]{3,2,1,0:T(8,128)(2,1)} custom-call(bf16[320,384]{1,0:T(8,128)(2,1)} %reshape_reshape_reshape.3.x_ref), custom_call_target="tpu_custom_call" | custom-call | tf_op jit(solution)/shard_map/pallas_call | solution.py:156
  121.0 2.8 %reshape_squeeze.10 = bf16[8,360,180]{1,0,2:T(8,128)(2,1)S(1)} reshape(bf16[1,2880,180]{1,2,0:T(8,128)(2,1)} %param.28) | data formatting | bytes 2073600 | tf_op jit(solution)/shard_map/reshape;squeeze | solution.py:317
  123.8 1.9 convert_reduce_fusion
  125.7 3.5 %fusion.6 = f32[640,180]{0,1:T(8,128)S(1)} fusion(bf16[8,640,384]{2,1,0:T(8,128)(2,1)} %bitcast.80, bf16[8,360,180]{1,0,2:T(8,128)(2,1)S(1)} %reshape_squeeze.10), kind=kOutput, calls=%fused_computation.10 | convolution fusion | flops 663552000 | bytes 5429760 | tf_op jit(solution)/shard_map/tsf,tfh->sh/dot_general | solution.py:321
  129.2 2.8 %reshape_squeeze.9 = bf16[8,360,180]{1,0,2:T(8,128)(2,1)S(1)} reshape(bf16[1,2880,180]{1,2,0:T(8,128)(2,1)} %param.27) | data formatting | bytes 2073600 | tf_op jit(solution)/shard_map/reshape;squeeze | solution.py:316
  132.0 3.5 %fusion.9 = f32[640,180]{0,1:T(8,128)S(1)} fusion(bf16[8,640,384]{2,1,0:T(8,128)(2,1)} %bitcast.81, bf16[8,360,180]{1,0,2:T(8,128)(2,1)S(1)} %reshape_squeeze.9), kind=kOutput, calls=%fused_computation.11 | convolution fusion | flops 663552000 | bytes 5429760 | tf_op jit(solution)/shard_map/tsf,tfh->sh/dot_general | solution.py:320
  136.5 37.0 %shard_map.149 = bf16[8,180,640]{2,1,0:T(8,128)(2,1)} custom-call(bf16[180,640]{1,0:T(8,128)(2,1)} %fusion.24.x_ref), custom_call_target="tpu_custom_call" | custom-call | tf_op jit(solution)/shard_map/pallas_call | solution.py:82
  173.5 2.3 %reshape_squeeze.11 = bf16[8,180,360]{2,1,0:T(8,128)(2,1)} reshape(bf16[1,1440,360]{2,1,0:T(8,128)(2,1)} %param.29) | data formatting | bytes 2073600 | tf_op jit(solution)/shard_map/reshape;squeeze | solution.py:330
  175.9 3.1 %fusion.5 = bf16[640,360]{0,1:T(8,128)(2,1)} fusion(bf16[8,180,640]{2,1,0:T(8,128)(2,1)S(1)} %copy-done.1, bf16[8,180,360]{2,1,0:T(8,128)(2,1)} %reshape_squeeze.11), kind=kOutput, calls=%fused_computation.8 | convolution fusion | flops 663782400 | bytes 3340800 | tf_op jit(solution)/shard_map/ths,thd->sd/dot_general | solution.py:331
  179.0 1.3 copy.82
  181.3 1.9 collective-permute-start
  183.5 1.6 collective-permute-done
  186.3 24.7 %shard_map.150 = bf16[32,29,128]{2,1,0:T(8,128)(2,1)} custom-call(bf16[32,29,128]{2,1,0:T(8,128)(2,1)} %reshape.355.x_ref), custom_call_target="tpu_custom_call" | custom-call | tf_op jit(solution)/shard_map/pallas_call | solution.py:82
  211.1 1.0 copy.90
  212.6 1.0 fusion.15
  (86 shorter events, 11.8 us)
Async XLA Ops:
  0.0 35.7 %copy-start = (bf16[256,2880]{0,1:T(8,128)(2,1)S(1)}, bf16[256,2880]{0,1:T(8,128)(2,1)}, u32[]{:S(2)}) copy-start(bf16[256,2880]{0,1:T(8,128)(2,1)} %param.22) | copy-start | bytes 4423684
  1.7 31.2 %copy-start.7 = (s32[1,64]{1,0:T(1,128)S(1)}, s32[1,64]{1,0:T(1,128)}, u32[]{:S(2)}) copy-start(s32[1,64]{1,0:T(1,128)} %param.19) | copy-start | bytes 772
  31.8 2.1 copy-start.6
  35.7 15.9 %copy-start.2 = (bf16[64,360]{1,0:T(8,128)(2,1)S(1)}, bf16[64,360]{1,0:T(8,128)(2,1)}, u32[]{:S(2)}) copy-start(bf16[64,360]{1,0:T(8,128)(2,1)} %param.23) | copy-start | bytes 138244
  35.7 16.3 %copy-start.4 = (s32[64,4]{0,1:T(4,128)S(1)}, s32[64,4]{0,1:T(4,128)}, u32[]{:S(2)}) copy-start(s32[64,4]{0,1:T(4,128)} %param.25) | copy-start | bytes 3076
  173.5 2.3 %copy-start.1 = (bf16[8,180,640]{2,1,0:T(8,128)(2,1)S(1)}, bf16[8,180,640]{2,1,0:T(8,128)(2,1)}, u32[]{:S(2)}) copy-start(bf16[8,180,640]{2,1,0:T(8,128)(2,1)} %shard_map.149) | copy-start | bytes 5529604
  179.0 4.4 %copy-start.5 = (f32[64,4]{0,1:T(4,128)S(1)}, f32[64,4]{0,1:T(4,128)}, u32[]{:S(2)}) copy-start(f32[64,4]{0,1:T(4,128)} %param.26) | copy-start | bytes 3076
  181.3 3.8 %collective-permute-start = (bf16[32,10,360]{2,1,0:T(8,128)(2,1)}, bf16[32,10,360]{2,1,0:T(8,128)(2,1)S(1)}, u32[]{:S(2)}, u32[]{:S(2)}) collective-permute-start(bf16[32,10,360]{2,1,0:T(8,128)(2,1)} %dynamic-slice_bitcast_fusion), channel_id=1, source_target_pairs={{0,8},{8,0},{16,24},{24,16},{32,40},{40,32},{48,56},{56,48},{64,72... | collective-permute-start | bytes 691208 | tf_op jit(solution)/shard_map/ppermute | solution.py:340
  185.2 27.4 %copy-start.3 = (bf16[64,360]{1,0:T(8,128)(2,1)S(1)}, bf16[64,360]{1,0:T(8,128)(2,1)}, u32[]{:S(2)}) copy-start(bf16[64,360]{1,0:T(8,128)(2,1)} %param.23) | copy-start | bytes 138244

commit v10 on v9

--- a/solution.py
+++ b/solution.py
@@ -13,6 +13,13 @@
 THETA = 150000.0
 ALPHA = 1.702
 EPSILON = 1e-05
+
+
+def _row_parts(rows, parts=4):
+    if not rows:
+        return [(0, 0)]
+    step = -(-rows // (parts * 16)) * 16
+    return [(first, min(step, rows - first)) for first in range(0, rows, step)]
 
 
 def _transfer_kernel(axis, gather, x_ref, o_ref, buf, send_sem, recv_sem, local_sem):
@@ -49,19 +56,26 @@
     local = pltpu.make_async_copy(piece(me), buf.at[me], local_sem)
     local.start()
 
-    def send(step, carry):
-        peer = lax.rem(me + step, count)
-        pltpu.make_async_remote_copy(
-            src_ref=piece(peer),
-            dst_ref=buf.at[me],
-            send_sem=send_sem,
-            recv_sem=recv_sem,
-            device_id=device(peer),
-            device_id_type=pl.DeviceIdType.MESH,
-        ).start()
-        return carry
-
-    lax.fori_loop(1, count, send, 0)
+    for first, size in _row_parts(buf.shape[1] if gather else 0):
+
+        def send(step, carry, first=first, size=size):
+            peer = lax.rem(me + step, count)
+            src = piece(peer)
+            dst = buf.at[me]
+            if size:
+                src = src.at[pl.ds(first, size)]
+                dst = dst.at[pl.ds(first, size)]
+            pltpu.make_async_remote_copy(
+                src_ref=src,
+                dst_ref=dst,
+                send_sem=send_sem,
+                recv_sem=recv_sem,
+                device_id=device(peer),
+                device_id_type=pl.DeviceIdType.MESH,
+            ).start()
+            return carry
+
+        lax.fori_loop(1, count, send, 0)
     local.wait()
     every = pltpu.make_async_remote_copy(
         src_ref=buf.at[pl.ds(0, count - 1)],
@@ -113,19 +127,21 @@
     local = pltpu.make_async_copy(x_ref, buf.at[tp_at, core], local_sem)
     local.start()
 
-    def send(step, carry):
-        peer = lax.rem(tp_at + step, count)
-        pltpu.make_async_remote_copy(
-            src_ref=x_ref,
-            dst_ref=buf.at[tp_at, core],
-            send_sem=send_sem,
-            recv_sem=recv_sem,
-            device_id=(group_at, peer),
-            device_id_type=pl.DeviceIdType.MESH,
-        ).start()
-        return carry
-
-    lax.fori_loop(1, count, send, 0)
+    for first, size in _row_parts(x_ref.shape[0]):
+
+        def send(step, carry, first=first, size=size):
+            peer = lax.rem(tp_at + step, count)
+            pltpu.make_async_remote_copy(
+                src_ref=x_ref.at[pl.ds(first, size)],
+                dst_ref=buf.at[tp_at, core, pl.ds(first, size)],
+                send_sem=send_sem,
+                recv_sem=recv_sem,
+                device_id=(group_at, peer),
+                device_id_type=pl.DeviceIdType.MESH,
+            ).start()
+            return carry
+
+        lax.fori_loop(1, count, send, 0)
     local.wait()
     every = pltpu.make_async_remote_copy(
         src_ref=buf.at[pl.ds(0, count - 1), 0],

time: 216 us -> 201 us (0.931)
  Pallas kernels: 167 us -> 154 us
    pallas_call x5, Pallas kernels: 127 us -> 119 us  [_transfer(): pl.pallas_call(functools.partial(_transfer_kernel, axis, gather), out_sha...]
    pallas_call x1, Pallas kernels: 39.9 us -> 34.8 us  [pair_gather(): pl.pallas_call(_pair_gather_kernel, out_shape=jax.ShapeDtypeStruct(shape,...]
where the time goes in v10:
time: 201 us; the launch traced here: 200 us
  Pallas kernels  154 us (77%)
  local copies, waits for them, and re-layouts  22.8 us (11%)
  matrix products  13.4 us (7%)
  other arithmetic  5.94 us (3%)
    pallas_call x5, Pallas kernels, _transfer(): pl.pallas_call(functools.partial(_transfer_kernel, axis, gather), out_sha...  119 us
    pallas_call x1, Pallas kernels, pair_gather(): pl.pallas_call(_pair_gather_kernel, out_shape=jax.ShapeDtypeStruct(shape,...  34.8 us
  transfers between devices with their start and end apart: 1, of which 1 were waited for; matrix products, arithmetic and copies ran while one was open for 0% of the time, Pallas kernels for 0%

profile of v10, /device:TPU:24, one launch (start us, length us, event | category | flops | bytes accessed | tf_op | source)
XLA Modules:
  0.0 200.4 jit_solution(13274654597087504397)
XLA Ops:
  0.8 0.9 reshape.359
  2.9 26.8 %shard_map.145 = bf16[64,8,128]{2,1,0:T(8,128)(2,1)} custom-call(bf16[64,8,128]{2,1,0:T(8,128)(2,1)} %bitcast.89), custom_call_target="tpu_custom_call" | custom-call | tf_op jit(solution)/shard_map/pallas_call | solution.py:96
  29.7 1.0 concatenate.53
  30.8 0.9 copy.65
  35.7 1.3 fusion.12.x_ref
  37.0 12.7 %shard_map.146 = bf16[8,64,360]{2,1,0:T(8,128)(2,1)} custom-call(bf16[8,64,360]{2,1,0:T(8,128)(2,1)} %fusion.12.x_ref), custom_call_target="tpu_custom_call" | custom-call | tf_op jit(solution)/shard_map/pallas_call | solution.py:96
  49.8 1.1 convert_reduce_fusion.1
  53.8 25.4 %shard_map.147 = bf16[32,30,128]{2,1,0:T(8,128)(2,1)} custom-call(bf16[32,30,128]{2,1,0:T(8,128)(2,1)} %reshape.351.x_ref), custom_call_target="tpu_custom_call" | custom-call | tf_op jit(solution)/shard_map/pallas_call | solution.py:96
  79.2 1.8 reshape_reshape_reshape.3.x_ref
  81.0 34.8 %shard_map.148 = bf16[8,2,320,384]{3,2,1,0:T(8,128)(2,1)} custom-call(bf16[320,384]{1,0:T(8,128)(2,1)} %reshape_reshape_reshape.3.x_ref), custom_call_target="tpu_custom_call" | custom-call | tf_op jit(solution)/shard_map/pallas_call | solution.py:172
  115.8 2.8 %reshape_squeeze.10 = bf16[8,360,180]{1,0,2:T(8,128)(2,1)S(1)} reshape(bf16[1,2880,180]{1,2,0:T(8,128)(2,1)} %param.28) | data formatting | bytes 2073600 | tf_op jit(solution)/shard_map/reshape;squeeze | solution.py:333
  118.6 1.9 convert_reduce_fusion
  120.5 3.5 %fusion.6 = f32[640,180]{0,1:T(8,128)S(1)} fusion(bf16[8,640,384]{2,1,0:T(8,128)(2,1)} %bitcast.80, bf16[8,360,180]{1,0,2:T(8,128)(2,1)S(1)} %reshape_squeeze.10), kind=kOutput, calls=%fused_computation.10 | convolution fusion | flops 663552000 | bytes 5429760 | tf_op jit(solution)/shard_map/tsf,tfh->sh/dot_general | solution.py:337
  124.1 2.8 %reshape_squeeze.9 = bf16[8,360,180]{1,0,2:T(8,128)(2,1)S(1)} reshape(bf16[1,2880,180]{1,2,0:T(8,128)(2,1)} %param.27) | data formatting | bytes 2073600 | tf_op jit(solution)/shard_map/reshape;squeeze | solution.py:332
  126.8 3.5 %fusion.9 = f32[640,180]{0,1:T(8,128)S(1)} fusion(bf16[8,640,384]{2,1,0:T(8,128)(2,1)} %bitcast.81, bf16[8,360,180]{1,0,2:T(8,128)(2,1)S(1)} %reshape_squeeze.9), kind=kOutput, calls=%fused_computation.11 | convolution fusion | flops 663552000 | bytes 5429760 | tf_op jit(solution)/shard_map/tsf,tfh->sh/dot_general | solution.py:336
  131.3 29.1 %shard_map.149 = bf16[8,180,640]{2,1,0:T(8,128)(2,1)} custom-call(bf16[180,640]{1,0:T(8,128)(2,1)} %fusion.24.x_ref), custom_call_target="tpu_custom_call" | custom-call | tf_op jit(solution)/shard_map/pallas_call | solution.py:96
  160.5 2.3 %reshape_squeeze.11 = bf16[8,180,360]{2,1,0:T(8,128)(2,1)} reshape(bf16[1,1440,360]{2,1,0:T(8,128)(2,1)} %param.29) | data formatting | bytes 2073600 | tf_op jit(solution)/shard_map/reshape;squeeze | solution.py:346
  162.8 3.1 %fusion.5 = bf16[640,360]{0,1:T(8,128)(2,1)} fusion(bf16[8,180,640]{2,1,0:T(8,128)(2,1)S(1)} %copy-done.1, bf16[8,180,360]{2,1,0:T(8,128)(2,1)} %reshape_squeeze.11), kind=kOutput, calls=%fused_computation.8 | convolution fusion | flops 663782400 | bytes 3340800 | tf_op jit(solution)/shard_map/ths,thd->sd/dot_general | solution.py:347
  165.9 1.3 copy.82
  168.2 1.9 collective-permute-start
  170.4 1.6 collective-permute-done
  173.3 24.6 %shard_map.150 = bf16[32,29,128]{2,1,0:T(8,128)(2,1)} custom-call(bf16[32,29,128]{2,1,0:T(8,128)(2,1)} %reshape.355.x_ref), custom_call_target="tpu_custom_call" | custom-call | tf_op jit(solution)/shard_map/pallas_call | solution.py:96
  197.9 1.0 copy.90
  199.4 1.0 fusion.15
  (86 shorter events, 11.8 us)
Async XLA Ops:
  0.0 35.7 %copy-start = (bf16[256,2880]{0,1:T(8,128)(2,1)S(1)}, bf16[256,2880]{0,1:T(8,128)(2,1)}, u32[]{:S(2)}) copy-start(bf16[256,2880]{0,1:T(8,128)(2,1)} %param.22) | copy-start | bytes 4423684
  1.7 31.2 %copy-start.7 = (s32[1,64]{1,0:T(1,128)S(1)}, s32[1,64]{1,0:T(1,128)}, u32[]{:S(2)}) copy-start(s32[1,64]{1,0:T(1,128)} %param.19) | copy-start | bytes 772
  31.8 2.1 %copy-start.6 = (f32[4]{0:T(128)S(1)}, f32[4]{0:T(128)}, u32[]{:S(2)}) copy-start(f32[4]{0:T(128)} %param.21) | copy-start | bytes 52
  35.7 15.9 %copy-start.2 = (bf16[64,360]{1,0:T(8,128)(2,1)S(1)}, bf16[64,360]{1,0:T(8,128)(2,1)}, u32[]{:S(2)}) copy-start(bf16[64,360]{1,0:T(8,128)(2,1)} %param.23) | copy-start | bytes 138244
  35.7 16.3 %copy-start.4 = (s32[64,4]{0,1:T(4,128)S(1)}, s32[64,4]{0,1:T(4,128)}, u32[]{:S(2)}) copy-start(s32[64,4]{0,1:T(4,128)} %param.25) | copy-start | bytes 3076
  160.5 2.3 %copy-start.1 = (bf16[8,180,640]{2,1,0:T(8,128)(2,1)S(1)}, bf16[8,180,640]{2,1,0:T(8,128)(2,1)}, u32[]{:S(2)}) copy-start(bf16[8,180,640]{2,1,0:T(8,128)(2,1)} %shard_map.149) | copy-start | bytes 5529604
  165.9 4.4 %copy-start.5 = (f32[64,4]{0,1:T(4,128)S(1)}, f32[64,4]{0,1:T(4,128)}, u32[]{:S(2)}) copy-start(f32[64,4]{0,1:T(4,128)} %param.26) | copy-start | bytes 3076
  168.2 3.8 %collective-permute-start = (bf16[32,10,360]{2,1,0:T(8,128)(2,1)}, bf16[32,10,360]{2,1,0:T(8,128)(2,1)S(1)}, u32[]{:S(2)}, u32[]{:S(2)}) collective-permute-start(bf16[32,10,360]{2,1,0:T(8,128)(2,1)} %dynamic-slice_bitcast_fusion), channel_id=1, source_target_pairs={{0,8},{8,0},{16,24},{24,16},{32,40},{40,32},{48,56},{56,48},{64,72... | collective-permute-start | bytes 691208 | tf_op jit(solution)/shard_map/ppermute | solution.py:356
  172.1 27.3 %copy-start.3 = (bf16[64,360]{1,0:T(8,128)(2,1)S(1)}, bf16[64,360]{1,0:T(8,128)(2,1)}, u32[]{:S(2)}) copy-start(bf16[64,360]{1,0:T(8,128)(2,1)} %param.23) | copy-start | bytes 138244

commit v11 on v10

--- a/solution.py
+++ b/solution.py
@@ -15,7 +15,7 @@
 EPSILON = 1e-05
 
 
-def _row_parts(rows, parts=4):
+def _row_parts(rows, parts=8):
     if not rows:
         return [(0, 0)]
     step = -(-rows // (parts * 16)) * 16
@@ -56,7 +56,7 @@
     local = pltpu.make_async_copy(piece(me), buf.at[me], local_sem)
     local.start()
 
-    for first, size in _row_parts(buf.shape[1] if gather else 0):
+    for first, size in _row_parts(buf.shape[1] if (gather or axis == "tp") else 0):
 
         def send(step, carry, first=first, size=size):
             peer = lax.rem(me + step, count)

time: 201 us -> 201 us (level)
  no operation moved by 1% of the time
where the time goes in v11:
time: 201 us; the launch traced here: 199 us
  Pallas kernels  152 us (76%)
  local copies, waits for them, and re-layouts  22.8 us (11%)
  matrix products  13.4 us (7%)
  other arithmetic  5.94 us (3%)
    pallas_call x5, Pallas kernels, _transfer(): pl.pallas_call(functools.partial(_transfer_kernel, axis, gather), out_sha...  117 us
    pallas_call x1, Pallas kernels, pair_gather(): pl.pallas_call(_pair_gather_kernel, out_shape=jax.ShapeDtypeStruct(shape,...  34.3 us
  transfers between devices with their start and end apart: 1, of which 1 were waited for; matrix products, arithmetic and copies ran while one was open for 0% of the time, Pallas kernels for 0%

profile of v11, /device:TPU:24, one launch (start us, length us, event | category | flops | bytes accessed | tf_op | source)
XLA Modules:
  0.0 198.7 jit_solution(127272891972675000)
XLA Ops:
  0.8 0.9 reshape.359
  2.9 26.8 %shard_map.145 = bf16[64,8,128]{2,1,0:T(8,128)(2,1)} custom-call(bf16[64,8,128]{2,1,0:T(8,128)(2,1)} %bitcast.89), custom_call_target="tpu_custom_call" | custom-call | tf_op jit(solution)/shard_map/pallas_call | solution.py:96
  29.7 1.0 concatenate.53
  30.8 0.9 copy.65
  35.7 1.3 fusion.12.x_ref
  37.0 12.5 %shard_map.146 = bf16[8,64,360]{2,1,0:T(8,128)(2,1)} custom-call(bf16[8,64,360]{2,1,0:T(8,128)(2,1)} %fusion.12.x_ref), custom_call_target="tpu_custom_call" | custom-call | tf_op jit(solution)/shard_map/pallas_call | solution.py:96
  49.6 1.1 convert_reduce_fusion.1
  53.6 25.4 %shard_map.147 = bf16[32,30,128]{2,1,0:T(8,128)(2,1)} custom-call(bf16[32,30,128]{2,1,0:T(8,128)(2,1)} %reshape.351.x_ref), custom_call_target="tpu_custom_call" | custom-call | tf_op jit(solution)/shard_map/pallas_call | solution.py:96
  79.0 1.8 reshape_reshape_reshape.3.x_ref
  80.8 34.3 %shard_map.148 = bf16[8,2,320,384]{3,2,1,0:T(8,128)(2,1)} custom-call(bf16[320,384]{1,0:T(8,128)(2,1)} %reshape_reshape_reshape.3.x_ref), custom_call_target="tpu_custom_call" | custom-call | tf_op jit(solution)/shard_map/pallas_call | solution.py:172
  115.1 2.8 %reshape_squeeze.10 = bf16[8,360,180]{1,0,2:T(8,128)(2,1)S(1)} reshape(bf16[1,2880,180]{1,2,0:T(8,128)(2,1)} %param.28) | data formatting | bytes 2073600 | tf_op jit(solution)/shard_map/reshape;squeeze | solution.py:333
  117.9 1.9 convert_reduce_fusion
  119.8 3.5 %fusion.6 = f32[640,180]{0,1:T(8,128)S(1)} fusion(bf16[8,640,384]{2,1,0:T(8,128)(2,1)} %bitcast.80, bf16[8,360,180]{1,0,2:T(8,128)(2,1)S(1)} %reshape_squeeze.10), kind=kOutput, calls=%fused_computation.10 | convolution fusion | flops 663552000 | bytes 5429760 | tf_op jit(solution)/shard_map/tsf,tfh->sh/dot_general | solution.py:337
  123.3 2.8 %reshape_squeeze.9 = bf16[8,360,180]{1,0,2:T(8,128)(2,1)S(1)} reshape(bf16[1,2880,180]{1,2,0:T(8,128)(2,1)} %param.27) | data formatting | bytes 2073600 | tf_op jit(solution)/shard_map/reshape;squeeze | solution.py:332
  126.1 3.5 %fusion.9 = f32[640,180]{0,1:T(8,128)S(1)} fusion(bf16[8,640,384]{2,1,0:T(8,128)(2,1)} %bitcast.81, bf16[8,360,180]{1,0,2:T(8,128)(2,1)S(1)} %reshape_squeeze.9), kind=kOutput, calls=%fused_computation.11 | convolution fusion | flops 663552000 | bytes 5429760 | tf_op jit(solution)/shard_map/tsf,tfh->sh/dot_general | solution.py:336
  130.6 28.9 %shard_map.149 = bf16[8,180,640]{2,1,0:T(8,128)(2,1)} custom-call(bf16[180,640]{1,0:T(8,128)(2,1)} %fusion.24.x_ref), custom_call_target="tpu_custom_call" | custom-call | tf_op jit(solution)/shard_map/pallas_call | solution.py:96
  159.5 2.3 %reshape_squeeze.11 = bf16[8,180,360]{2,1,0:T(8,128)(2,1)} reshape(bf16[1,1440,360]{2,1,0:T(8,128)(2,1)} %param.29) | data formatting | bytes 2073600 | tf_op jit(solution)/shard_map/reshape;squeeze | solution.py:346
  161.9 3.1 %fusion.5 = bf16[640,360]{0,1:T(8,128)(2,1)} fusion(bf16[8,180,640]{2,1,0:T(8,128)(2,1)S(1)} %copy-done.1, bf16[8,180,360]{2,1,0:T(8,128)(2,1)} %reshape_squeeze.11), kind=kOutput, calls=%fused_computation.8 | convolution fusion | flops 663782400 | bytes 3340800 | tf_op jit(solution)/shard_map/ths,thd->sd/dot_general | solution.py:347
  165.0 1.3 copy.82
  167.3 1.9 collective-permute-start
  169.5 1.6 collective-permute-done
  172.4 23.8 %shard_map.150 = bf16[32,29,128]{2,1,0:T(8,128)(2,1)} custom-call(bf16[32,29,128]{2,1,0:T(8,128)(2,1)} %reshape.355.x_ref), custom_call_target="tpu_custom_call" | custom-call | tf_op jit(solution)/shard_map/pallas_call | solution.py:96
  196.2 1.0 copy.90
  197.7 1.0 fusion.15
  (86 shorter events, 11.8 us)
Async XLA Ops:
  0.0 35.7 %copy-start = (bf16[256,2880]{0,1:T(8,128)(2,1)S(1)}, bf16[256,2880]{0,1:T(8,128)(2,1)}, u32[]{:S(2)}) copy-start(bf16[256,2880]{0,1:T(8,128)(2,1)} %param.22) | copy-start | bytes 4423684
  1.7 31.2 %copy-start.7 = (s32[1,64]{1,0:T(1,128)S(1)}, s32[1,64]{1,0:T(1,128)}, u32[]{:S(2)}) copy-start(s32[1,64]{1,0:T(1,128)} %param.19) | copy-start | bytes 772
  31.8 2.1 %copy-start.6 = (f32[4]{0:T(128)S(1)}, f32[4]{0:T(128)}, u32[]{:S(2)}) copy-start(f32[4]{0:T(128)} %param.21) | copy-start | bytes 52
  35.7 15.8 %copy-start.2 = (bf16[64,360]{1,0:T(8,128)(2,1)S(1)}, bf16[64,360]{1,0:T(8,128)(2,1)}, u32[]{:S(2)}) copy-start(bf16[64,360]{1,0:T(8,128)(2,1)} %param.23) | copy-start | bytes 138244
  35.7 16.1 %copy-start.4 = (s32[64,4]{0,1:T(4,128)S(1)}, s32[64,4]{0,1:T(4,128)}, u32[]{:S(2)}) copy-start(s32[64,4]{0,1:T(4,128)} %param.25) | copy-start | bytes 3076
  159.5 2.3 %copy-start.1 = (bf16[8,180,640]{2,1,0:T(8,128)(2,1)S(1)}, bf16[8,180,640]{2,1,0:T(8,128)(2,1)}, u32[]{:S(2)}) copy-start(bf16[8,180,640]{2,1,0:T(8,128)(2,1)} %shard_map.149) | copy-start | bytes 5529604
  165.0 4.4 %copy-start.5 = (f32[64,4]{0,1:T(4,128)S(1)}, f32[64,4]{0,1:T(4,128)}, u32[]{:S(2)}) copy-start(f32[64,4]{0,1:T(4,128)} %param.26) | copy-start | bytes 3076
  167.3 3.8 %collective-permute-start = (bf16[32,10,360]{2,1,0:T(8,128)(2,1)}, bf16[32,10,360]{2,1,0:T(8,128)(2,1)S(1)}, u32[]{:S(2)}, u32[]{:S(2)}) collective-permute-start(bf16[32,10,360]{2,1,0:T(8,128)(2,1)} %dynamic-slice_bitcast_fusion), channel_id=1, source_target_pairs={{0,8},{8,0},{16,24},{24,16},{32,40},{40,32},{48,56},{56,48},{64,72... | collective-permute-start | bytes 691208 | tf_op jit(solution)/shard_map/ppermute | solution.py:356
  171.2 26.5 %copy-start.3 = (bf16[64,360]{1,0:T(8,128)(2,1)S(1)}, bf16[64,360]{1,0:T(8,128)(2,1)}, u32[]{:S(2)}) copy-start(bf16[64,360]{1,0:T(8,128)(2,1)} %param.23) | copy-start | bytes 138244

commit v12 on v11

--- a/solution.py
+++ b/solution.py
@@ -126,6 +126,14 @@
     pl.semaphore_wait(barrier, count)
     local = pltpu.make_async_copy(x_ref, buf.at[tp_at, core], local_sem)
     local.start()
+    pltpu.make_async_remote_copy(
+        src_ref=x_ref,
+        dst_ref=buf.at[tp_at, core],
+        send_sem=pass_send,
+        recv_sem=pass_recv,
+        device_id=sibling,
+        device_id_type=pl.DeviceIdType.MESH,
+    ).start()
 
     for first, size in _row_parts(x_ref.shape[0]):
 
@@ -152,6 +160,20 @@
         device_id_type=pl.DeviceIdType.MESH,
     )
     every.wait_recv()
+
+    def relay(step, carry):
+        source = lax.rem(tp_at + count - step, count)
+        pltpu.make_async_remote_copy(
+            src_ref=buf.at[source, core],
+            dst_ref=buf.at[source, core],
+            send_sem=pass_send,
+            recv_sem=pass_recv,
+            device_id=sibling,
+            device_id_type=pl.DeviceIdType.MESH,
+        ).start()
+        return carry
+
+    lax.fori_loop(1, count, relay, 0)
     onward = pltpu.make_async_remote_copy(
         src_ref=buf.at[:, core],
         dst_ref=buf.at[:, core],
@@ -160,7 +182,6 @@
         device_id=sibling,
         device_id_type=pl.DeviceIdType.MESH,
     )
-    onward.start()
     every.wait_send()
     onward.wait_send()
     onward.wait_recv()

time: 201 us -> 201 us (level)
  no operation moved by 1% of the time
where the time goes in v12:
time: 201 us; the launch traced here: 198 us
  Pallas kernels  151 us (75%)
  local copies, waits for them, and re-layouts  22.8 us (11%)
  matrix products  13.4 us (7%)
  other arithmetic  5.94 us (3%)
    pallas_call x5, Pallas kernels, _transfer(): pl.pallas_call(functools.partial(_transfer_kernel, axis, gather), out_sha...  117 us
    pallas_call x1, Pallas kernels, pair_gather(): pl.pallas_call(_pair_gather_kernel, out_shape=jax.ShapeDtypeStruct(shape,...  33.9 us
  transfers between devices with their start and end apart: 1, of which 1 were waited for; matrix products, arithmetic and copies ran while one was open for 0% of the time, Pallas kernels for 0%

profile of v12, /device:TPU:24, one launch (start us, length us, event | category | flops | bytes accessed | tf_op | source)
XLA Modules:
  0.0 198.3 jit_solution(18342306648379704586)
XLA Ops:
  0.8 0.9 reshape.359
  2.9 26.8 %shard_map.145 = bf16[64,8,128]{2,1,0:T(8,128)(2,1)} custom-call(bf16[64,8,128]{2,1,0:T(8,128)(2,1)} %bitcast.89), custom_call_target="tpu_custom_call" | custom-call | tf_op jit(solution)/shard_map/pallas_call | solution.py:96
  29.7 1.0 concatenate.53
  30.8 0.9 copy.65
  35.7 1.3 fusion.12.x_ref
  37.0 12.5 %shard_map.146 = bf16[8,64,360]{2,1,0:T(8,128)(2,1)} custom-call(bf16[8,64,360]{2,1,0:T(8,128)(2,1)} %fusion.12.x_ref), custom_call_target="tpu_custom_call" | custom-call | tf_op jit(solution)/shard_map/pallas_call | solution.py:96
  49.6 1.1 convert_reduce_fusion.1
  53.6 25.4 %shard_map.147 = bf16[32,30,128]{2,1,0:T(8,128)(2,1)} custom-call(bf16[32,30,128]{2,1,0:T(8,128)(2,1)} %reshape.351.x_ref), custom_call_target="tpu_custom_call" | custom-call | tf_op jit(solution)/shard_map/pallas_call | solution.py:96
  79.0 1.8 reshape_reshape_reshape.3.x_ref
  80.8 33.9 %shard_map.148 = bf16[8,2,320,384]{3,2,1,0:T(8,128)(2,1)} custom-call(bf16[320,384]{1,0:T(8,128)(2,1)} %reshape_reshape_reshape.3.x_ref), custom_call_target="tpu_custom_call" | custom-call | tf_op jit(solution)/shard_map/pallas_call | solution.py:193
  114.8 2.8 %reshape_squeeze.10 = bf16[8,360,180]{1,0,2:T(8,128)(2,1)S(1)} reshape(bf16[1,2880,180]{1,2,0:T(8,128)(2,1)} %param.28) | data formatting | bytes 2073600 | tf_op jit(solution)/shard_map/reshape;squeeze | solution.py:354
  117.6 1.9 convert_reduce_fusion
  119.5 3.5 %fusion.6 = f32[640,180]{0,1:T(8,128)S(1)} fusion(bf16[8,640,384]{2,1,0:T(8,128)(2,1)} %bitcast.80, bf16[8,360,180]{1,0,2:T(8,128)(2,1)S(1)} %reshape_squeeze.10), kind=kOutput, calls=%fused_computation.10 | convolution fusion | flops 663552000 | bytes 5429760 | tf_op jit(solution)/shard_map/tsf,tfh->sh/dot_general | solution.py:358
  123.0 2.8 %reshape_squeeze.9 = bf16[8,360,180]{1,0,2:T(8,128)(2,1)S(1)} reshape(bf16[1,2880,180]{1,2,0:T(8,128)(2,1)} %param.27) | data formatting | bytes 2073600 | tf_op jit(solution)/shard_map/reshape;squeeze | solution.py:353
  125.8 3.5 %fusion.9 = f32[640,180]{0,1:T(8,128)S(1)} fusion(bf16[8,640,384]{2,1,0:T(8,128)(2,1)} %bitcast.81, bf16[8,360,180]{1,0,2:T(8,128)(2,1)S(1)} %reshape_squeeze.9), kind=kOutput, calls=%fused_computation.11 | convolution fusion | flops 663552000 | bytes 5429760 | tf_op jit(solution)/shard_map/tsf,tfh->sh/dot_general | solution.py:357
  130.3 28.9 %shard_map.149 = bf16[8,180,640]{2,1,0:T(8,128)(2,1)} custom-call(bf16[180,640]{1,0:T(8,128)(2,1)} %fusion.24.x_ref), custom_call_target="tpu_custom_call" | custom-call | tf_op jit(solution)/shard_map/pallas_call | solution.py:96
  159.2 2.3 %reshape_squeeze.11 = bf16[8,180,360]{2,1,0:T(8,128)(2,1)} reshape(bf16[1,1440,360]{2,1,0:T(8,128)(2,1)} %param.29) | data formatting | bytes 2073600 | tf_op jit(solution)/shard_map/reshape;squeeze | solution.py:367
  161.5 3.1 %fusion.5 = bf16[640,360]{0,1:T(8,128)(2,1)} fusion(bf16[8,180,640]{2,1,0:T(8,128)(2,1)S(1)} %copy-done.1, bf16[8,180,360]{2,1,0:T(8,128)(2,1)} %reshape_squeeze.11), kind=kOutput, calls=%fused_computation.8 | convolution fusion | flops 663782400 | bytes 3340800 | tf_op jit(solution)/shard_map/ths,thd->sd/dot_general | solution.py:368
  164.6 1.3 copy.82
  166.9 1.9 collective-permute-start
  169.1 1.6 collective-permute-done
  172.0 23.8 %shard_map.150 = bf16[32,29,128]{2,1,0:T(8,128)(2,1)} custom-call(bf16[32,29,128]{2,1,0:T(8,128)(2,1)} %reshape.355.x_ref), custom_call_target="tpu_custom_call" | custom-call | tf_op jit(solution)/shard_map/pallas_call | solution.py:96
  195.8 1.0 copy.90
  197.3 1.0 fusion.15
  (86 shorter events, 11.8 us)
Async XLA Ops:
  0.0 35.7 %copy-start = (bf16[256,2880]{0,1:T(8,128)(2,1)S(1)}, bf16[256,2880]{0,1:T(8,128)(2,1)}, u32[]{:S(2)}) copy-start(bf16[256,2880]{0,1:T(8,128)(2,1)} %param.22) | copy-start | bytes 4423684
  1.7 31.2 %copy-start.7 = (s32[1,64]{1,0:T(1,128)S(1)}, s32[1,64]{1,0:T(1,128)}, u32[]{:S(2)}) copy-start(s32[1,64]{1,0:T(1,128)} %param.19) | copy-start | bytes 772
  31.8 2.1 %copy-start.6 = (f32[4]{0:T(128)S(1)}, f32[4]{0:T(128)}, u32[]{:S(2)}) copy-start(f32[4]{0:T(128)} %param.21) | copy-start | bytes 52
  35.7 15.8 %copy-start.2 = (bf16[64,360]{1,0:T(8,128)(2,1)S(1)}, bf16[64,360]{1,0:T(8,128)(2,1)}, u32[]{:S(2)}) copy-start(bf16[64,360]{1,0:T(8,128)(2,1)} %param.23) | copy-start | bytes 138244
  35.7 16.1 %copy-start.4 = (s32[64,4]{0,1:T(4,128)S(1)}, s32[64,4]{0,1:T(4,128)}, u32[]{:S(2)}) copy-start(s32[64,4]{0,1:T(4,128)} %param.25) | copy-start | bytes 3076
  159.2 2.3 %copy-start.1 = (bf16[8,180,640]{2,1,0:T(8,128)(2,1)S(1)}, bf16[8,180,640]{2,1,0:T(8,128)(2,1)}, u32[]{:S(2)}) copy-start(bf16[8,180,640]{2,1,0:T(8,128)(2,1)} %shard_map.149) | copy-start | bytes 5529604
  164.6 4.4 %copy-start.5 = (f32[64,4]{0,1:T(4,128)S(1)}, f32[64,4]{0,1:T(4,128)}, u32[]{:S(2)}) copy-start(f32[64,4]{0,1:T(4,128)} %param.26) | copy-start | bytes 3076
  166.9 3.8 %collective-permute-start = (bf16[32,10,360]{2,1,0:T(8,128)(2,1)}, bf16[32,10,360]{2,1,0:T(8,128)(2,1)S(1)}, u32[]{:S(2)}, u32[]{:S(2)}) collective-permute-start(bf16[32,10,360]{2,1,0:T(8,128)(2,1)} %dynamic-slice_bitcast_fusion), channel_id=1, source_target_pairs={{0,8},{8,0},{16,24},{24,16},{32,40},{40,32},{48,56},{56,48},{64,72... | collective-permute-start | bytes 691208 | tf_op jit(solution)/shard_map/ppermute | solution.py:377
  170.8 26.5 %copy-start.3 = (bf16[64,360]{1,0:T(8,128)(2,1)S(1)}, bf16[64,360]{1,0:T(8,128)(2,1)}, u32[]{:S(2)}) copy-start(bf16[64,360]{1,0:T(8,128)(2,1)} %param.23) | copy-start | bytes 138244

commit v13 on v12

--- a/solution.py
+++ b/solution.py
@@ -13,6 +13,11 @@
 THETA = 150000.0
 ALPHA = 1.702
 EPSILON = 1e-05
+
+
+def _offset(step, count):
+    odd = lax.rem(step, 2)
+    return odd * lax.div(step + 1, 2) + (1 - odd) * (count - lax.div(step, 2))
 
 
 def _row_parts(rows, parts=8):
@@ -59,7 +64,7 @@
     for first, size in _row_parts(buf.shape[1] if (gather or axis == "tp") else 0):
 
         def send(step, carry, first=first, size=size):
-            peer = lax.rem(me + step, count)
+            peer = lax.rem(me + _offset(step, count), count)
             src = piece(peer)
             dst = buf.at[me]
             if size:
@@ -138,7 +143,7 @@
     for first, size in _row_parts(x_ref.shape[0]):
 
         def send(step, carry, first=first, size=size):
-            peer = lax.rem(tp_at + step, count)
+            peer = lax.rem(tp_at + _offset(step, count), count)
             pltpu.make_async_remote_copy(
                 src_ref=x_ref.at[pl.ds(first, size)],
                 dst_ref=buf.at[tp_at, core, pl.ds(first, size)],

time: 201 us -> 203 us (level)
  Pallas kernels: 151 us -> 155 us
    pallas_call x5, Pallas kernels: 117 us -> 122 us  [_transfer(): pl.pallas_call(functools.partial(_transfer_kernel, axis, gather), out_sha...]
where the time goes in v13:
time: 203 us; the launch traced here: 202 us
  Pallas kernels  155 us (76%)
  local copies, waits for them, and re-layouts  22.8 us (11%)
  matrix products  13.4 us (7%)
  other arithmetic  5.94 us (3%)
    pallas_call x5, Pallas kernels, _transfer(): pl.pallas_call(functools.partial(_transfer_kernel, axis, gather), out_sha...  122 us
    pallas_call x1, Pallas kernels, pair_gather(): pl.pallas_call(_pair_gather_kernel, out_shape=jax.ShapeDtypeStruct(shape,...  32.7 us
  transfers between devices with their start and end apart: 1, of which 1 were waited for; matrix products, arithmetic and copies ran while one was open for 0% of the time, Pallas kernels for 0%

profile of v13, /device:TPU:24, one launch (start us, length us, event | category | flops | bytes accessed | tf_op | source)
XLA Modules:
  0.0 201.6 jit_solution(17485768795806602969)
XLA Ops:
  0.8 0.9 reshape.359
  2.9 28.7 %shard_map.145 = bf16[64,8,128]{2,1,0:T(8,128)(2,1)} custom-call(bf16[64,8,128]{2,1,0:T(8,128)(2,1)} %bitcast.89), custom_call_target="tpu_custom_call" | custom-call | tf_op jit(solution)/shard_map/pallas_call | solution.py:101
  31.6 1.0 concatenate.53
  32.7 0.9 copy.65
  37.6 1.3 fusion.12.x_ref
  38.9 12.1 %shard_map.146 = bf16[8,64,360]{2,1,0:T(8,128)(2,1)} custom-call(bf16[8,64,360]{2,1,0:T(8,128)(2,1)} %fusion.12.x_ref), custom_call_target="tpu_custom_call" | custom-call | tf_op jit(solution)/shard_map/pallas_call | solution.py:101
  51.1 1.1 convert_reduce_fusion.1
  55.1 25.1 %shard_map.147 = bf16[32,30,128]{2,1,0:T(8,128)(2,1)} custom-call(bf16[32,30,128]{2,1,0:T(8,128)(2,1)} %reshape.351.x_ref), custom_call_target="tpu_custom_call" | custom-call | tf_op jit(solution)/shard_map/pallas_call | solution.py:101
  80.2 1.8 reshape_reshape_reshape.3.x_ref
  82.0 32.7 %shard_map.148 = bf16[8,2,320,384]{3,2,1,0:T(8,128)(2,1)} custom-call(bf16[320,384]{1,0:T(8,128)(2,1)} %reshape_reshape_reshape.3.x_ref), custom_call_target="tpu_custom_call" | custom-call | tf_op jit(solution)/shard_map/pallas_call | solution.py:198
  114.7 2.8 %reshape_squeeze.10 = bf16[8,360,180]{1,0,2:T(8,128)(2,1)S(1)} reshape(bf16[1,2880,180]{1,2,0:T(8,128)(2,1)} %param.28) | data formatting | bytes 2073600 | tf_op jit(solution)/shard_map/reshape;squeeze | solution.py:359
  117.5 1.9 convert_reduce_fusion
  119.4 3.5 %fusion.6 = f32[640,180]{0,1:T(8,128)S(1)} fusion(bf16[8,640,384]{2,1,0:T(8,128)(2,1)} %bitcast.80, bf16[8,360,180]{1,0,2:T(8,128)(2,1)S(1)} %reshape_squeeze.10), kind=kOutput, calls=%fused_computation.10 | convolution fusion | flops 663552000 | bytes 5429760 | tf_op jit(solution)/shard_map/tsf,tfh->sh/dot_general | solution.py:363
  123.0 2.8 %reshape_squeeze.9 = bf16[8,360,180]{1,0,2:T(8,128)(2,1)S(1)} reshape(bf16[1,2880,180]{1,2,0:T(8,128)(2,1)} %param.27) | data formatting | bytes 2073600 | tf_op jit(solution)/shard_map/reshape;squeeze | solution.py:358
  125.8 3.5 %fusion.9 = f32[640,180]{0,1:T(8,128)S(1)} fusion(bf16[8,640,384]{2,1,0:T(8,128)(2,1)} %bitcast.81, bf16[8,360,180]{1,0,2:T(8,128)(2,1)S(1)} %reshape_squeeze.9), kind=kOutput, calls=%fused_computation.11 | convolution fusion | flops 663552000 | bytes 5429760 | tf_op jit(solution)/shard_map/tsf,tfh->sh/dot_general | solution.py:362
  130.3 28.6 %shard_map.149 = bf16[8,180,640]{2,1,0:T(8,128)(2,1)} custom-call(bf16[180,640]{1,0:T(8,128)(2,1)} %fusion.24.x_ref), custom_call_target="tpu_custom_call" | custom-call | tf_op jit(solution)/shard_map/pallas_call | solution.py:101
  158.9 2.3 %reshape_squeeze.11 = bf16[8,180,360]{2,1,0:T(8,128)(2,1)} reshape(bf16[1,1440,360]{2,1,0:T(8,128)(2,1)} %param.29) | data formatting | bytes 2073600 | tf_op jit(solution)/shard_map/reshape;squeeze | solution.py:372
  161.2 3.1 %fusion.5 = bf16[640,360]{0,1:T(8,128)(2,1)} fusion(bf16[8,180,640]{2,1,0:T(8,128)(2,1)S(1)} %copy-done.1, bf16[8,180,360]{2,1,0:T(8,128)(2,1)} %reshape_squeeze.11), kind=kOutput, calls=%fused_computation.8 | convolution fusion | flops 663782400 | bytes 3340800 | tf_op jit(solution)/shard_map/ths,thd->sd/dot_general | solution.py:373
  164.3 1.3 copy.82
  166.6 1.9 collective-permute-start
  168.8 1.6 collective-permute-done
  171.7 27.4 %shard_map.150 = bf16[32,29,128]{2,1,0:T(8,128)(2,1)} custom-call(bf16[32,29,128]{2,1,0:T(8,128)(2,1)} %reshape.355.x_ref), custom_call_target="tpu_custom_call" | custom-call | tf_op jit(solution)/shard_map/pallas_call | solution.py:101
  199.1 1.0 copy.90
  200.6 1.0 fusion.15
  (86 shorter events, 11.8 us)
Async XLA Ops:
  0.0 37.6 %copy-start = (bf16[256,2880]{0,1:T(8,128)(2,1)S(1)}, bf16[256,2880]{0,1:T(8,128)(2,1)}, u32[]{:S(2)}) copy-start(bf16[256,2880]{0,1:T(8,128)(2,1)} %param.22) | copy-start | bytes 4423684
  1.7 33.1 %copy-start.7 = (s32[1,64]{1,0:T(1,128)S(1)}, s32[1,64]{1,0:T(1,128)}, u32[]{:S(2)}) copy-start(s32[1,64]{1,0:T(1,128)} %param.19) | copy-start | bytes 772
  33.8 2.1 %copy-start.6 = (f32[4]{0:T(128)S(1)}, f32[4]{0:T(128)}, u32[]{:S(2)}) copy-start(f32[4]{0:T(128)} %param.21) | copy-start | bytes 52
  37.6 15.3 %copy-start.2 = (bf16[64,360]{1,0:T(8,128)(2,1)S(1)}, bf16[64,360]{1,0:T(8,128)(2,1)}, u32[]{:S(2)}) copy-start(bf16[64,360]{1,0:T(8,128)(2,1)} %param.23) | copy-start | bytes 138244
  37.6 15.7 %copy-start.4 = (s32[64,4]{0,1:T(4,128)S(1)}, s32[64,4]{0,1:T(4,128)}, u32[]{:S(2)}) copy-start(s32[64,4]{0,1:T(4,128)} %param.25) | copy-start | bytes 3076
  158.9 2.3 %copy-start.1 = (bf16[8,180,640]{2,1,0:T(8,128)(2,1)S(1)}, bf16[8,180,640]{2,1,0:T(8,128)(2,1)}, u32[]{:S(2)}) copy-start(bf16[8,180,640]{2,1,0:T(8,128)(2,1)} %shard_map.149) | copy-start | bytes 5529604
  164.3 4.4 %copy-start.5 = (f32[64,4]{0,1:T(4,128)S(1)}, f32[64,4]{0,1:T(4,128)}, u32[]{:S(2)}) copy-start(f32[64,4]{0,1:T(4,128)} %param.26) | copy-start | bytes 3076
  166.6 3.8 %collective-permute-start = (bf16[32,10,360]{2,1,0:T(8,128)(2,1)}, bf16[32,10,360]{2,1,0:T(8,128)(2,1)S(1)}, u32[]{:S(2)}, u32[]{:S(2)}) collective-permute-start(bf16[32,10,360]{2,1,0:T(8,128)(2,1)} %dynamic-slice_bitcast_fusion), channel_id=1, source_target_pairs={{0,8},{8,0},{16,24},{24,16},{32,40},{40,32},{48,56},{56,48},{64,72... | collective-permute-start | bytes 691208 | tf_op jit(solution)/shard_map/ppermute | solution.py:382
  170.5 30.1 %copy-start.3 = (bf16[64,360]{1,0:T(8,128)(2,1)S(1)}, bf16[64,360]{1,0:T(8,128)(2,1)}, u32[]{:S(2)}) copy-start(bf16[64,360]{1,0:T(8,128)(2,1)} %param.23) | copy-start | bytes 138244

commit v14 on v12

--- a/solution.py
+++ b/solution.py
@@ -22,7 +22,7 @@
     return [(first, min(step, rows - first)) for first in range(0, rows, step)]
 
 
-def _transfer_kernel(axis, gather, x_ref, o_ref, buf, send_sem, recv_sem, local_sem):
+def _transfer_kernel(axis, gather, x_ref, buf, send_sem, recv_sem, local_sem):
     count = buf.shape[0]
     group_at = lax.axis_index("group")
     tp_at = lax.axis_index("tp")
@@ -87,7 +87,6 @@
     )
     every.wait_send()
     every.wait_recv()
-    o_ref[...] = buf[...]
 
 
 def _transfer(x, axis, gather, collective_id):
@@ -99,7 +98,6 @@
         in_specs=[pl.BlockSpec(memory_space=pltpu.VMEM)],
         out_specs=pl.BlockSpec(memory_space=pltpu.VMEM),
         scratch_shapes=[
-            pltpu.VMEM(shape, x.dtype),
             pltpu.SemaphoreType.DMA(()),
             pltpu.SemaphoreType.DMA(()),
             pltpu.SemaphoreType.DMA(()),
@@ -108,7 +106,7 @@
     )(x)
 
 
-def _pair_gather_kernel(x_ref, o_ref, buf, send_sem, recv_sem, local_sem, pass_send, pass_recv):
+def _pair_gather_kernel(x_ref, buf, send_sem, recv_sem, local_sem, pass_send, pass_recv):
     count = buf.shape[0]
     group_at = lax.axis_index("group")
     tp_at = lax.axis_index("tp")
@@ -185,7 +183,6 @@
     every.wait_send()
     onward.wait_send()
     onward.wait_recv()
-    o_ref[...] = buf[...]
 
 
 def pair_gather(x, collective_id):
@@ -195,7 +192,7 @@
         out_shape=jax.ShapeDtypeStruct(shape, x.dtype),
         in_specs=[pl.BlockSpec(memory_space=pltpu.VMEM)],
         out_specs=pl.BlockSpec(memory_space=pltpu.VMEM),
-        scratch_shapes=[pltpu.VMEM(shape, x.dtype)] + [pltpu.SemaphoreType.DMA(())] * 5,
+        scratch_shapes=[pltpu.SemaphoreType.DMA(())] * 5,
         compiler_params=pltpu.CompilerParams(collective_id=collective_id, has_side_effects=True),
     )(x)
 

time: 201 us -> 200 us (level)
  no operation moved by 1% of the time
where the time goes in v14:
time: 200 us; the launch traced here: 198 us
  Pallas kernels  151 us (76%)
  local copies, waits for them, and re-layouts  22.8 us (11%)
  matrix products  13.4 us (7%)
  other arithmetic  5.94 us (3%)
    pallas_call x5, Pallas kernels, _transfer(): pl.pallas_call(functools.partial(_transfer_kernel, axis, gather), out_sha...  117 us
    pallas_call x1, Pallas kernels, pair_gather(): pl.pallas_call(_pair_gather_kernel, out_shape=jax.ShapeDtypeStruct(shape,...  33.6 us
  transfers between devices with their start and end apart: 1, of which 1 were waited for; matrix products, arithmetic and copies ran while one was open for 0% of the time, Pallas kernels for 0%

profile of v14, /device:TPU:24, one launch (start us, length us, event | category | flops | bytes accessed | tf_op | source)
XLA Modules:
  0.0 197.7 jit_solution(8372126263178784131)
XLA Ops:
  0.8 0.9 reshape.359
  2.9 26.8 %shard_map.145 = bf16[64,8,128]{2,1,0:T(8,128)(2,1)} custom-call(bf16[64,8,128]{2,1,0:T(8,128)(2,1)} %bitcast.89), custom_call_target="tpu_custom_call" | custom-call | tf_op jit(solution)/shard_map/pallas_call | solution.py:95
  29.7 1.0 concatenate.53
  30.8 0.9 copy.65
  35.7 1.3 fusion.12.x_ref
  37.0 12.5 %shard_map.146 = bf16[8,64,360]{2,1,0:T(8,128)(2,1)} custom-call(bf16[8,64,360]{2,1,0:T(8,128)(2,1)} %fusion.12.x_ref), custom_call_target="tpu_custom_call" | custom-call | tf_op jit(solution)/shard_map/pallas_call | solution.py:95
  49.5 1.1 convert_reduce_fusion.1
  53.6 25.3 %shard_map.147 = bf16[32,30,128]{2,1,0:T(8,128)(2,1)} custom-call(bf16[32,30,128]{2,1,0:T(8,128)(2,1)} %reshape.351.x_ref), custom_call_target="tpu_custom_call" | custom-call | tf_op jit(solution)/shard_map/pallas_call | solution.py:95
  78.9 1.8 reshape_reshape_reshape.3.x_ref
  80.7 33.6 %shard_map.148 = bf16[8,2,320,384]{3,2,1,0:T(8,128)(2,1)} custom-call(bf16[320,384]{1,0:T(8,128)(2,1)} %reshape_reshape_reshape.3.x_ref), custom_call_target="tpu_custom_call" | custom-call | tf_op jit(solution)/shard_map/pallas_call | solution.py:190
  114.4 2.8 %reshape_squeeze.10 = bf16[8,360,180]{1,0,2:T(8,128)(2,1)S(1)} reshape(bf16[1,2880,180]{1,2,0:T(8,128)(2,1)} %param.28) | data formatting | bytes 2073600 | tf_op jit(solution)/shard_map/reshape;squeeze | solution.py:351
  117.1 1.9 convert_reduce_fusion
  119.0 3.5 %fusion.6 = f32[640,180]{0,1:T(8,128)S(1)} fusion(bf16[8,640,384]{2,1,0:T(8,128)(2,1)} %bitcast.80, bf16[8,360,180]{1,0,2:T(8,128)(2,1)S(1)} %reshape_squeeze.10), kind=kOutput, calls=%fused_computation.10 | convolution fusion | flops 663552000 | bytes 5429760 | tf_op jit(solution)/shard_map/tsf,tfh->sh/dot_general | solution.py:355
  122.6 2.8 %reshape_squeeze.9 = bf16[8,360,180]{1,0,2:T(8,128)(2,1)S(1)} reshape(bf16[1,2880,180]{1,2,0:T(8,128)(2,1)} %param.27) | data formatting | bytes 2073600 | tf_op jit(solution)/shard_map/reshape;squeeze | solution.py:350
  125.4 3.5 %fusion.9 = f32[640,180]{0,1:T(8,128)S(1)} fusion(bf16[8,640,384]{2,1,0:T(8,128)(2,1)} %bitcast.81, bf16[8,360,180]{1,0,2:T(8,128)(2,1)S(1)} %reshape_squeeze.9), kind=kOutput, calls=%fused_computation.11 | convolution fusion | flops 663552000 | bytes 5429760 | tf_op jit(solution)/shard_map/tsf,tfh->sh/dot_general | solution.py:354
  129.9 28.8 %shard_map.149 = bf16[8,180,640]{2,1,0:T(8,128)(2,1)} custom-call(bf16[180,640]{1,0:T(8,128)(2,1)} %fusion.24.x_ref), custom_call_target="tpu_custom_call" | custom-call | tf_op jit(solution)/shard_map/pallas_call | solution.py:95
  158.7 2.3 %reshape_squeeze.11 = bf16[8,180,360]{2,1,0:T(8,128)(2,1)} reshape(bf16[1,1440,360]{2,1,0:T(8,128)(2,1)} %param.29) | data formatting | bytes 2073600 | tf_op jit(solution)/shard_map/reshape;squeeze | solution.py:364
  161.0 3.1 %fusion.5 = bf16[640,360]{0,1:T(8,128)(2,1)} fusion(bf16[8,180,640]{2,1,0:T(8,128)(2,1)S(1)} %copy-done.1, bf16[8,180,360]{2,1,0:T(8,128)(2,1)} %reshape_squeeze.11), kind=kOutput, calls=%fused_computation.8 | convolution fusion | flops 663782400 | bytes 3340800 | tf_op jit(solution)/shard_map/ths,thd->sd/dot_general | solution.py:365
  164.1 1.3 copy.82
  166.4 1.9 collective-permute-start
  168.6 1.6 collective-permute-done
  171.5 23.8 %shard_map.150 = bf16[32,29,128]{2,1,0:T(8,128)(2,1)} custom-call(bf16[32,29,128]{2,1,0:T(8,128)(2,1)} %reshape.355.x_ref), custom_call_target="tpu_custom_call" | custom-call | tf_op jit(solution)/shard_map/pallas_call | solution.py:95
  195.2 1.0 copy.90
  196.7 1.0 fusion.15
  (86 shorter events, 11.8 us)
Async XLA Ops:
  0.0 35.7 %copy-start = (bf16[256,2880]{0,1:T(8,128)(2,1)S(1)}, bf16[256,2880]{0,1:T(8,128)(2,1)}, u32[]{:S(2)}) copy-start(bf16[256,2880]{0,1:T(8,128)(2,1)} %param.22) | copy-start | bytes 4423684
  1.7 31.2 %copy-start.7 = (s32[1,64]{1,0:T(1,128)S(1)}, s32[1,64]{1,0:T(1,128)}, u32[]{:S(2)}) copy-start(s32[1,64]{1,0:T(1,128)} %param.19) | copy-start | bytes 772
  31.8 2.1 %copy-start.6 = (f32[4]{0:T(128)S(1)}, f32[4]{0:T(128)}, u32[]{:S(2)}) copy-start(f32[4]{0:T(128)} %param.21) | copy-start | bytes 52
  35.7 15.7 %copy-start.2 = (bf16[64,360]{1,0:T(8,128)(2,1)S(1)}, bf16[64,360]{1,0:T(8,128)(2,1)}, u32[]{:S(2)}) copy-start(bf16[64,360]{1,0:T(8,128)(2,1)} %param.23) | copy-start | bytes 138244
  35.7 16.1 %copy-start.4 = (s32[64,4]{0,1:T(4,128)S(1)}, s32[64,4]{0,1:T(4,128)}, u32[]{:S(2)}) copy-start(s32[64,4]{0,1:T(4,128)} %param.25) | copy-start | bytes 3076
  158.6 2.3 %copy-start.1 = (bf16[8,180,640]{2,1,0:T(8,128)(2,1)S(1)}, bf16[8,180,640]{2,1,0:T(8,128)(2,1)}, u32[]{:S(2)}) copy-start(bf16[8,180,640]{2,1,0:T(8,128)(2,1)} %shard_map.149) | copy-start | bytes 5529604
  164.1 4.4 %copy-start.5 = (f32[64,4]{0,1:T(4,128)S(1)}, f32[64,4]{0,1:T(4,128)}, u32[]{:S(2)}) copy-start(f32[64,4]{0,1:T(4,128)} %param.26) | copy-start | bytes 3076
  166.4 3.8 %collective-permute-start = (bf16[32,10,360]{2,1,0:T(8,128)(2,1)}, bf16[32,10,360]{2,1,0:T(8,128)(2,1)S(1)}, u32[]{:S(2)}, u32[]{:S(2)}) collective-permute-start(bf16[32,10,360]{2,1,0:T(8,128)(2,1)} %dynamic-slice_bitcast_fusion), channel_id=1, source_target_pairs={{0,8},{8,0},{16,24},{24,16},{32,40},{40,32},{48,56},{56,48},{64,72... | collective-permute-start | bytes 691208 | tf_op jit(solution)/shard_map/ppermute | solution.py:374
  170.3 26.4 %copy-start.3 = (bf16[64,360]{1,0:T(8,128)(2,1)S(1)}, bf16[64,360]{1,0:T(8,128)(2,1)}, u32[]{:S(2)}) copy-start(bf16[64,360]{1,0:T(8,128)(2,1)} %param.23) | copy-start | bytes 138244

commit v15 on v14

--- a/solution.py
+++ b/solution.py
@@ -141,7 +141,7 @@
                 src_ref=x_ref.at[pl.ds(first, size)],
                 dst_ref=buf.at[tp_at, core, pl.ds(first, size)],
                 send_sem=send_sem,
-                recv_sem=recv_sem,
+                recv_sem=recv_sem.at[tp_at],
                 device_id=(group_at, peer),
                 device_id_type=pl.DeviceIdType.MESH,
             ).start()
@@ -153,14 +153,21 @@
         src_ref=buf.at[pl.ds(0, count - 1), 0],
         dst_ref=buf.at[pl.ds(0, count - 1), 0],
         send_sem=send_sem,
-        recv_sem=recv_sem,
+        recv_sem=recv_sem.at[0],
         device_id=(group_at, lax.rem(tp_at + 1, count)),
         device_id_type=pl.DeviceIdType.MESH,
     )
-    every.wait_recv()
 
     def relay(step, carry):
         source = lax.rem(tp_at + count - step, count)
+        pltpu.make_async_remote_copy(
+            src_ref=buf.at[source, core],
+            dst_ref=buf.at[source, core],
+            send_sem=pass_send,
+            recv_sem=recv_sem.at[source],
+            device_id=sibling,
+            device_id_type=pl.DeviceIdType.MESH,
+        ).wait_recv()
         pltpu.make_async_remote_copy(
             src_ref=buf.at[source, core],
             dst_ref=buf.at[source, core],
@@ -192,7 +199,7 @@
         out_shape=jax.ShapeDtypeStruct(shape, x.dtype),
         in_specs=[pl.BlockSpec(memory_space=pltpu.VMEM)],
         out_specs=pl.BlockSpec(memory_space=pltpu.VMEM),
-        scratch_shapes=[pltpu.SemaphoreType.DMA(())] * 5,
+        scratch_shapes=[pltpu.SemaphoreType.DMA(()), pltpu.SemaphoreType.DMA((shape[0],))] + [pltpu.SemaphoreType.DMA(())] * 3,
         compiler_params=pltpu.CompilerParams(collective_id=collective_id, has_side_effects=True),
     )(x)
 

time: 200 us -> 200 us (level)
  no operation moved by 1% of the time
where the time goes in v15:
time: 200 us; the launch traced here: 198 us
  Pallas kernels  151 us (76%)
  local copies, waits for them, and re-layouts  22.8 us (11%)
  matrix products  13.4 us (7%)
  other arithmetic  5.94 us (3%)
    pallas_call x5, Pallas kernels, _transfer(): pl.pallas_call(functools.partial(_transfer_kernel, axis, gather), out_sha...  118 us
    pallas_call x1, Pallas kernels, pair_gather(): pl.pallas_call(_pair_gather_kernel, out_shape=jax.ShapeDtypeStruct(shape,...  32.3 us
  transfers between devices with their start and end apart: 1, of which 1 were waited for; matrix products, arithmetic and copies ran while one was open for 0% of the time, Pallas kernels for 0%

profile of v15, /device:TPU:24, one launch (start us, length us, event | category | flops | bytes accessed | tf_op | source)
XLA Modules:
  0.0 197.6 jit_solution(842263728986789990)
XLA Ops:
  0.8 0.9 reshape.359
  2.9 26.8 %shard_map.145 = bf16[64,8,128]{2,1,0:T(8,128)(2,1)} custom-call(bf16[64,8,128]{2,1,0:T(8,128)(2,1)} %bitcast.89), custom_call_target="tpu_custom_call" | custom-call | tf_op jit(solution)/shard_map/pallas_call | solution.py:95
  29.7 1.0 concatenate.53
  30.8 0.9 copy.65
  35.7 1.3 fusion.12.x_ref
  37.0 12.5 %shard_map.146 = bf16[8,64,360]{2,1,0:T(8,128)(2,1)} custom-call(bf16[8,64,360]{2,1,0:T(8,128)(2,1)} %fusion.12.x_ref), custom_call_target="tpu_custom_call" | custom-call | tf_op jit(solution)/shard_map/pallas_call | solution.py:95
  49.5 1.1 convert_reduce_fusion.1
  53.6 25.3 %shard_map.147 = bf16[32,30,128]{2,1,0:T(8,128)(2,1)} custom-call(bf16[32,30,128]{2,1,0:T(8,128)(2,1)} %reshape.351.x_ref), custom_call_target="tpu_custom_call" | custom-call | tf_op jit(solution)/shard_map/pallas_call | solution.py:95
  78.9 1.8 reshape_reshape_reshape.3.x_ref
  80.7 32.3 %shard_map.148 = bf16[8,2,320,384]{3,2,1,0:T(8,128)(2,1)} custom-call(bf16[320,384]{1,0:T(8,128)(2,1)} %reshape_reshape_reshape.3.x_ref), custom_call_target="tpu_custom_call" | custom-call | tf_op jit(solution)/shard_map/pallas_call | solution.py:197
  113.0 2.8 %reshape_squeeze.10 = bf16[8,360,180]{1,0,2:T(8,128)(2,1)S(1)} reshape(bf16[1,2880,180]{1,2,0:T(8,128)(2,1)} %param.28) | data formatting | bytes 2073600 | tf_op jit(solution)/shard_map/reshape;squeeze | solution.py:358
  115.8 1.9 convert_reduce_fusion
  117.7 3.5 %fusion.6 = f32[640,180]{0,1:T(8,128)S(1)} fusion(bf16[8,640,384]{2,1,0:T(8,128)(2,1)} %bitcast.80, bf16[8,360,180]{1,0,2:T(8,128)(2,1)S(1)} %reshape_squeeze.10), kind=kOutput, calls=%fused_computation.10 | convolution fusion | flops 663552000 | bytes 5429760 | tf_op jit(solution)/shard_map/tsf,tfh->sh/dot_general | solution.py:362
  121.2 2.8 %reshape_squeeze.9 = bf16[8,360,180]{1,0,2:T(8,128)(2,1)S(1)} reshape(bf16[1,2880,180]{1,2,0:T(8,128)(2,1)} %param.27) | data formatting | bytes 2073600 | tf_op jit(solution)/shard_map/reshape;squeeze | solution.py:357
  124.0 3.5 %fusion.9 = f32[640,180]{0,1:T(8,128)S(1)} fusion(bf16[8,640,384]{2,1,0:T(8,128)(2,1)} %bitcast.81, bf16[8,360,180]{1,0,2:T(8,128)(2,1)S(1)} %reshape_squeeze.9), kind=kOutput, calls=%fused_computation.11 | convolution fusion | flops 663552000 | bytes 5429760 | tf_op jit(solution)/shard_map/tsf,tfh->sh/dot_general | solution.py:361
  128.5 28.9 %shard_map.149 = bf16[8,180,640]{2,1,0:T(8,128)(2,1)} custom-call(bf16[180,640]{1,0:T(8,128)(2,1)} %fusion.24.x_ref), custom_call_target="tpu_custom_call" | custom-call | tf_op jit(solution)/shard_map/pallas_call | solution.py:95
  157.4 2.3 %reshape_squeeze.11 = bf16[8,180,360]{2,1,0:T(8,128)(2,1)} reshape(bf16[1,1440,360]{2,1,0:T(8,128)(2,1)} %param.29) | data formatting | bytes 2073600 | tf_op jit(solution)/shard_map/reshape;squeeze | solution.py:371
  159.7 3.1 %fusion.5 = bf16[640,360]{0,1:T(8,128)(2,1)} fusion(bf16[8,180,640]{2,1,0:T(8,128)(2,1)S(1)} %copy-done.1, bf16[8,180,360]{2,1,0:T(8,128)(2,1)} %reshape_squeeze.11), kind=kOutput, calls=%fused_computation.8 | convolution fusion | flops 663782400 | bytes 3340800 | tf_op jit(solution)/shard_map/ths,thd->sd/dot_general | solution.py:372
  162.8 1.3 copy.82
  165.1 1.9 collective-permute-start
  167.4 1.6 collective-permute-done
  170.2 24.9 %shard_map.150 = bf16[32,29,128]{2,1,0:T(8,128)(2,1)} custom-call(bf16[32,29,128]{2,1,0:T(8,128)(2,1)} %reshape.355.x_ref), custom_call_target="tpu_custom_call" | custom-call | tf_op jit(solution)/shard_map/pallas_call | solution.py:95
  195.1 1.0 copy.90
  196.6 1.0 fusion.15
  (86 shorter events, 11.8 us)
Async XLA Ops:
  0.0 35.7 %copy-start = (bf16[256,2880]{0,1:T(8,128)(2,1)S(1)}, bf16[256,2880]{0,1:T(8,128)(2,1)}, u32[]{:S(2)}) copy-start(bf16[256,2880]{0,1:T(8,128)(2,1)} %param.22) | copy-start | bytes 4423684
  1.7 31.2 %copy-start.7 = (s32[1,64]{1,0:T(1,128)S(1)}, s32[1,64]{1,0:T(1,128)}, u32[]{:S(2)}) copy-start(s32[1,64]{1,0:T(1,128)} %param.19) | copy-start | bytes 772
  31.8 2.1 %copy-start.6 = (f32[4]{0:T(128)S(1)}, f32[4]{0:T(128)}, u32[]{:S(2)}) copy-start(f32[4]{0:T(128)} %param.21) | copy-start | bytes 52
  35.7 15.7 %copy-start.2 = (bf16[64,360]{1,0:T(8,128)(2,1)S(1)}, bf16[64,360]{1,0:T(8,128)(2,1)}, u32[]{:S(2)}) copy-start(bf16[64,360]{1,0:T(8,128)(2,1)} %param.23) | copy-start | bytes 138244
  35.7 16.1 %copy-start.4 = (s32[64,4]{0,1:T(4,128)S(1)}, s32[64,4]{0,1:T(4,128)}, u32[]{:S(2)}) copy-start(s32[64,4]{0,1:T(4,128)} %param.25) | copy-start | bytes 3076
  157.4 2.3 %copy-start.1 = (bf16[8,180,640]{2,1,0:T(8,128)(2,1)S(1)}, bf16[8,180,640]{2,1,0:T(8,128)(2,1)}, u32[]{:S(2)}) copy-start(bf16[8,180,640]{2,1,0:T(8,128)(2,1)} %shard_map.149) | copy-start | bytes 5529604
  162.8 4.4 %copy-start.5 = (f32[64,4]{0,1:T(4,128)S(1)}, f32[64,4]{0,1:T(4,128)}, u32[]{:S(2)}) copy-start(f32[64,4]{0,1:T(4,128)} %param.26) | copy-start | bytes 3076
  165.1 3.8 %collective-permute-start = (bf16[32,10,360]{2,1,0:T(8,128)(2,1)}, bf16[32,10,360]{2,1,0:T(8,128)(2,1)S(1)}, u32[]{:S(2)}, u32[]{:S(2)}) collective-permute-start(bf16[32,10,360]{2,1,0:T(8,128)(2,1)} %dynamic-slice_bitcast_fusion), channel_id=1, source_target_pairs={{0,8},{8,0},{16,24},{24,16},{32,40},{40,32},{48,56},{56,48},{64,72... | collective-permute-start | bytes 691208 | tf_op jit(solution)/shard_map/ppermute | solution.py:381
  169.0 27.5 %copy-start.3 = (bf16[64,360]{1,0:T(8,128)(2,1)S(1)}, bf16[64,360]{1,0:T(8,128)(2,1)}, u32[]{:S(2)}) copy-start(bf16[64,360]{1,0:T(8,128)(2,1)} %param.23) | copy-start | bytes 138244

commit v16 on v15

--- a/solution.py
+++ b/solution.py
@@ -13,6 +13,11 @@
 THETA = 150000.0
 ALPHA = 1.702
 EPSILON = 1e-05
+
+
+def _offset(step, count):
+    odd = lax.rem(step, 2)
+    return odd * lax.div(step + 1, 2) + (1 - odd) * (count - lax.div(step, 2))
 
 
 def _row_parts(rows, parts=8):
@@ -59,7 +64,7 @@
     for first, size in _row_parts(buf.shape[1] if (gather or axis == "tp") else 0):
 
         def send(step, carry, first=first, size=size):
-            peer = lax.rem(me + step, count)
+            peer = lax.rem(me + (_offset(step, count) if axis == "tp" else step), count)
             src = piece(peer)
             dst = buf.at[me]
             if size:
@@ -136,7 +141,7 @@
     for first, size in _row_parts(x_ref.shape[0]):
 
         def send(step, carry, first=first, size=size):
-            peer = lax.rem(tp_at + step, count)
+            peer = lax.rem(tp_at + _offset(step, count), count)
             pltpu.make_async_remote_copy(
                 src_ref=x_ref.at[pl.ds(first, size)],
                 dst_ref=buf.at[tp_at, core, pl.ds(first, size)],

time: 200 us -> 199 us (level)
  no operation moved by 1% of the time
where the time goes in v16:
time: 199 us; the launch traced here: 197 us
  Pallas kernels  150 us (75%)
  local copies, waits for them, and re-layouts  22.8 us (11%)
  matrix products  13.4 us (7%)
  other arithmetic  5.94 us (3%)
    pallas_call x5, Pallas kernels, _transfer(): pl.pallas_call(functools.partial(_transfer_kernel, axis, gather), out_sha...  118 us
    pallas_call x1, Pallas kernels, pair_gather(): pl.pallas_call(_pair_gather_kernel, out_shape=jax.ShapeDtypeStruct(shape,...  31.7 us
  transfers between devices with their start and end apart: 1, of which 1 were waited for; matrix products, arithmetic and copies ran while one was open for 0% of the time, Pallas kernels for 0%

profile of v16, /device:TPU:24, one launch (start us, length us, event | category | flops | bytes accessed | tf_op | source)
XLA Modules:
  0.0 197.0 jit_solution(13704289763365878840)
XLA Ops:
  0.8 0.9 reshape.359
  2.9 26.8 %shard_map.145 = bf16[64,8,128]{2,1,0:T(8,128)(2,1)} custom-call(bf16[64,8,128]{2,1,0:T(8,128)(2,1)} %bitcast.89), custom_call_target="tpu_custom_call" | custom-call | tf_op jit(solution)/shard_map/pallas_call | solution.py:100
  29.7 1.0 concatenate.53
  30.8 0.9 copy.65
  35.7 1.3 fusion.12.x_ref
  37.0 12.4 %shard_map.146 = bf16[8,64,360]{2,1,0:T(8,128)(2,1)} custom-call(bf16[8,64,360]{2,1,0:T(8,128)(2,1)} %fusion.12.x_ref), custom_call_target="tpu_custom_call" | custom-call | tf_op jit(solution)/shard_map/pallas_call | solution.py:100
  49.4 1.1 convert_reduce_fusion.1
  53.5 25.2 %shard_map.147 = bf16[32,30,128]{2,1,0:T(8,128)(2,1)} custom-call(bf16[32,30,128]{2,1,0:T(8,128)(2,1)} %reshape.351.x_ref), custom_call_target="tpu_custom_call" | custom-call | tf_op jit(solution)/shard_map/pallas_call | solution.py:100
  78.7 1.8 reshape_reshape_reshape.3.x_ref
  80.6 31.7 %shard_map.148 = bf16[8,2,320,384]{3,2,1,0:T(8,128)(2,1)} custom-call(bf16[320,384]{1,0:T(8,128)(2,1)} %reshape_reshape_reshape.3.x_ref), custom_call_target="tpu_custom_call" | custom-call | tf_op jit(solution)/shard_map/pallas_call | solution.py:202
  112.3 2.8 %reshape_squeeze.10 = bf16[8,360,180]{1,0,2:T(8,128)(2,1)S(1)} reshape(bf16[1,2880,180]{1,2,0:T(8,128)(2,1)} %param.28) | data formatting | bytes 2073600 | tf_op jit(solution)/shard_map/reshape;squeeze | solution.py:363
  115.1 1.9 convert_reduce_fusion
  116.9 3.5 %fusion.6 = f32[640,180]{0,1:T(8,128)S(1)} fusion(bf16[8,640,384]{2,1,0:T(8,128)(2,1)} %bitcast.80, bf16[8,360,180]{1,0,2:T(8,128)(2,1)S(1)} %reshape_squeeze.10), kind=kOutput, calls=%fused_computation.10 | convolution fusion | flops 663552000 | bytes 5429760 | tf_op jit(solution)/shard_map/tsf,tfh->sh/dot_general | solution.py:367
  120.5 2.8 %reshape_squeeze.9 = bf16[8,360,180]{1,0,2:T(8,128)(2,1)S(1)} reshape(bf16[1,2880,180]{1,2,0:T(8,128)(2,1)} %param.27) | data formatting | bytes 2073600 | tf_op jit(solution)/shard_map/reshape;squeeze | solution.py:362
  123.3 3.5 %fusion.9 = f32[640,180]{0,1:T(8,128)S(1)} fusion(bf16[8,640,384]{2,1,0:T(8,128)(2,1)} %bitcast.81, bf16[8,360,180]{1,0,2:T(8,128)(2,1)S(1)} %reshape_squeeze.9), kind=kOutput, calls=%fused_computation.11 | convolution fusion | flops 663552000 | bytes 5429760 | tf_op jit(solution)/shard_map/tsf,tfh->sh/dot_general | solution.py:366
  127.8 29.0 %shard_map.149 = bf16[8,180,640]{2,1,0:T(8,128)(2,1)} custom-call(bf16[180,640]{1,0:T(8,128)(2,1)} %fusion.24.x_ref), custom_call_target="tpu_custom_call" | custom-call | tf_op jit(solution)/shard_map/pallas_call | solution.py:100
  156.8 2.3 %reshape_squeeze.11 = bf16[8,180,360]{2,1,0:T(8,128)(2,1)} reshape(bf16[1,1440,360]{2,1,0:T(8,128)(2,1)} %param.29) | data formatting | bytes 2073600 | tf_op jit(solution)/shard_map/reshape;squeeze | solution.py:376
  159.2 3.1 %fusion.5 = bf16[640,360]{0,1:T(8,128)(2,1)} fusion(bf16[8,180,640]{2,1,0:T(8,128)(2,1)S(1)} %copy-done.1, bf16[8,180,360]{2,1,0:T(8,128)(2,1)} %reshape_squeeze.11), kind=kOutput, calls=%fused_computation.8 | convolution fusion | flops 663782400 | bytes 3340800 | tf_op jit(solution)/shard_map/ths,thd->sd/dot_general | solution.py:377
  162.3 1.3 copy.82
  164.6 1.9 collective-permute-start
  166.8 1.6 collective-permute-done
  169.6 24.9 %shard_map.150 = bf16[32,29,128]{2,1,0:T(8,128)(2,1)} custom-call(bf16[32,29,128]{2,1,0:T(8,128)(2,1)} %reshape.355.x_ref), custom_call_target="tpu_custom_call" | custom-call | tf_op jit(solution)/shard_map/pallas_call | solution.py:100
  194.5 1.0 copy.90
  196.0 1.0 fusion.15
  (86 shorter events, 11.8 us)
Async XLA Ops:
  0.0 35.7 %copy-start = (bf16[256,2880]{0,1:T(8,128)(2,1)S(1)}, bf16[256,2880]{0,1:T(8,128)(2,1)}, u32[]{:S(2)}) copy-start(bf16[256,2880]{0,1:T(8,128)(2,1)} %param.22) | copy-start | bytes 4423684
  1.7 31.2 %copy-start.7 = (s32[1,64]{1,0:T(1,128)S(1)}, s32[1,64]{1,0:T(1,128)}, u32[]{:S(2)}) copy-start(s32[1,64]{1,0:T(1,128)} %param.19) | copy-start | bytes 772
  31.8 2.1 %copy-start.6 = (f32[4]{0:T(128)S(1)}, f32[4]{0:T(128)}, u32[]{:S(2)}) copy-start(f32[4]{0:T(128)} %param.21) | copy-start | bytes 52
  35.7 15.6 %copy-start.2 = (bf16[64,360]{1,0:T(8,128)(2,1)S(1)}, bf16[64,360]{1,0:T(8,128)(2,1)}, u32[]{:S(2)}) copy-start(bf16[64,360]{1,0:T(8,128)(2,1)} %param.23) | copy-start | bytes 138244
  35.7 16.0 %copy-start.4 = (s32[64,4]{0,1:T(4,128)S(1)}, s32[64,4]{0,1:T(4,128)}, u32[]{:S(2)}) copy-start(s32[64,4]{0,1:T(4,128)} %param.25) | copy-start | bytes 3076
  156.8 2.3 %copy-start.1 = (bf16[8,180,640]{2,1,0:T(8,128)(2,1)S(1)}, bf16[8,180,640]{2,1,0:T(8,128)(2,1)}, u32[]{:S(2)}) copy-start(bf16[8,180,640]{2,1,0:T(8,128)(2,1)} %shard_map.149) | copy-start | bytes 5529604
  162.3 4.4 %copy-start.5 = (f32[64,4]{0,1:T(4,128)S(1)}, f32[64,4]{0,1:T(4,128)}, u32[]{:S(2)}) copy-start(f32[64,4]{0,1:T(4,128)} %param.26) | copy-start | bytes 3076
  164.6 3.8 %collective-permute-start = (bf16[32,10,360]{2,1,0:T(8,128)(2,1)}, bf16[32,10,360]{2,1,0:T(8,128)(2,1)S(1)}, u32[]{:S(2)}, u32[]{:S(2)}) collective-permute-start(bf16[32,10,360]{2,1,0:T(8,128)(2,1)} %dynamic-slice_bitcast_fusion), channel_id=1, source_target_pairs={{0,8},{8,0},{16,24},{24,16},{32,40},{40,32},{48,56},{56,48},{64,72... | collective-permute-start | bytes 691208 | tf_op jit(solution)/shard_map/ppermute | solution.py:386
  168.5 27.5 %copy-start.3 = (bf16[64,360]{1,0:T(8,128)(2,1)S(1)}, bf16[64,360]{1,0:T(8,128)(2,1)}, u32[]{:S(2)}) copy-start(bf16[64,360]{1,0:T(8,128)(2,1)} %param.23) | copy-start | bytes 138244
